TPU v7x, 256 devices: a whole 4x4x8 slice. The times are simulated.
256 devices in a mesh: row: 32 (over z, y), col: 8 (over x, core).
Axes of the slice: x: 4, y: 4, z: 8, core: 2. Of those that a mesh axis runs over, the one named last changes fastest.
Arguments:
- object_field: float32 [2, 3, 8192, 2048], P(None, None, 'row', 'col'), may hold values from -1 to 1
- probe: float32 [2, 128, 128], replicated, may hold values from -4 to 4
- propagator: float32 [128, 128], replicated, may hold values from -3.140625 to 3.140625
- measured: float32 [32, 8, 6, 128, 128], P('row', 'col'), may hold values from 0 to 1
- offsets: int32 [32, 8, 6, 2], P('row', 'col'), may hold values from 0 to 255
Outputs:
- updated: float32 [2, 3, 8192, 2048], P(None, None, 'row', 'col')
Inputs may be any that keep to these rules, and one draw needn't show every extreme that they name: `offsets`: entry 0 is the row offset and entry 1 the column offset of a window inside its tile.
All inputs are finite; a program needn't handle non-finite values.
Results may differ from a plain program's by a relative error of at most 0.0003.
Values sent between devices are 32-bit elements; how exact they have to be, the bound alone decides.
No kernel may reach another device: no remote copies, remote signals or barrier semaphores. Data moves between devices by JAX's collectives and lax.ppermute only.
A program may use at most 64 MiB of HBM per device.

v0:
```python
import functools
import math

import jax
import jax.numpy as jnp
import numpy as np
from jax import lax
from jax.experimental import pallas as pl
from jax.experimental.pallas import tpu as pltpu
from jax.sharding import PartitionSpec as P


PROBE = 128
SLICES = 3
POS = 6
TILE = 256
EXT = TILE + PROBE
SUB = 8
STEP = 0.05
F32 = jnp.float32
BF16 = jnp.bfloat16


def dft_tables():
    index = np.arange(PROBE)
    angle = (index[:, None] * index[None, :] % PROBE) * (-2.0 * math.pi / PROBE)
    cosines, sines = np.cos(angle) / math.sqrt(PROBE), np.sin(angle) / math.sqrt(PROBE)
    right = np.block([[cosines, sines], [-sines, cosines]]).astype(np.float32)
    left = np.block([[cosines, -sines], [sines, cosines]]).astype(np.float32)
    parts = []
    for matrix in (right, left):
        high = matrix.astype(BF16)
        parts += [high, (matrix - high.astype(np.float32)).astype(BF16)]
    return np.stack(parts)


def split(value):
    high = value.astype(BF16)
    return high, (value - high.astype(F32)).astype(BF16)


def dot(a, b):
    return jnp.dot(a, b, preferred_element_type=F32)


def times_right(block, table):
    high, low = block
    wide, fine = table
    return dot(jnp.concatenate([high, low, high], axis=1), jnp.concatenate([wide, wide, fine], axis=0))


def times_left(block, table):
    high, low = block
    wide, fine = table
    return dot(jnp.concatenate([wide, wide, fine], axis=1), jnp.concatenate([high, low, high], axis=0))


def side_to_stack(block):
    h = PROBE
    top = jnp.concatenate([block[:h, :h], block[h:, :h]], axis=1)
    low = jnp.concatenate([block[:h, h:], block[h:, h:]], axis=1)
    return jnp.concatenate([top, low], axis=0)


def times_phase(block, phase_real, phase_imag):
    h = PROBE
    re, im = block[:h], block[h:]
    pr = jnp.concatenate([phase_real, phase_real], axis=1)
    pi = jnp.concatenate([phase_imag, phase_imag], axis=1)
    return jnp.concatenate([re * pr - im * pi, re * pi + im * pr], axis=0)


def keep(work, n, slot, block):
    work[slot, n, 0], work[slot, n, 1] = split(block)


def kept(work, n, slot):
    return work[slot, n, 0], work[slot, n, 1]


PAIRS = POS // 2


def propagate(work, right, left, phase_real, phase_imag, finish):
    for n in range(PAIRS):
        keep(work, n, 1, side_to_stack(times_right(kept(work, n, 0), right)))
    for n in range(PAIRS):
        keep(work, n, 0, times_phase(times_left(kept(work, n, 1), left), phase_real, phase_imag))
    for n in range(PAIRS):
        keep(work, n, 1, side_to_stack(times_left(kept(work, n, 0), right)))
    for n in range(PAIRS):
        finish(n, times_right(kept(work, n, 1), left))


def tables_of(table_ref):
    right = (table_ref[0], table_ref[1])
    left = (table_ref[2], table_ref[3])
    return right, left


def pair_of(ref, p):
    top = jnp.concatenate([ref[0, p], ref[1, p]], axis=1)
    low = jnp.concatenate([ref[0, p + 1], ref[1, p + 1]], axis=1)
    return jnp.concatenate([top, low], axis=0)


def put_pair(ref, p, block):
    h = PROBE
    ref[0, p] = block[:h, :h]
    ref[1, p] = block[:h, h:]
    ref[0, p + 1] = block[h:, :h]
    ref[1, p + 1] = block[h:, h:]


def place(offset_ref, p):
    row, col = offset_ref[p, 0], offset_ref[p, 1]
    over = lax.rem(row, SUB)
    base = jnp.where(col >= PROBE, PROBE, 0)
    return pl.multiple_of(row - over, SUB), over, pl.multiple_of(base, PROBE), col - base


TALL = PROBE + SUB


def lanes(rows):
    return lax.broadcasted_iota(jnp.int32, (rows, PROBE), 1)


def take_window(ext, offset_ref, p, part):
    row, over, base, shift = place(offset_ref, p)
    after = pl.multiple_of(base + PROBE, PROBE)
    first = ext[part, pl.ds(row, TALL), pl.ds(base, PROBE)]
    second = ext[part, pl.ds(row, TALL), pl.ds(after, PROBE)]
    block = jnp.where(lanes(TALL) >= shift, first, second)
    block = pltpu.roll(block, jnp.where(shift == 0, 0, PROBE - shift), 1)
    return pltpu.roll(block, jnp.where(over == 0, 0, TALL - over), 0)[:PROBE]


def turn_window(offset_ref, p, value):
    _, over, _, shift = place(offset_ref, p)
    block = jnp.concatenate([value, jnp.zeros((SUB, PROBE), F32)], axis=0)
    return pltpu.roll(pltpu.roll(block, over, 0), shift, 1)


def add_windows(grads, offset_ref, turned):
    for p in range(POS):
        row, _, base, shift = place(offset_ref, p)
        after = pl.multiple_of(base + PROBE, PROBE)
        here = lanes(TALL) >= shift
        for part in range(2):
            block = turned[part, p]
            where = (pl.ds(row, TALL), pl.ds(base, PROBE))
            grads[part][where] = grads[part][where] + jnp.where(here, block, 0.0)
            where = (pl.ds(row, TALL), pl.ds(after, PROBE))
            grads[part][where] = grads[part][where] + jnp.where(here, 0.0, block)


def times(ar, ai, br, bi):
    return ar * br - ai * bi, ar * bi + ai * br


def times_conj(ar, ai, br, bi):
    return ar * br + ai * bi, ar * bi - ai * br


def fill_first(ext, refs):
    tile, low, right, corner = refs
    t = TILE
    ext[:, :t, :t] = tile[:, 0]
    ext[:, t:, :t] = low[...]
    ext[:, :t, t:] = right[...]
    ext[:, t:, t:] = corner[...]


def fill_next(ext, refs):
    left, middle, right = refs
    t, h = TILE, PROBE
    ext[:, :, :h] = left[...]
    ext[:, :, h:t] = middle[...]
    ext[:, :, t:] = right[...]


def forward_kernel(fill, n_field, first, *refs):
    offset_ref, table_ref, phase_ref, wave = refs[:4]
    field = refs[4 : 4 + n_field]
    windows, out, ext, work = refs[4 + n_field :]
    fill(ext, field)
    right, left = tables_of(table_ref)
    for n in range(PAIRS):
        rows = []
        for q in (2 * n, 2 * n + 1):
            tr = take_window(ext, offset_ref, q, 0)
            ti = take_window(ext, offset_ref, q, 1)
            windows[0, q] = tr
            windows[1, q] = ti
            if first:
                wr, wi = wave[0], wave[1]
            else:
                wr, wi = wave[0, q], wave[1, q]
            rows.append(jnp.concatenate(times(wr, wi, tr, ti), axis=1))
        keep(work, n, 0, jnp.concatenate(rows, axis=0))

    def finish(n, block):
        put_pair(out, 2 * n, block)

    propagate(work, right, left, phase_ref[0], phase_ref[1], finish)


def write_gradient(grads, outs):
    for n, out in enumerate(outs):
        for part in range(2):
            out[part] = grads[part][:, n * PROBE : (n + 1) * PROBE]


def turn_kernel(fill, n_field, *refs):
    offset_ref, table_ref, intensity, wave = refs[:4]
    field = refs[4 : 4 + n_field]
    outs = refs[4 + n_field : 7 + n_field]
    back, ext, windows, work, turned, *grads = refs[7 + n_field :]
    fill(ext, field)
    for part in grads:
        part[...] = jnp.zeros_like(part)
    right, left = tables_of(table_ref)
    h = PROBE
    for n in range(PAIRS):
        rows = []
        for q in (2 * n, 2 * n + 1):
            tr = take_window(ext, offset_ref, q, 0)
            ti = take_window(ext, offset_ref, q, 1)
            windows[0, q] = tr
            windows[1, q] = ti
            rows.append(jnp.concatenate(times(wave[0, q], wave[1, q], tr, ti), axis=1))
        keep(work, n, 0, jnp.concatenate(rows, axis=0))
    for n in range(PAIRS):
        keep(work, n, 1, side_to_stack(times_right(kept(work, n, 0), right)))
    for n in range(PAIRS):
        block = times_left(kept(work, n, 1), left)
        re, im = block[:h], block[h:]
        target = jnp.concatenate([intensity[2 * n], intensity[2 * n + 1]], axis=1)
        weight = 4.0 * (re * re + im * im - target)
        keep(work, n, 0, jnp.concatenate([re * weight, im * weight], axis=0))
    for n in range(PAIRS):
        keep(work, n, 1, side_to_stack(times_left(kept(work, n, 0), right)))
    for n in range(PAIRS):
        block = times_right(kept(work, n, 1), left)
        for i in range(2):
            q = 2 * n + i
            gr, gi = block[i * h : (i + 1) * h, :h], block[i * h : (i + 1) * h, h:]
            br, bi = times_conj(windows[0, q], windows[1, q], gr, gi)
            back[0, q] = br
            back[1, q] = bi
            dr, di = times_conj(wave[0, q], wave[1, q], gr, gi)
            turned[0, q] = turn_window(offset_ref, q, dr)
            turned[1, q] = turn_window(offset_ref, q, di)
    add_windows(grads, offset_ref, turned)
    write_gradient(grads, outs)


def backward_kernel(first, *refs):
    if first:
        offset_ref, table_ref, phase_ref, back_in, wave = refs[:5]
        outs = refs[5:8]
    else:
        offset_ref, table_ref, phase_ref, back_in, wave, windows = refs[:6]
        outs, back = refs[6:9], refs[9]
    work, turned, *grads = refs[-4:]
    for part in grads:
        part[...] = jnp.zeros_like(part)
    right, left = tables_of(table_ref)
    h = PROBE
    for n in range(PAIRS):
        keep(work, n, 0, pair_of(back_in, 2 * n))

    def finish(n, block):
        for i in range(2):
            q = 2 * n + i
            gr, gi = block[i * h : (i + 1) * h, :h], block[i * h : (i + 1) * h, h:]
            if first:
                dr, di = times_conj(wave[0], wave[1], gr, gi)
            else:
                br, bi = times_conj(windows[0, q], windows[1, q], gr, gi)
                back[0, q] = br
                back[1, q] = bi
                dr, di = times_conj(wave[0, q], wave[1, q], gr, gi)
            turned[0, q] = turn_window(offset_ref, q, dr)
            turned[1, q] = turn_window(offset_ref, q, di)

    propagate(work, right, left, phase_ref[0], -phase_ref[1], finish)
    add_windows(grads, offset_ref, turned)
    write_gradient(grads, outs)


def whole(array):
    rank = len(array.shape)
    return pl.BlockSpec(array.shape, lambda i: (0,) * rank)


def tile_of(layer):
    return pl.BlockSpec((2, 1, TILE, TILE), lambda i: (0, layer, 0, 0))


def shape(*dims):
    return jax.ShapeDtypeStruct(dims, F32)


STACK = (2, POS, PROBE, PROBE)
GRADIENT = [shape(2, EXT, PROBE)] * 3
WORK = pltpu.VMEM((2, PAIRS, 2, 256, 256), BF16)
SCRATCH = pltpu.VMEM((2, EXT, EXT), F32)
GRADS = [pltpu.VMEM((2, POS, TALL, PROBE), F32)] + [pltpu.VMEM((EXT, EXT), F32)] * 2


def run(body, operands, outs, scratch, stages, specs=None):
    specs = specs or {}
    flops = stages * POS * PROBE * 256 * 256 * 2 * 3
    moved = sum(math.prod(o.shape) * 4 for o in operands) + sum(math.prod(o.shape) * 4 for o in outs)
    in_specs = [pl.BlockSpec(memory_space=pltpu.SMEM)]
    in_specs += [specs.get(n, None) or whole(o) for n, o in enumerate(operands) if n > 0]
    return pl.pallas_call(
        body,
        grid=(1,),
        in_specs=in_specs,
        out_specs=[whole(o) for o in outs],
        out_shape=outs,
        scratch_shapes=scratch,
        cost_estimate=pl.CostEstimate(flops=flops, bytes_accessed=moved, transcendentals=0),
        compiler_params=pltpu.CompilerParams(vmem_limit_bytes=40 * 2**20),
    )(*operands)


def forward(offsets, tables, phase, wave, field, layer, fill, first):
    operands = [offsets, tables, phase, wave, *field]
    specs = {4: tile_of(layer)} if fill is fill_first else {}
    body = functools.partial(forward_kernel, fill, len(field), first)
    return run(body, operands, [shape(*STACK)] * 2, [SCRATCH, WORK], 4, specs)


def turn(offsets, tables, intensity, wave, field, layer, fill):
    operands = [offsets, tables, intensity, wave, *field]
    specs = {4: tile_of(layer)} if fill is fill_first else {}
    body = functools.partial(turn_kernel, fill, len(field))
    return run(body, operands, [*GRADIENT, shape(*STACK)], [SCRATCH, pltpu.VMEM(STACK, F32), WORK, *GRADS], 4, specs)


def backward(offsets, tables, phase, back, wave, windows):
    first = windows is None
    operands = [offsets, tables, phase, back, wave] + ([] if first else [windows])
    outs = [*GRADIENT] if first else [*GRADIENT, shape(*STACK)]
    return run(functools.partial(backward_kernel, first), operands, outs, [WORK, *GRADS], 4)


def shifted(block, axis, distance):
    size = lax.axis_size(axis)
    return lax.ppermute(block, axis, [((i - distance) % size, i) for i in range(size)])


def plain(body, outs, operands, specs=None, aliases=None, out_specs=None):
    specs = specs or {}
    moved = sum(math.prod(o.shape) * 4 for o in outs)
    return pl.pallas_call(
        body,
        grid=(1,),
        in_specs=[specs.get(n, None) or whole(o) for n, o in enumerate(operands)],
        out_specs=out_specs or [whole(o) for o in outs],
        out_shape=outs,
        input_output_aliases=aliases or {},
        cost_estimate=pl.CostEstimate(flops=0, bytes_accessed=2 * moved, transcendentals=0),
        compiler_params=pltpu.CompilerParams(vmem_limit_bytes=24 * 2**20),
    )(*operands)


ROWS = shape(2, PROBE, TILE)
SIDE = shape(2, EXT, PROBE)


def pack_kernel(layer, tile, rows, cols, sems):
    first = pltpu.make_async_copy(tile.at[:, layer, pl.ds(0, PROBE)], rows, sems.at[0])
    second = pltpu.make_async_copy(tile.at[:, layer, :, pl.ds(0, PROBE)], cols, sems.at[1])
    first.start()
    second.start()
    first.wait()
    second.wait()


def pack(object_field, layer):
    cols = shape(2, TILE, PROBE)
    return pl.pallas_call(
        functools.partial(pack_kernel, layer),
        in_specs=[pl.BlockSpec(memory_space=pltpu.HBM)],
        out_specs=[pl.BlockSpec(memory_space=pltpu.VMEM)] * 2,
        out_shape=[ROWS, cols],
        scratch_shapes=[pltpu.SemaphoreType.DMA((2,))],
        name="pack",
        cost_estimate=pl.CostEstimate(flops=0, bytes_accessed=4 * 2**18, transcendentals=0),
    )(object_field)


def sums_kernel(both, left, middle, from_left, *outs):
    h, t = PROBE, TILE
    down = outs[0]
    down[:, :, :h] = left[:, t:] + from_left[:, t:]
    down[:, :, h:] = middle[:, t:]
    if both:
        up = outs[1]
        up[:, :, :h] = left[:, :h] + from_left[:, :h]
        up[:, :, h:] = middle[:, :h]


def sums(left, middle, from_left, both):
    body = functools.partial(sums_kernel, both)
    return plain(body, [ROWS] * (1 + both), [left, middle, from_left])


def update_kernel(tile, low, left, middle, from_left, above, below, new_l, new_m):
    h, t = PROBE, TILE
    top, mid, end = slice(0, h), slice(h, t), slice(t, t + h)
    for new, grad, cols in ((new_l, left, slice(0, h)), (new_m, middle, slice(h, t))):
        extra = (lambda rows: grad[:, rows] + from_left[:, rows]) if new is new_l else (lambda rows: grad[:, rows])
        new[:, top] = tile[:, 0, top, cols] - STEP * (extra(top) + above[:, :, cols])
        new[:, mid] = tile[:, 0, mid, cols] - STEP * extra(mid)
        new[:, end] = low[:, :, cols] - STEP * (extra(end) + below[:, :, cols])


def update(object_field, layer, low, grad, from_left, above, below):
    operands = [object_field, low, grad[0], grad[1], from_left, above, below]
    return plain(update_kernel, [SIDE] * 2, operands, {0: tile_of(layer)})


def last_kernel(n_alias, *refs):
    old_l, old_m, left, middle, from_left, above = refs[:6]
    out = refs[6 + n_alias]
    h, t = PROBE, TILE
    out[:, 0, :h, :h] = old_l[:, :h] - STEP * (left[:, :h] + from_left[:, :h] + above[:, :, :h])
    out[:, 0, h:, :h] = old_l[:, h:t] - STEP * (left[:, h:t] + from_left[:, h:t])
    out[:, 0, :h, h:] = old_m[:, :h] - STEP * (middle[:, :h] + above[:, :, h:])
    out[:, 0, h:, h:] = old_m[:, h:t] - STEP * middle[:, h:t]


def last(result, layer, field, grad, from_left, above):
    operands = [field[0], field[1], grad[0], grad[1], from_left, above]
    specs, aliases = {}, {}
    if result is not None:
        operands.append(result)
        specs, aliases = {6: pl.BlockSpec(memory_space=pl.ANY)}, {6: 0}
    return plain(
        functools.partial(last_kernel, len(operands) - 6),
        [shape(2, SLICES, TILE, TILE)],
        operands,
        specs,
        aliases,
        [tile_of(layer)],
    )[0]


def on_device(object_field, probe, propagator, measured, offsets):
    h = PROBE
    tables = jnp.asarray(dft_tables())
    offsets = offsets.reshape(POS, 2)
    intensity = measured.reshape(POS, h, h)
    phase = jnp.stack([jnp.cos(propagator), jnp.sin(propagator)])

    packed = [pack(object_field, layer) for layer in range(SLICES)]
    lows, fields = [], []
    for rows, cols in packed:
        low = shifted(rows, "row", -1)
        right = shifted(cols, "col", -1)
        corner = shifted(low[:, :, :h], "col", -1)
        lows.append(low)
        fields.append([object_field, low, right, corner])

    def gradients(fields, fill):
        _, wave1 = forward(offsets, tables, phase, probe, fields[0], 0, fill, True)
        win1, wave2 = forward(offsets, tables, phase, wave1, fields[1], 1, fill, False)
        *grad2, back = turn(offsets, tables, intensity, wave2, fields[2], 2, fill)
        *grad1, back = backward(offsets, tables, phase, back, wave1, win1)
        grad0 = backward(offsets, tables, phase, back, probe, None)
        return [grad0, grad1, grad2]

    grads = gradients(fields, fill_first)
    fields = [None] * SLICES
    for layer in (2, 1, 0):
        grad = grads[layer]
        from_left = shifted(grad[2], "col", 1)
        down, up = sums(grad[0], grad[1], from_left, True)
        above = shifted(down, "row", 1)
        below = shifted(up, "row", -1)
        new_l, new_m = update(object_field, layer, lows[layer], grad, from_left, above, below)
        fields[layer] = [new_l, new_m, shifted(new_l, "col", -1)]
    grads = gradients(fields, fill_next)
    result = None
    for layer in (2, 1, 0):
        grad = grads[layer]
        from_left = shifted(grad[2], "col", 1)
        down = sums(grad[0], grad[1], from_left, False)[0]
        above = shifted(down, "row", 1)
        result = last(result, layer, fields[layer], grad, from_left, above)
    return result


def solution(mesh):
    placed = (
        P(None, None, "row", "col"),
        P(),
        P(),
        P("row", "col", None, None, None),
        P("row", "col", None, None),
    )
    return jax.shard_map(
        on_device,
        mesh=mesh,
        in_specs=placed,
        out_specs=P(None, None, "row", "col"),
        check_vma=False,
    )
```

profile of v0, /device:TPU:7, one launch (start us, length us, event | category | flops | bytes accessed | tf_op | source)
XLA Modules:
  0.0 116.7 jit_solution(8041863206837826197)
XLA Ops:
  1.9 8.1 %collective-permute-start = (f32[2,128,256]{2,1,0:T(8,128)}, f32[2,128,256]{2,1,0:T(8,128)S(1)}, u32[]{:S(2)}, u32[]{:S(2)}) collective-permute-start(f32[2,128,256]{2,1,0:T(8,128)} %get-tuple-element.51), channel_id=1, source_target_pairs={{8,0},{16,8},{24,16},{32,24},{40,32},{48,40},{56,48},{64,56},{72,6... | collective-permute-start | bytes 786440 | tf_op jit(solution)/shard_map/ppermute | solution.py:354
  20.9 2.7 %collective-permute-start.7 = (f32[2,256,128]{2,1,0:T(8,128)}, f32[2,256,128]{2,1,0:T(8,128)S(1)}, u32[]{:S(2)}, u32[]{:S(2)}) collective-permute-start(f32[2,256,128]{2,1,0:T(8,128)} %get-tuple-element.58), channel_id=1, source_target_pairs={{1,0},{2,1},{3,2},{4,3},{5,4},{6,5},{7,6},{0,7},{9,8},{10,9},{11,1... | collective-permute-start | bytes 786440 | tf_op jit(solution)/shard_map/ppermute | solution.py:354
  24.2 2.3 %collective-permute-done.6.refs_5_.low = f32[2,128,256]{2,1,0:T(8,128)S(1)} collective-permute-done((f32[2,128,256]{2,1,0:T(8,128)}, f32[2,128,256]{2,1,0:T(8,128)S(1)}, u32[]{:S(2)}, u32[]{:S(2)}) %collective-permute-start.6) | collective-permute-done | bytes 262176 | tf_op jit(solution)/shard_map/ppermute | solution.py:354
  29.3 2.5 %shard_map.64 = (f32[2,6,128,128]{3,2,1,0:T(8,128)}, f32[2,6,128,128]{3,2,1,0:T(8,128)S(1)}) custom-call(s32[6,2]{1,0:T(8,128)S(1)} %copy.13.refs_0_, bf16[4,256,256]{2,1,0:T(8,128)(2,1)S(1)} %copy-done.3, f32[2,128,128]{2,1,0:T(8,128)S(1)} %pad_maximum_fusion.refs_2_, f32[2,128,128]{2,1,0:T(8,128)S(1)} %copy-done.2, f32[2,3,256,256]{3,2,1,0:T(8,128)S(1)} %copy-done, ...), custom_call_target="tpu_custom_call" | custom-call | flops 1207959552 | bytes 5111856 | tf_op jit(solution)/shard_map/pallas_call | solution.py:319
  32.4 2.9 %shard_map.65 = (f32[2,6,128,128]{3,2,1,0:T(8,128)S(1)}, f32[2,6,128,128]{3,2,1,0:T(8,128)S(1)}) custom-call(s32[6,2]{1,0:T(8,128)S(1)} %copy.13.refs_0_, bf16[4,256,256]{2,1,0:T(8,128)(2,1)S(1)} %copy-done.4, f32[2,128,128]{2,1,0:T(8,128)S(1)} %pad_maximum_fusion.refs_2_, f32[2,6,128,128]{3,2,1,0:T(8,128)S(1)} %get-tuple-element.53.refs_3_.refs_4_, ...), custom_call_target="tpu_custom_call" | custom-call | flops 1207959552 | bytes 5767216 | tf_op jit(solution)/shard_map/pallas_call | solution.py:319
  35.3 3.0 %shard_map.66 = (f32[2,384,128]{2,1,0:T(8,128)S(1)}, f32[2,384,128]{2,1,0:T(8,128)S(1)}, f32[2,384,128]{2,1,0:T(8,128)S(1)}, f32[2,6,128,128]{3,2,1,0:T(8,128)S(1)}) custom-call(s32[6,2]{1,0:T(8,128)S(1)} %copy.13.refs_0_, bf16[4,256,256]{2,1,0:T(8,128)(2,1)S(1)} %copy-done.4, f32[6,128,128]{2,1,0:T(8,128)S(1)} %bitcast.6, ...), custom_call_target="tpu_custom_call" | custom-call | flops 1207959552 | bytes 6422576 | tf_op jit(solution)/shard_map/pallas_call | solution.py:319
  38.3 2.7 %shard_map.67 = (f32[2,384,128]{2,1,0:T(8,128)S(1)}, f32[2,384,128]{2,1,0:T(8,128)S(1)}, f32[2,384,128]{2,1,0:T(8,128)S(1)}, f32[2,6,128,128]{3,2,1,0:T(8,128)S(1)}) custom-call(s32[6,2]{1,0:T(8,128)S(1)} %copy.13.refs_0_, bf16[4,256,256]{2,1,0:T(8,128)(2,1)S(1)} %copy-done.4, f32[2,128,128]{2,1,0:T(8,128)S(1)} %pad_maximum_fusion.refs_2_, ...), custom_call_target="tpu_custom_call" | custom-call | flops 1207959552 | bytes 5505072 | tf_op jit(solution)/shard_map/pallas_call | solution.py:319
  41.0 2.6 %shard_map.68 = (f32[2,384,128]{2,1,0:T(8,128)S(1)}, f32[2,384,128]{2,1,0:T(8,128)S(1)}, f32[2,384,128]{2,1,0:T(8,128)S(1)}) custom-call(s32[6,2]{1,0:T(8,128)S(1)} %copy.13.refs_0_, bf16[4,256,256]{2,1,0:T(8,128)(2,1)S(1)} %copy-done.4, f32[2,128,128]{2,1,0:T(8,128)S(1)} %pad_maximum_fusion.refs_2_, f32[2,6,128,128]{3,2,1,0:T(8,128)S(1)} %get-tuple-element.61.refs_3_, ...), custom_call_target="tpu_custom_call" | custom-call | flops 1207959552 | bytes 3276848 | tf_op jit(solution)/shard_map/pallas_call | solution.py:319
  43.6 2.3 %collective-permute-start.9 = (f32[2,384,128]{2,1,0:T(8,128)S(1)}, f32[2,384,128]{2,1,0:T(8,128)S(1)}, u32[]{:S(2)}, u32[]{:S(2)}) collective-permute-start(f32[2,384,128]{2,1,0:T(8,128)S(1)} %get-tuple-element.64), channel_id=1, source_target_pairs={{7,0},{0,1},{1,2},{2,3},{3,4},{4,5},{5,6},{6,7},{15,8},{8,9},{9,10... | collective-permute-start | bytes 1179656 | tf_op jit(solution)/shard_map/ppermute | solution.py:354
  46.0 4.7 %collective-permute-done.9.from_left = f32[2,384,128]{2,1,0:T(8,128)S(1)} collective-permute-done((f32[2,384,128]{2,1,0:T(8,128)S(1)}, f32[2,384,128]{2,1,0:T(8,128)S(1)}, u32[]{:S(2)}, u32[]{:S(2)}) %collective-permute-start.9) | collective-permute-done | bytes 393248 | tf_op jit(solution)/shard_map/ppermute | solution.py:354
  50.8 5.5 %collective-permute-start.11 = (f32[2,128,256]{2,1,0:T(8,128)S(1)}, f32[2,128,256]{2,1,0:T(8,128)S(1)}, u32[]{:S(2)}, u32[]{:S(2)}) collective-permute-start(f32[2,128,256]{2,1,0:T(8,128)S(1)} %get-tuple-element.66), channel_id=1, source_target_pairs={{8,0},{16,8},{24,16},{32,24},{40,32},{48,40},{56,48},{64,56},{72,6... | collective-permute-start | bytes 786440 | tf_op jit(solution)/shard_map/ppermute | solution.py:354
  56.5 4.8 %collective-permute-start.15 = (f32[2,128,256]{2,1,0:T(8,128)S(1)}, f32[2,128,256]{2,1,0:T(8,128)S(1)}, u32[]{:S(2)}, u32[]{:S(2)}) collective-permute-start(f32[2,128,256]{2,1,0:T(8,128)S(1)} %get-tuple-element.74), channel_id=1, source_target_pairs={{8,0},{16,8},{24,16},{32,24},{40,32},{48,40},{56,48},{64,56},{72,6... | collective-permute-start | bytes 786440 | tf_op jit(solution)/shard_map/ppermute | solution.py:354
  62.4 3.7 %collective-permute-start.19 = (f32[2,128,256]{2,1,0:T(8,128)S(1)}, f32[2,128,256]{2,1,0:T(8,128)S(1)}, u32[]{:S(2)}, u32[]{:S(2)}) collective-permute-start(f32[2,128,256]{2,1,0:T(8,128)S(1)} %get-tuple-element.82), channel_id=1, source_target_pairs={{8,0},{16,8},{24,16},{32,24},{40,32},{48,40},{56,48},{64,56},{72,6... | collective-permute-start | bytes 786440 | tf_op jit(solution)/shard_map/ppermute | solution.py:354
  69.9 3.8 %collective-permute-done.18.above = f32[2,128,256]{2,1,0:T(8,128)S(1)} collective-permute-done((f32[2,128,256]{2,1,0:T(8,128)S(1)}, f32[2,128,256]{2,1,0:T(8,128)S(1)}, u32[]{:S(2)}, u32[]{:S(2)}) %collective-permute-start.18) | collective-permute-done | bytes 262176 | tf_op jit(solution)/shard_map/ppermute | solution.py:354
  76.9 2.5 %shard_map.71 = (f32[2,6,128,128]{3,2,1,0:T(8,128)}, f32[2,6,128,128]{3,2,1,0:T(8,128)S(1)}) custom-call(s32[6,2]{1,0:T(8,128)S(1)} %copy.13.refs_0_, bf16[4,256,256]{2,1,0:T(8,128)(2,1)S(1)} %copy-done.4, f32[2,128,128]{2,1,0:T(8,128)S(1)} %pad_maximum_fusion.refs_2_, f32[2,128,128]{2,1,0:T(8,128)S(1)} %copy-done.2, ...), custom_call_target="tpu_custom_call" | custom-call | flops 1207959552 | bytes 4063280 | tf_op jit(solution)/shard_map/pallas_call | solution.py:319
  81.1 2.5 %shard_map.74 = (f32[2,6,128,128]{3,2,1,0:T(8,128)S(1)}, f32[2,6,128,128]{3,2,1,0:T(8,128)S(1)}) custom-call(s32[6,2]{1,0:T(8,128)S(1)} %copy.13.refs_0_, bf16[4,256,256]{2,1,0:T(8,128)(2,1)S(1)} %copy-done.4, f32[2,128,128]{2,1,0:T(8,128)S(1)} %pad_maximum_fusion.refs_2_, f32[2,6,128,128]{3,2,1,0:T(8,128)S(1)} %get-tuple-element.69.refs_3_.refs_4_, ...), custom_call_target="tpu_custom_call" | custom-call | flops 1207959552 | bytes 4718640 | tf_op jit(solution)/shard_map/pallas_call | solution.py:319
  85.3 3.0 %shard_map.77 = (f32[2,384,128]{2,1,0:T(8,128)S(1)}, f32[2,384,128]{2,1,0:T(8,128)S(1)}, f32[2,384,128]{2,1,0:T(8,128)S(1)}, f32[2,6,128,128]{3,2,1,0:T(8,128)S(1)}) custom-call(s32[6,2]{1,0:T(8,128)S(1)} %copy.13.refs_0_, bf16[4,256,256]{2,1,0:T(8,128)(2,1)S(1)} %copy-done.4, f32[6,128,128]{2,1,0:T(8,128)S(1)} %bitcast.7, ...), custom_call_target="tpu_custom_call" | custom-call | flops 1207959552 | bytes 5374000 | tf_op jit(solution)/shard_map/pallas_call | solution.py:319
  88.3 2.7 %shard_map.78 = (f32[2,384,128]{2,1,0:T(8,128)S(1)}, f32[2,384,128]{2,1,0:T(8,128)S(1)}, f32[2,384,128]{2,1,0:T(8,128)S(1)}, f32[2,6,128,128]{3,2,1,0:T(8,128)S(1)}) custom-call(s32[6,2]{1,0:T(8,128)S(1)} %copy.13.refs_0_, bf16[4,256,256]{2,1,0:T(8,128)(2,1)S(1)} %copy-done.4, f32[2,128,128]{2,1,0:T(8,128)S(1)} %pad_maximum_fusion.refs_2_, ...), custom_call_target="tpu_custom_call" | custom-call | flops 1207959552 | bytes 5505072 | tf_op jit(solution)/shard_map/pallas_call | solution.py:319
  91.1 2.6 %shard_map.79 = (f32[2,384,128]{2,1,0:T(8,128)S(1)}, f32[2,384,128]{2,1,0:T(8,128)S(1)}, f32[2,384,128]{2,1,0:T(8,128)S(1)}) custom-call(s32[6,2]{1,0:T(8,128)S(1)} %copy.13.refs_0_, bf16[4,256,256]{2,1,0:T(8,128)(2,1)S(1)} %copy-done.4, f32[2,128,128]{2,1,0:T(8,128)S(1)} %pad_maximum_fusion.refs_2_, f32[2,6,128,128]{3,2,1,0:T(8,128)S(1)} %get-tuple-element.87.refs_3_, ...), custom_call_target="tpu_custom_call" | custom-call | flops 1207959552 | bytes 3276848 | tf_op jit(solution)/shard_map/pallas_call | solution.py:319
  93.9 3.4 %collective-permute-done.23.from_left.refs_4_ = f32[2,384,128]{2,1,0:T(8,128)S(1)} collective-permute-done((f32[2,384,128]{2,1,0:T(8,128)S(1)}, f32[2,384,128]{2,1,0:T(8,128)S(1)}, u32[]{:S(2)}, u32[]{:S(2)}) %collective-permute-start.23) | collective-permute-done | bytes 393248 | tf_op jit(solution)/shard_map/ppermute | solution.py:354
  97.4 4.1 %collective-permute-done.21.from_left.refs_4_ = f32[2,384,128]{2,1,0:T(8,128)S(1)} collective-permute-done((f32[2,384,128]{2,1,0:T(8,128)S(1)}, f32[2,384,128]{2,1,0:T(8,128)S(1)}, u32[]{:S(2)}, u32[]{:S(2)}) %collective-permute-start.21) | collective-permute-done | bytes 393248 | tf_op jit(solution)/shard_map/ppermute | solution.py:354
  101.6 2.9 %collective-permute-done.26.refs_5_ = f32[2,128,256]{2,1,0:T(8,128)S(1)} collective-permute-done((f32[2,128,256]{2,1,0:T(8,128)S(1)}, f32[2,128,256]{2,1,0:T(8,128)S(1)}, u32[]{:S(2)}, u32[]{:S(2)}) %collective-permute-start.26) | collective-permute-done | bytes 262176 | tf_op jit(solution)/shard_map/ppermute | solution.py:354
  105.4 4.7 %collective-permute-done.24.refs_5_ = f32[2,128,256]{2,1,0:T(8,128)S(1)} collective-permute-done((f32[2,128,256]{2,1,0:T(8,128)S(1)}, f32[2,128,256]{2,1,0:T(8,128)S(1)}, u32[]{:S(2)}, u32[]{:S(2)}) %collective-permute-start.24) | collective-permute-done | bytes 262176 | tf_op jit(solution)/shard_map/ppermute | solution.py:354
  111.0 4.7 %collective-permute-done.22.refs_5_ = f32[2,128,256]{2,1,0:T(8,128)S(1)} collective-permute-done((f32[2,128,256]{2,1,0:T(8,128)S(1)}, f32[2,128,256]{2,1,0:T(8,128)S(1)}, u32[]{:S(2)}, u32[]{:S(2)}) %collective-permute-start.22) | collective-permute-done | bytes 262176 | tf_op jit(solution)/shard_map/ppermute | solution.py:354
  (75 shorter events, 31.6 us)
Async XLA Ops:
  1.9 14.4 %collective-permute-start = (f32[2,128,256]{2,1,0:T(8,128)}, f32[2,128,256]{2,1,0:T(8,128)S(1)}, u32[]{:S(2)}, u32[]{:S(2)}) collective-permute-start(f32[2,128,256]{2,1,0:T(8,128)} %get-tuple-element.51), channel_id=1, source_target_pairs={{8,0},{16,8},{24,16},{32,24},{40,32},{48,40},{56,48},{64,56},{72,6... | collective-permute-start | bytes 786440 | tf_op jit(solution)/shard_map/ppermute | solution.py:354
  11.9 9.0 %collective-permute-start.3 = (f32[2,128,256]{2,1,0:T(8,128)}, f32[2,128,256]{2,1,0:T(8,128)S(1)}, u32[]{:S(2)}, u32[]{:S(2)}) collective-permute-start(f32[2,128,256]{2,1,0:T(8,128)} %get-tuple-element.54), channel_id=1, source_target_pairs={{8,0},{16,8},{24,16},{32,24},{40,32},{48,40},{56,48},{64,56},{72,6... | collective-permute-start | bytes 786440 | tf_op jit(solution)/shard_map/ppermute | solution.py:354
  14.3 12.2 %collective-permute-start.6 = (f32[2,128,256]{2,1,0:T(8,128)}, f32[2,128,256]{2,1,0:T(8,128)S(1)}, u32[]{:S(2)}, u32[]{:S(2)}) collective-permute-start(f32[2,128,256]{2,1,0:T(8,128)} %get-tuple-element.57), channel_id=1, source_target_pairs={{8,0},{16,8},{24,16},{32,24},{40,32},{48,40},{56,48},{64,56},{72,6... | collective-permute-start | bytes 786440 | tf_op jit(solution)/shard_map/ppermute | solution.py:354
  14.8 13.3 %collective-permute-start.1 = (f32[2,256,128]{2,1,0:T(8,128)}, f32[2,256,128]{2,1,0:T(8,128)S(1)}, u32[]{:S(2)}, u32[]{:S(2)}) collective-permute-start(f32[2,256,128]{2,1,0:T(8,128)} %get-tuple-element.52), channel_id=1, source_target_pairs={{1,0},{2,1},{3,2},{4,3},{5,4},{6,5},{7,6},{0,7},{9,8},{10,9},{11,1... | collective-permute-start | bytes 786440 | tf_op jit(solution)/shard_map/ppermute | solution.py:354
  16.2 15.5 %collective-permute-start.4 = (f32[2,256,128]{2,1,0:T(8,128)}, f32[2,256,128]{2,1,0:T(8,128)S(1)}, u32[]{:S(2)}, u32[]{:S(2)}) collective-permute-start(f32[2,256,128]{2,1,0:T(8,128)} %get-tuple-element.55), channel_id=1, source_target_pairs={{1,0},{2,1},{3,2},{4,3},{5,4},{6,5},{7,6},{0,7},{9,8},{10,9},{11,1... | collective-permute-start | bytes 786440 | tf_op jit(solution)/shard_map/ppermute | solution.py:354
  16.9 11.3 %collective-permute-start.2 = (f32[2,128,128]{2,1,0:T(8,128)}, f32[2,128,128]{2,1,0:T(8,128)S(1)}, u32[]{:S(2)}, u32[]{:S(2)}) collective-permute-start(f32[2,128,128]{2,1,0:T(8,128)} %slice.12), channel_id=1, source_target_pairs={{1,0},{2,1},{3,2},{4,3},{5,4},{6,5},{7,6},{0,7},{9,8},{10,9},{11,1... | collective-permute-start | bytes 393224 | tf_op jit(solution)/shard_map/ppermute | solution.py:354
  20.9 14.4 %collective-permute-start.7 = (f32[2,256,128]{2,1,0:T(8,128)}, f32[2,256,128]{2,1,0:T(8,128)S(1)}, u32[]{:S(2)}, u32[]{:S(2)}) collective-permute-start(f32[2,256,128]{2,1,0:T(8,128)} %get-tuple-element.58), channel_id=1, source_target_pairs={{1,0},{2,1},{3,2},{4,3},{5,4},{6,5},{7,6},{0,7},{9,8},{10,9},{11,1... | collective-permute-start | bytes 786440 | tf_op jit(solution)/shard_map/ppermute | solution.py:354
  28.2 7.1 %collective-permute-start.8 = (f32[2,128,128]{2,1,0:T(8,128)S(1)}, f32[2,128,128]{2,1,0:T(8,128)S(1)}, u32[]{:S(2)}, u32[]{:S(2)}) collective-permute-start(f32[2,128,128]{2,1,0:T(8,128)S(1)} %slice.14), channel_id=1, source_target_pairs={{1,0},{2,1},{3,2},{4,3},{5,4},{6,5},{7,6},{0,7},{9,8},{10,9},{11,1... | collective-permute-start | bytes 393224 | tf_op jit(solution)/shard_map/ppermute | solution.py:354
  43.6 7.0 %collective-permute-start.9 = (f32[2,384,128]{2,1,0:T(8,128)S(1)}, f32[2,384,128]{2,1,0:T(8,128)S(1)}, u32[]{:S(2)}, u32[]{:S(2)}) collective-permute-start(f32[2,384,128]{2,1,0:T(8,128)S(1)} %get-tuple-element.64), channel_id=1, source_target_pairs={{7,0},{0,1},{1,2},{2,3},{3,4},{4,5},{5,6},{6,7},{15,8},{8,9},{9,10... | collective-permute-start | bytes 1179656 | tf_op jit(solution)/shard_map/ppermute | solution.py:354
  45.9 10.4 %collective-permute-start.13 = (f32[2,384,128]{2,1,0:T(8,128)S(1)}, f32[2,384,128]{2,1,0:T(8,128)S(1)}, u32[]{:S(2)}, u32[]{:S(2)}) collective-permute-start(f32[2,384,128]{2,1,0:T(8,128)S(1)} %get-tuple-element.72), channel_id=1, source_target_pairs={{7,0},{0,1},{1,2},{2,3},{3,4},{4,5},{5,6},{6,7},{15,8},{8,9},{9,10... | collective-permute-start | bytes 1179656 | tf_op jit(solution)/shard_map/ppermute | solution.py:354
  46.0 15.3 %collective-permute-start.17 = (f32[2,384,128]{2,1,0:T(8,128)S(1)}, f32[2,384,128]{2,1,0:T(8,128)S(1)}, u32[]{:S(2)}, u32[]{:S(2)}) collective-permute-start(f32[2,384,128]{2,1,0:T(8,128)S(1)} %get-tuple-element.80), channel_id=1, source_target_pairs={{7,0},{0,1},{1,2},{2,3},{3,4},{4,5},{5,6},{6,7},{15,8},{8,9},{9,10... | collective-permute-start | bytes 1179656 | tf_op jit(solution)/shard_map/ppermute | solution.py:354
  50.7 11.7 %collective-permute-start.10 = (f32[2,128,256]{2,1,0:T(8,128)S(1)}, f32[2,128,256]{2,1,0:T(8,128)S(1)}, u32[]{:S(2)}, u32[]{:S(2)}) collective-permute-start(f32[2,128,256]{2,1,0:T(8,128)S(1)} %get-tuple-element.65), channel_id=1, source_target_pairs={{248,0},{0,8},{8,16},{16,24},{24,32},{32,40},{40,48},{48,56},{56,6... | collective-permute-start | bytes 786440 | tf_op jit(solution)/shard_map/ppermute | solution.py:354
  50.8 15.3 %collective-permute-start.11 = (f32[2,128,256]{2,1,0:T(8,128)S(1)}, f32[2,128,256]{2,1,0:T(8,128)S(1)}, u32[]{:S(2)}, u32[]{:S(2)}) collective-permute-start(f32[2,128,256]{2,1,0:T(8,128)S(1)} %get-tuple-element.66), channel_id=1, source_target_pairs={{8,0},{16,8},{24,16},{32,24},{40,32},{48,40},{56,48},{64,56},{72,6... | collective-permute-start | bytes 786440 | tf_op jit(solution)/shard_map/ppermute | solution.py:354
  56.4 11.8 %collective-permute-start.14 = (f32[2,128,256]{2,1,0:T(8,128)S(1)}, f32[2,128,256]{2,1,0:T(8,128)S(1)}, u32[]{:S(2)}, u32[]{:S(2)}) collective-permute-start(f32[2,128,256]{2,1,0:T(8,128)S(1)} %get-tuple-element.73), channel_id=1, source_target_pairs={{248,0},{0,8},{8,16},{16,24},{24,32},{32,40},{40,48},{48,56},{56,6... | collective-permute-start | bytes 786440 | tf_op jit(solution)/shard_map/ppermute | solution.py:354
  56.5 11.8 %collective-permute-start.15 = (f32[2,128,256]{2,1,0:T(8,128)S(1)}, f32[2,128,256]{2,1,0:T(8,128)S(1)}, u32[]{:S(2)}, u32[]{:S(2)}) collective-permute-start(f32[2,128,256]{2,1,0:T(8,128)S(1)} %get-tuple-element.74), channel_id=1, source_target_pairs={{8,0},{16,8},{24,16},{32,24},{40,32},{48,40},{56,48},{64,56},{72,6... | collective-permute-start | bytes 786440 | tf_op jit(solution)/shard_map/ppermute | solution.py:354
  61.3 12.4 %collective-permute-start.18 = (f32[2,128,256]{2,1,0:T(8,128)S(1)}, f32[2,128,256]{2,1,0:T(8,128)S(1)}, u32[]{:S(2)}, u32[]{:S(2)}) collective-permute-start(f32[2,128,256]{2,1,0:T(8,128)S(1)} %get-tuple-element.81), channel_id=1, source_target_pairs={{248,0},{0,8},{8,16},{16,24},{24,32},{32,40},{40,48},{48,56},{56,6... | collective-permute-start | bytes 786440 | tf_op jit(solution)/shard_map/ppermute | solution.py:354
  62.4 11.3 %collective-permute-start.19 = (f32[2,128,256]{2,1,0:T(8,128)S(1)}, f32[2,128,256]{2,1,0:T(8,128)S(1)}, u32[]{:S(2)}, u32[]{:S(2)}) collective-permute-start(f32[2,128,256]{2,1,0:T(8,128)S(1)} %get-tuple-element.82), channel_id=1, source_target_pairs={{8,0},{16,8},{24,16},{32,24},{40,32},{48,40},{56,48},{64,56},{72,6... | collective-permute-start | bytes 786440 | tf_op jit(solution)/shard_map/ppermute | solution.py:354
  66.3 10.6 %collective-permute-start.12 = (f32[2,384,128]{2,1,0:T(8,128)S(1)}, f32[2,384,128]{2,1,0:T(8,128)S(1)}, u32[]{:S(2)}, u32[]{:S(2)}) collective-permute-start(f32[2,384,128]{2,1,0:T(8,128)S(1)} %get-tuple-element.67.refs_4_.refs_0_), channel_id=1, source_target_pairs={{1,0},{2,1},{3,2},{4,3},{5,4},{6,5},{7,6},{0,7},{9,8},{10,9},{11,1... | collective-permute-start | bytes 1179656 | tf_op jit(solution)/shard_map/ppermute | solution.py:354
  68.4 12.7 %collective-permute-start.16 = (f32[2,384,128]{2,1,0:T(8,128)S(1)}, f32[2,384,128]{2,1,0:T(8,128)S(1)}, u32[]{:S(2)}, u32[]{:S(2)}) collective-permute-start(f32[2,384,128]{2,1,0:T(8,128)S(1)} %get-tuple-element.75.refs_4_.refs_0_), channel_id=1, source_target_pairs={{1,0},{2,1},{3,2},{4,3},{5,4},{6,5},{7,6},{0,7},{9,8},{10,9},{11,1... | collective-permute-start | bytes 1179656 | tf_op jit(solution)/shard_map/ppermute | solution.py:354
  73.9 11.4 %collective-permute-start.20 = (f32[2,384,128]{2,1,0:T(8,128)S(1)}, f32[2,384,128]{2,1,0:T(8,128)S(1)}, u32[]{:S(2)}, u32[]{:S(2)}) collective-permute-start(f32[2,384,128]{2,1,0:T(8,128)S(1)} %get-tuple-element.83.refs_4_.refs_0_), channel_id=1, source_target_pairs={{1,0},{2,1},{3,2},{4,3},{5,4},{6,5},{7,6},{0,7},{9,8},{10,9},{11,1... | collective-permute-start | bytes 1179656 | tf_op jit(solution)/shard_map/ppermute | solution.py:354
  93.7 7.8 %collective-permute-start.21 = (f32[2,384,128]{2,1,0:T(8,128)S(1)}, f32[2,384,128]{2,1,0:T(8,128)S(1)}, u32[]{:S(2)}, u32[]{:S(2)}) collective-permute-start(f32[2,384,128]{2,1,0:T(8,128)S(1)} %get-tuple-element.90), channel_id=1, source_target_pairs={{7,0},{0,1},{1,2},{2,3},{3,4},{4,5},{5,6},{6,7},{15,8},{8,9},{9,10... | collective-permute-start | bytes 1179656 | tf_op jit(solution)/shard_map/ppermute | solution.py:354
  93.8 10.8 %collective-permute-start.26 = (f32[2,128,256]{2,1,0:T(8,128)S(1)}, f32[2,128,256]{2,1,0:T(8,128)S(1)}, u32[]{:S(2)}, u32[]{:S(2)}) collective-permute-start(f32[2,128,256]{2,1,0:T(8,128)S(1)} %shard_map.82), channel_id=1, source_target_pairs={{248,0},{0,8},{8,16},{16,24},{24,32},{32,40},{40,48},{48,56},{56,6... | collective-permute-start | bytes 786440 | tf_op jit(solution)/shard_map/ppermute | solution.py:354
  97.3 12.9 %collective-permute-start.24 = (f32[2,128,256]{2,1,0:T(8,128)S(1)}, f32[2,128,256]{2,1,0:T(8,128)S(1)}, u32[]{:S(2)}, u32[]{:S(2)}) collective-permute-start(f32[2,128,256]{2,1,0:T(8,128)S(1)} %shard_map.81), channel_id=1, source_target_pairs={{248,0},{0,8},{8,16},{16,24},{24,32},{32,40},{40,48},{48,56},{56,6... | collective-permute-start | bytes 786440 | tf_op jit(solution)/shard_map/ppermute | solution.py:354
  101.5 14.3 %collective-permute-start.22 = (f32[2,128,256]{2,1,0:T(8,128)S(1)}, f32[2,128,256]{2,1,0:T(8,128)S(1)}, u32[]{:S(2)}, u32[]{:S(2)}) collective-permute-start(f32[2,128,256]{2,1,0:T(8,128)S(1)} %shard_map.80), channel_id=1, source_target_pairs={{248,0},{0,8},{8,16},{16,24},{24,32},{32,40},{40,48},{48,56},{56,6... | collective-permute-start | bytes 786440 | tf_op jit(solution)/shard_map/ppermute | solution.py:354
  (10 other events, 90.3 us)
where the time goes:
time: 119 us; the launch traced here: 117 us
  waiting for transfers between devices  40 us (34%)
  starting transfers between devices  37.8 us (32%)
  Pallas kernels  35.8 us (30%)
  local copies, waits for them, and re-layouts  2.73 us (2%)
    ppermute x27, waiting for transfers between devices, shifted(): lax.ppermute(block, axis, [((i - distance) % size, i) for i in range(size)])  40 us
    ppermute x27, starting transfers between devices, shifted(): lax.ppermute(block, axis, [((i - distance) % size, i) for i in range(size)])  37.8 us
    pallas_call x10, Pallas kernels, run(): pl.pallas_call(body, grid=(1,), in_specs=in_specs, out_specs=[whole(o) fo...  26.9 us
    pallas_call x3, Pallas kernels, pack(): pl.pallas_call(functools.partial(pack_kernel, layer), in_specs=[pl.BlockS...  5.56 us
    pallas_call x12, Pallas kernels, plain(): pl.pallas_call(body, grid=(1,), in_specs=[specs.get(n, None) or whole(o)...  3.31 us
  transfers between devices with their start and end apart: 27, of which 14 were waited for; matrix products, arithmetic and copies ran while one was open for 1% of the time, Pallas kernels for 19%

commit v1 on v0

--- a/solution.py
+++ b/solution.py
@@ -181,9 +181,10 @@
 
 
 def forward_kernel(fill, n_field, first, *refs):
-    offset_ref, table_ref, phase_ref, wave = refs[:4]
-    field = refs[4 : 4 + n_field]
-    windows, out, ext, work = refs[4 + n_field :]
+    offset_ref, table_ref, phase_ref = refs[:3]
+    wave = None if first else refs[3]
+    field = refs[4 - first : 4 - first + n_field]
+    windows, out, ext, work = refs[4 - first + n_field :]
     fill(ext, field)
     right, left = tables_of(table_ref)
     for n in range(PAIRS):
@@ -194,7 +195,7 @@
             windows[0, q] = tr
             windows[1, q] = ti
             if first:
-                wr, wi = wave[0], wave[1]
+                wr, wi = phase_ref[0], phase_ref[1]
             else:
                 wr, wi = wave[0, q], wave[1, q]
             rows.append(jnp.concatenate(times(wr, wi, tr, ti), axis=1))
@@ -203,20 +204,24 @@
     def finish(n, block):
         put_pair(out, 2 * n, block)
 
-    propagate(work, right, left, phase_ref[0], phase_ref[1], finish)
+    propagate(work, right, left, phase_ref[2], phase_ref[3], finish)
 
 
 def write_gradient(grads, outs):
-    for n, out in enumerate(outs):
-        for part in range(2):
-            out[part] = grads[part][:, n * PROBE : (n + 1) * PROBE]
+    left, middle, low, right = outs
+    h, t = PROBE, TILE
+    for part in range(2):
+        left[part] = grads[part][:, :h]
+        middle[part] = grads[part][:t, h:t]
+        low[part] = grads[part][t:, h:t]
+        right[part] = grads[part][:, t:]
 
 
 def turn_kernel(fill, n_field, *refs):
     offset_ref, table_ref, intensity, wave = refs[:4]
     field = refs[4 : 4 + n_field]
-    outs = refs[4 + n_field : 7 + n_field]
-    back, ext, windows, work, turned, *grads = refs[7 + n_field :]
+    outs = refs[4 + n_field : 8 + n_field]
+    back, ext, windows, work, turned, *grads = refs[8 + n_field :]
     fill(ext, field)
     for part in grads:
         part[...] = jnp.zeros_like(part)
@@ -258,11 +263,11 @@
 
 def backward_kernel(first, *refs):
     if first:
-        offset_ref, table_ref, phase_ref, back_in, wave = refs[:5]
-        outs = refs[5:8]
+        offset_ref, table_ref, phase_ref, back_in = refs[:4]
+        outs = refs[4:8]
     else:
         offset_ref, table_ref, phase_ref, back_in, wave, windows = refs[:6]
-        outs, back = refs[6:9], refs[9]
+        outs, back = refs[6:10], refs[10]
     work, turned, *grads = refs[-4:]
     for part in grads:
         part[...] = jnp.zeros_like(part)
@@ -276,7 +281,7 @@
             q = 2 * n + i
             gr, gi = block[i * h : (i + 1) * h, :h], block[i * h : (i + 1) * h, h:]
             if first:
-                dr, di = times_conj(wave[0], wave[1], gr, gi)
+                dr, di = times_conj(phase_ref[0], phase_ref[1], gr, gi)
             else:
                 br, bi = times_conj(windows[0, q], windows[1, q], gr, gi)
                 back[0, q] = br
@@ -285,7 +290,7 @@
             turned[0, q] = turn_window(offset_ref, q, dr)
             turned[1, q] = turn_window(offset_ref, q, di)
 
-    propagate(work, right, left, phase_ref[0], -phase_ref[1], finish)
+    propagate(work, right, left, phase_ref[2], -phase_ref[3], finish)
     add_windows(grads, offset_ref, turned)
     write_gradient(grads, outs)
 
@@ -304,7 +309,12 @@
 
 
 STACK = (2, POS, PROBE, PROBE)
-GRADIENT = [shape(2, EXT, PROBE)] * 3
+GRADIENT = [
+    shape(2, EXT, PROBE),
+    shape(2, TILE, PROBE),
+    shape(2, PROBE, PROBE),
+    shape(2, EXT, PROBE),
+]
 WORK = pltpu.VMEM((2, PAIRS, 2, 256, 256), BF16)
 SCRATCH = pltpu.VMEM((2, EXT, EXT), F32)
 GRADS = [pltpu.VMEM((2, POS, TALL, PROBE), F32)] + [pltpu.VMEM((EXT, EXT), F32)] * 2
@@ -328,23 +338,34 @@
     )(*operands)
 
 
-def forward(offsets, tables, phase, wave, field, layer, fill, first):
-    operands = [offsets, tables, phase, wave, *field]
-    specs = {4: tile_of(layer)} if fill is fill_first else {}
+def field_specs(start, layer, fill):
+    if fill is not fill_first:
+        return {}
+    specs = {start: tile_of(layer)}
+    if layer > 0:
+        specs[start + 2] = pl.BlockSpec((2, None, TILE, PROBE), lambda i: (0, layer - 1, 0, 0))
+    return specs
+
+
+def forward(offsets, tables, phase, wave, field, layer, fill):
+    first = wave is None
+    operands = [offsets, tables, phase] + ([] if first else [wave])
+    specs = field_specs(len(operands), layer, fill)
     body = functools.partial(forward_kernel, fill, len(field), first)
-    return run(body, operands, [shape(*STACK)] * 2, [SCRATCH, WORK], 4, specs)
+    return run(body, operands + field, [shape(*STACK)] * 2, [SCRATCH, WORK], 4, specs)
 
 
 def turn(offsets, tables, intensity, wave, field, layer, fill):
-    operands = [offsets, tables, intensity, wave, *field]
-    specs = {4: tile_of(layer)} if fill is fill_first else {}
+    operands = [offsets, tables, intensity, wave]
+    specs = field_specs(len(operands), layer, fill)
     body = functools.partial(turn_kernel, fill, len(field))
-    return run(body, operands, [*GRADIENT, shape(*STACK)], [SCRATCH, pltpu.VMEM(STACK, F32), WORK, *GRADS], 4, specs)
+    scratch = [SCRATCH, pltpu.VMEM(STACK, F32), WORK, *GRADS]
+    return run(body, operands + field, [*GRADIENT, shape(*STACK)], scratch, 4, specs)
 
 
 def backward(offsets, tables, phase, back, wave, windows):
-    first = windows is None
-    operands = [offsets, tables, phase, back, wave] + ([] if first else [windows])
+    first = wave is None
+    operands = [offsets, tables, phase, back] + ([] if first else [wave, windows])
     outs = [*GRADIENT] if first else [*GRADIENT, shape(*STACK)]
     return run(functools.partial(backward_kernel, first), operands, outs, [WORK, *GRADS], 4)
 
@@ -352,6 +373,14 @@
 def shifted(block, axis, distance):
     size = lax.axis_size(axis)
     return lax.ppermute(block, axis, [((i - distance) % size, i) for i in range(size)])
+
+
+def swapped(block, odd):
+    size = lax.axis_size("row")
+    route = []
+    for i in range(odd, size + odd, 2):
+        route += [(i % size, (i + 1) % size), ((i + 1) % size, i % size)]
+    return lax.ppermute(block, "row", sorted(route))
 
 
 def plain(body, outs, operands, specs=None, aliases=None, out_specs=None):
@@ -369,81 +398,131 @@
     )(*operands)
 
 
-ROWS = shape(2, PROBE, TILE)
+IN_SMEM = pl.BlockSpec(memory_space=pltpu.SMEM)
 SIDE = shape(2, EXT, PROBE)
 
 
-def pack_kernel(layer, tile, rows, cols, sems):
-    first = pltpu.make_async_copy(tile.at[:, layer, pl.ds(0, PROBE)], rows, sems.at[0])
-    second = pltpu.make_async_copy(tile.at[:, layer, :, pl.ds(0, PROBE)], cols, sems.at[1])
-    first.start()
-    second.start()
-    first.wait()
-    second.wait()
-
-
-def pack(object_field, layer):
-    cols = shape(2, TILE, PROBE)
+def pack_kernel(jobs, tile, *refs):
+    outs, sems = refs[:-1], refs[-1]
+    copies = [
+        pltpu.make_async_copy(tile.at[:, layer, rows, cols], out, sems.at[n])
+        for n, ((layer, rows, cols), out) in enumerate(zip(jobs, outs))
+    ]
+    for copy in copies:
+        copy.start()
+    for copy in copies:
+        copy.wait()
+
+
+def pack(object_field, jobs, outs):
     return pl.pallas_call(
-        functools.partial(pack_kernel, layer),
+        functools.partial(pack_kernel, jobs),
         in_specs=[pl.BlockSpec(memory_space=pltpu.HBM)],
-        out_specs=[pl.BlockSpec(memory_space=pltpu.VMEM)] * 2,
-        out_shape=[ROWS, cols],
-        scratch_shapes=[pltpu.SemaphoreType.DMA((2,))],
+        out_specs=[pl.BlockSpec(memory_space=pltpu.VMEM)] * len(outs),
+        out_shape=outs,
+        scratch_shapes=[pltpu.SemaphoreType.DMA((len(outs),))],
         name="pack",
         cost_estimate=pl.CostEstimate(flops=0, bytes_accessed=4 * 2**18, transcendentals=0),
     )(object_field)
 
 
-def sums_kernel(both, left, middle, from_left, *outs):
+def sums_kernel(wide, parity, left, middle, low, right, from_left, *refs):
     h, t = PROBE, TILE
-    down = outs[0]
-    down[:, :, :h] = left[:, t:] + from_left[:, t:]
-    down[:, :, h:] = middle[:, t:]
-    if both:
-        up = outs[1]
+    from_right = refs[0] if wide else None
+    even_out, odd_out = refs[-2:]
+
+    def fill(down, up):
+        down[:, :, :h] = left[:, t:] + from_left[:, t:]
         up[:, :, :h] = left[:, :h] + from_left[:, :h]
-        up[:, :, h:] = middle[:, :h]
-
-
-def sums(left, middle, from_left, both):
-    body = functools.partial(sums_kernel, both)
-    return plain(body, [ROWS] * (1 + both), [left, middle, from_left])
-
-
-def update_kernel(tile, low, left, middle, from_left, above, below, new_l, new_m):
+        down[:, :, h:t] = low[...]
+        up[:, :, h:t] = middle[:, :h]
+        if wide:
+            down[:, :, t:] = right[:, t:] + from_right[:, t:]
+            up[:, :, t:] = right[:, :h] + from_right[:, :h]
+
+    @pl.when(parity[0] == 0)
+    def _():
+        fill(even_out, odd_out)
+
+    @pl.when(parity[0] == 1)
+    def _():
+        fill(odd_out, even_out)
+
+
+def sums(parity, grad, from_left, from_right):
+    wide = from_right is not None
+    operands = [parity, *grad, from_left] + ([from_right] if wide else [])
+    outs = [shape(2, PROBE, EXT if wide else TILE)] * 2
+    return plain(functools.partial(sums_kernel, wide), outs, operands, {0: IN_SMEM})
+
+
+def update_kernel(wide, parity, *refs):
     h, t = PROBE, TILE
+    if wide:
+        tile, low, side, corner, left, middle, bottom, right, from_left, from_right, even, odd = refs[:12]
+        new_l, new_m, new_r = refs[12:]
+    else:
+        tile, low, left, middle, bottom, from_left, even, odd, new_l, new_m = refs
     top, mid, end = slice(0, h), slice(h, t), slice(t, t + h)
-    for new, grad, cols in ((new_l, left, slice(0, h)), (new_m, middle, slice(h, t))):
-        extra = (lambda rows: grad[:, rows] + from_left[:, rows]) if new is new_l else (lambda rows: grad[:, rows])
-        new[:, top] = tile[:, 0, top, cols] - STEP * (extra(top) + above[:, :, cols])
-        new[:, mid] = tile[:, 0, mid, cols] - STEP * extra(mid)
-        new[:, end] = low[:, :, cols] - STEP * (extra(end) + below[:, :, cols])
-
-
-def update(object_field, layer, low, grad, from_left, above, below):
-    operands = [object_field, low, grad[0], grad[1], from_left, above, below]
-    return plain(update_kernel, [SIDE] * 2, operands, {0: tile_of(layer)})
+    first, second, third = slice(0, h), slice(h, t), slice(t, t + h)
+
+    swap = parity[0] == 1
+
+    class Chosen:
+        def __init__(self, first, second):
+            self.first, self.second = first, second
+
+        def __getitem__(self, where):
+            return jnp.where(swap, self.second[where], self.first[where])
+
+    def fill(above, below):
+        new_l[:, top] = tile[:, 0, top, first] - STEP * (left[:, top] + from_left[:, top] + above[:, :, first])
+        new_l[:, mid] = tile[:, 0, mid, first] - STEP * (left[:, mid] + from_left[:, mid])
+        new_l[:, end] = low[:, :, first] - STEP * (left[:, end] + from_left[:, end] + below[:, :, first])
+        new_m[:, top] = tile[:, 0, top, second] - STEP * (middle[:, top] + above[:, :, second])
+        new_m[:, mid] = tile[:, 0, mid, second] - STEP * middle[:, mid]
+        new_m[:, end] = low[:, :, second] - STEP * (bottom[...] + below[:, :, second])
+        if wide:
+            new_r[:, top] = side[:, top] - STEP * (right[:, top] + from_right[:, top] + above[:, :, third])
+            new_r[:, mid] = side[:, mid] - STEP * (right[:, mid] + from_right[:, mid])
+            new_r[:, end] = corner[...] - STEP * (right[:, end] + from_right[:, end] + below[:, :, third])
+
+    fill(Chosen(odd, even), Chosen(even, odd))
+
+
+def update(parity, layer, field, grad, from_left, from_right, even, odd):
+    tile, low, side, corner = field
+    if from_right is None:
+        operands = [parity, tile, low, *grad[:3], from_left, even, odd]
+        specs = {0: IN_SMEM, 1: tile_of(layer)}
+        return plain(functools.partial(update_kernel, False), [SIDE] * 2, operands, specs)
+    operands = [parity, tile, low, side, corner, *grad, from_left, from_right, even, odd]
+    specs = {0: IN_SMEM, **field_specs(1, layer, fill_first)}
+    return plain(functools.partial(update_kernel, True), [SIDE] * 3, operands, specs)
+
+
+def spill_kernel(left, from_left, down):
+    down[...] = left[:, TILE:] + from_left[:, TILE:]
 
 
 def last_kernel(n_alias, *refs):
-    old_l, old_m, left, middle, from_left, above = refs[:6]
-    out = refs[6 + n_alias]
+    old_l, old_m, left, middle, from_left, above_l, above_m = refs[:7]
+    out = refs[7 + n_alias]
     h, t = PROBE, TILE
-    out[:, 0, :h, :h] = old_l[:, :h] - STEP * (left[:, :h] + from_left[:, :h] + above[:, :, :h])
+    out[:, 0, :h, :h] = old_l[:, :h] - STEP * (left[:, :h] + from_left[:, :h] + above_l[...])
     out[:, 0, h:, :h] = old_l[:, h:t] - STEP * (left[:, h:t] + from_left[:, h:t])
-    out[:, 0, :h, h:] = old_m[:, :h] - STEP * (middle[:, :h] + above[:, :, h:])
+    out[:, 0, :h, h:] = old_m[:, :h] - STEP * (middle[:, :h] + above_m[...])
     out[:, 0, h:, h:] = old_m[:, h:t] - STEP * middle[:, h:t]
 
 
-def last(result, layer, field, grad, from_left, above):
-    operands = [field[0], field[1], grad[0], grad[1], from_left, above]
+def last(result, layer, field, grad, from_left, above_l, above_m):
+    operands = [field[0], field[1], grad[0], grad[1], from_left, above_l, above_m]
     specs, aliases = {}, {}
     if result is not None:
         operands.append(result)
-        specs, aliases = {6: pl.BlockSpec(memory_space=pl.ANY)}, {6: 0}
+        specs, aliases = {7: pl.BlockSpec(memory_space=pl.ANY)}, {7: 0}
     return plain(
-        functools.partial(last_kernel, len(operands) - 6),
+        functools.partial(last_kernel, len(operands) - 7),
         [shape(2, SLICES, TILE, TILE)],
         operands,
         specs,
@@ -453,47 +532,62 @@
 
 
 def on_device(object_field, probe, propagator, measured, offsets):
-    h = PROBE
+    h, t = PROBE, TILE
     tables = jnp.asarray(dft_tables())
     offsets = offsets.reshape(POS, 2)
     intensity = measured.reshape(POS, h, h)
-    phase = jnp.stack([jnp.cos(propagator), jnp.sin(propagator)])
-
-    packed = [pack(object_field, layer) for layer in range(SLICES)]
-    lows, fields = [], []
-    for rows, cols in packed:
+    phase = jnp.stack([probe[0], probe[1], jnp.cos(propagator), jnp.sin(propagator)])
+    parity = (lax.axis_index("row") & 1).astype(jnp.int32).reshape(1)
+
+    top, all_rows, left, all_cols = pl.ds(0, h), pl.ds(0, t), pl.ds(0, h), pl.ds(0, t)
+    rows_shape = shape(2, h, t)
+    rows0, cols0 = pack(
+        object_field, [(0, top, all_cols), (0, all_rows, left)], [rows_shape, shape(2, t, h)]
+    )
+    rows1, rows2, cols12 = pack(
+        object_field,
+        [(1, top, all_cols), (2, top, all_cols), (pl.ds(1, 2), all_rows, left)],
+        [rows_shape, rows_shape, shape(2, 2, t, h)],
+    )
+    right0 = shifted(cols0, "col", -1)
+    right12 = shifted(cols12, "col", -1)
+    fields = []
+    for layer, rows in enumerate((rows0, rows1, rows2)):
         low = shifted(rows, "row", -1)
-        right = shifted(cols, "col", -1)
         corner = shifted(low[:, :, :h], "col", -1)
-        lows.append(low)
-        fields.append([object_field, low, right, corner])
+        fields.append([object_field, low, right0 if layer == 0 else right12, corner])
 
     def gradients(fields, fill):
-        _, wave1 = forward(offsets, tables, phase, probe, fields[0], 0, fill, True)
-        win1, wave2 = forward(offsets, tables, phase, wave1, fields[1], 1, fill, False)
+        _, wave1 = forward(offsets, tables, phase, None, fields[0], 0, fill)
+        win1, wave2 = forward(offsets, tables, phase, wave1, fields[1], 1, fill)
         *grad2, back = turn(offsets, tables, intensity, wave2, fields[2], 2, fill)
         *grad1, back = backward(offsets, tables, phase, back, wave1, win1)
-        grad0 = backward(offsets, tables, phase, back, probe, None)
+        grad0 = backward(offsets, tables, phase, back, None, None)
         return [grad0, grad1, grad2]
 
     grads = gradients(fields, fill_first)
-    fields = [None] * SLICES
-    for layer in (2, 1, 0):
-        grad = grads[layer]
-        from_left = shifted(grad[2], "col", 1)
-        down, up = sums(grad[0], grad[1], from_left, True)
-        above = shifted(down, "row", 1)
-        below = shifted(up, "row", -1)
-        new_l, new_m = update(object_field, layer, lows[layer], grad, from_left, above, below)
-        fields[layer] = [new_l, new_m, shifted(new_l, "col", -1)]
-    grads = gradients(fields, fill_next)
+    renewed = [None] * SLICES
+    for layer in (2, 0, 1):
+        grad, from_right = grads[layer], None
+        from_left = shifted(grad[3], "col", 1)
+        if layer == 1:
+            from_right = shifted(grad[0], "col", -1)
+        for_even, for_odd = sums(parity, grad, from_left, from_right)
+        even = swapped(for_even, 0)
+        odd = swapped(for_odd, 1)
+        new = update(parity, layer, fields[layer], grad, from_left, from_right, even, odd)
+        if layer != 1:
+            new = [*new, shifted(new[0], "col", -1)]
+        renewed[layer] = list(new)
+    grads = gradients(renewed, fill_next)
     result = None
     for layer in (2, 1, 0):
         grad = grads[layer]
-        from_left = shifted(grad[2], "col", 1)
-        down = sums(grad[0], grad[1], from_left, False)[0]
-        above = shifted(down, "row", 1)
-        result = last(result, layer, fields[layer], grad, from_left, above)
+        from_left = shifted(grad[3], "col", 1)
+        above_m = shifted(grad[2], "row", 1)
+        down = plain(spill_kernel, [shape(2, h, h)], [grad[0], from_left])[0]
+        above_l = shifted(down, "row", 1)
+        result = last(result, layer, renewed[layer], grad, from_left, above_l, above_m)
     return result
 
 

time: 119 us -> 127 us (1.067)
  the two profiles are of different devices: /device:TPU:7 before, /device:TPU:1 now
where the time goes in v1:
time: 127 us
  starting transfers between devices  50.4 us (40%)
  Pallas kernels  41.5 us (33%)
  waiting for transfers between devices  26.9 us (21%)
  local copies, waits for them, and re-layouts  6.84 us (5%)
    ppermute x23, starting transfers between devices, shifted(): lax.ppermute(block, axis, [((i - distance) % size, i) for i in range(size)])  38.4 us
    pallas_call x10, Pallas kernels, run(): pl.pallas_call(body, grid=(1,), in_specs=in_specs, out_specs=[whole(o) fo...  29.2 us
    ppermute x23, waiting for transfers between devices, shifted(): lax.ppermute(block, axis, [((i - distance) % size, i) for i in range(size)])  26.4 us
    ppermute x6, starting transfers between devices, swapped(): return lax.ppermute(block, 'row', sorted(route))  12 us
    pallas_call x12, Pallas kernels, plain(): pl.pallas_call(body, grid=(1,), in_specs=[specs.get(n, None) or whole(o)...  8.19 us
    unnamed x70, local copies, waits for them, and re-layouts  5.09 us
    pallas_call x2, Pallas kernels, pack(): pl.pallas_call(functools.partial(pack_kernel, jobs), in_specs=[pl.BlockSp...  4.13 us
  transfers between devices with their start and end apart: 29, of which 10 were waited for; matrix products, arithmetic and copies ran while one was open for 2% of the time, Pallas kernels for 20%

profile of v1, /device:TPU:1, one launch (start us, length us, event | category | flops | bytes accessed | tf_op | source)
XLA Modules:
  0.0 127.1 jit_solution(6099550754939675155)
XLA Ops:
  1.9 8.9 %collective-permute-start = (f32[2,128,256]{2,1,0:T(8,128)}, f32[2,128,256]{2,1,0:T(8,128)S(1)}, u32[]{:S(2)}, u32[]{:S(2)}) collective-permute-start(f32[2,128,256]{2,1,0:T(8,128)} %get-tuple-element.57), channel_id=1, source_target_pairs={{8,0},{16,8},{24,16},{32,24},{40,32},{48,40},{56,48},{64,56},{72,6... | collective-permute-start | bytes 786440 | tf_op jit(solution)/shard_map/ppermute | solution.py:375
  10.8 2.3 %pack.3 = (f32[2,128,256]{2,1,0:T(8,128)}, f32[2,128,256]{2,1,0:T(8,128)}, f32[2,2,256,128]{3,2,1,0:T(8,128)}) custom-call(f32[2,3,256,256]{3,2,1,0:T(8,128)} %refs_0_.5), custom_call_target="tpu_custom_call" | custom-call | bytes 1048576 | tf_op jit(solution)/shard_map/pack/pallas_call | solution.py:418
  14.5 2.2 %collective-permute-start.1 = (f32[2,256,128]{2,1,0:T(8,128)}, f32[2,256,128]{2,1,0:T(8,128)S(1)}, u32[]{:S(2)}, u32[]{:S(2)}) collective-permute-start(f32[2,256,128]{2,1,0:T(8,128)} %get-tuple-element.58), channel_id=1, source_target_pairs={{1,0},{2,1},{3,2},{4,3},{5,4},{6,5},{7,6},{0,7},{9,8},{10,9},{11,1... | collective-permute-start | bytes 786440 | tf_op jit(solution)/shard_map/ppermute | solution.py:375
  22.4 3.6 %collective-permute-start.5 = (f32[2,128,128]{2,1,0:T(8,128)}, f32[2,128,128]{2,1,0:T(8,128)S(1)}, u32[]{:S(2)}, u32[]{:S(2)}) collective-permute-start(f32[2,128,128]{2,1,0:T(8,128)} %slice.16), channel_id=1, source_target_pairs={{1,0},{2,1},{3,2},{4,3},{5,4},{6,5},{7,6},{0,7},{9,8},{10,9},{11,1... | collective-permute-start | bytes 393224 | tf_op jit(solution)/shard_map/ppermute | solution.py:375
  30.0 2.9 %shard_map.64 = (f32[2,6,128,128]{3,2,1,0:T(8,128)}, f32[2,6,128,128]{3,2,1,0:T(8,128)S(1)}) custom-call(s32[6,2]{1,0:T(8,128)S(1)} %copy.13.refs_0_, bf16[4,256,256]{2,1,0:T(8,128)(2,1)S(1)} %copy-done.30, f32[4,128,128]{2,1,0:T(8,128)S(1)} %pad_maximum_fusion.refs_2_, f32[2,3,256,256]{3,2,1,0:T(8,128)S(1)} %copy-done, ...), custom_call_target="tpu_custom_call" | custom-call | flops 1207959552 | bytes 5111856 | tf_op jit(solution)/shard_map/pallas_call | solution.py:329
  33.0 2.5 %shard_map.65 = (f32[2,6,128,128]{3,2,1,0:T(8,128)S(1)}, f32[2,6,128,128]{3,2,1,0:T(8,128)S(1)}) custom-call(s32[6,2]{1,0:T(8,128)S(1)} %copy.13.refs_0_, bf16[4,256,256]{2,1,0:T(8,128)(2,1)S(1)} %copy-done.31, f32[4,128,128]{2,1,0:T(8,128)S(1)} %pad_maximum_fusion.refs_2_, f32[2,6,128,128]{3,2,1,0:T(8,128)S(1)} %get-tuple-element.59.refs_3_.refs_4_, ...), custom_call_target="tpu_custom_call" | custom-call | flops 1207959552 | bytes 6160432 | tf_op jit(solution)/shard_map/pallas_call | solution.py:329
  35.5 3.7 %shard_map.66 = (f32[2,384,128]{2,1,0:T(8,128)S(1)}, f32[2,256,128]{2,1,0:T(8,128)S(1)}, f32[2,128,128]{2,1,0:T(8,128)S(1)}, f32[2,384,128]{2,1,0:T(8,128)}, f32[2,6,128,128]{3,2,1,0:T(8,128)S(1)}) custom-call(s32[6,2]{1,0:T(8,128)S(1)} %copy.13.refs_0_, bf16[4,256,256]{2,1,0:T(8,128)(2,1)S(1)} %copy-done.31, f32[6,128,128]{2,1,0:T(8,128)S(1)} %bitcast.7, ...), custom_call_target="tpu_custom_call" | custom-call | flops 1207959552 | bytes 6684720 | tf_op jit(solution)/shard_map/pallas_call | solution.py:329
  39.9 3.5 %shard_map.67 = (f32[2,384,128]{2,1,0:T(8,128)S(1)}, f32[2,256,128]{2,1,0:T(8,128)S(1)}, f32[2,128,128]{2,1,0:T(8,128)S(1)}, f32[2,384,128]{2,1,0:T(8,128)}, f32[2,6,128,128]{3,2,1,0:T(8,128)S(1)}) custom-call(s32[6,2]{1,0:T(8,128)S(1)} %copy.13.refs_0_, bf16[4,256,256]{2,1,0:T(8,128)(2,1)S(1)} %copy-done.31, f32[4,128,128]{2,1,0:T(8,128)S(1)} %copy-done.24, ...), custom_call_target="tpu_custom_call" | custom-call | flops 1207959552 | bytes 5636144 | tf_op jit(solution)/shard_map/pallas_call | solution.py:329
  43.4 3.4 %shard_map.68 = (f32[2,384,128]{2,1,0:T(8,128)S(1)}, f32[2,256,128]{2,1,0:T(8,128)S(1)}, f32[2,128,128]{2,1,0:T(8,128)S(1)}, f32[2,384,128]{2,1,0:T(8,128)}) custom-call(s32[6,2]{1,0:T(8,128)S(1)} %copy.13.refs_0_, bf16[4,256,256]{2,1,0:T(8,128)(2,1)S(1)} %copy-done.31, f32[4,128,128]{2,1,0:T(8,128)S(1)} %copy-done.24, ...), custom_call_target="tpu_custom_call" | custom-call | flops 1207959552 | bytes 3276848 | tf_op jit(solution)/shard_map/pallas_call | solution.py:329
  51.0 3.4 %collective-permute-done.8.from_left.refs_5_ = f32[2,384,128]{2,1,0:T(8,128)S(1)} collective-permute-done((f32[2,384,128]{2,1,0:T(8,128)}, f32[2,384,128]{2,1,0:T(8,128)S(1)}, u32[]{:S(2)}, u32[]{:S(2)}) %collective-permute-start.8) | collective-permute-done | bytes 393248 | tf_op jit(solution)/shard_map/ppermute | solution.py:375
  57.3 5.5 %collective-permute-start.10 = (f32[2,128,256]{2,1,0:T(8,128)S(1)}, f32[2,128,256]{2,1,0:T(8,128)S(1)}, u32[]{:S(2)}, u32[]{:S(2)}) collective-permute-start(f32[2,128,256]{2,1,0:T(8,128)S(1)} %get-tuple-element.72), channel_id=1, source_target_pairs={{0,248},{8,16},{16,8},{24,32},{32,24},{40,48},{48,40},{56,64},{64,... | collective-permute-start | bytes 786440 | tf_op jit(solution)/shard_map/ppermute | solution.py:383
  65.6 2.7 %collective-permute-start.18 = (f32[2,128,256]{2,1,0:T(8,128)S(1)}, f32[2,128,256]{2,1,0:T(8,128)S(1)}, u32[]{:S(2)}, u32[]{:S(2)}) collective-permute-start(f32[2,128,256]{2,1,0:T(8,128)S(1)} %get-tuple-element.91), channel_id=1, source_target_pairs={{0,248},{8,16},{16,8},{24,32},{32,24},{40,48},{48,40},{56,64},{64,... | collective-permute-start | bytes 786440 | tf_op jit(solution)/shard_map/ppermute | solution.py:383
  69.7 2.2 %collective-permute-start.15 = (f32[2,128,384]{2,1,0:T(8,128)S(1)}, f32[2,128,384]{2,1,0:T(8,128)S(1)}, u32[]{:S(2)}, u32[]{:S(2)}) collective-permute-start(f32[2,128,384]{2,1,0:T(8,128)S(1)} %get-tuple-element.81), channel_id=1, source_target_pairs={{0,248},{8,16},{16,8},{24,32},{32,24},{40,48},{48,40},{56,64},{64,... | collective-permute-start | bytes 1179656 | tf_op jit(solution)/shard_map/ppermute | solution.py:383
  72.1 6.4 %collective-permute-start.11 = (f32[2,384,128]{2,1,0:T(8,128)S(1)}, f32[2,384,128]{2,1,0:T(8,128)S(1)}, u32[]{:S(2)}, u32[]{:S(2)}) collective-permute-start(f32[2,384,128]{2,1,0:T(8,128)S(1)} %get-tuple-element.73.refs_3_.refs_0_), channel_id=1, source_target_pairs={{1,0},{2,1},{3,2},{4,3},{5,4},{6,5},{7,6},{0,7},{9,8},{10,9},{11,1... | collective-permute-start | bytes 1179656 | tf_op jit(solution)/shard_map/ppermute | solution.py:375
  78.7 4.2 %collective-permute-start.19 = (f32[2,384,128]{2,1,0:T(8,128)S(1)}, f32[2,384,128]{2,1,0:T(8,128)S(1)}, u32[]{:S(2)}, u32[]{:S(2)}) collective-permute-start(f32[2,384,128]{2,1,0:T(8,128)S(1)} %get-tuple-element.92.refs_4_.refs_0_), channel_id=1, source_target_pairs={{1,0},{2,1},{3,2},{4,3},{5,4},{6,5},{7,6},{0,7},{9,8},{10,9},{11,1... | collective-permute-start | bytes 1179656 | tf_op jit(solution)/shard_map/ppermute | solution.py:375
  85.0 2.5 %shard_map.71 = (f32[2,6,128,128]{3,2,1,0:T(8,128)}, f32[2,6,128,128]{3,2,1,0:T(8,128)S(1)}) custom-call(s32[6,2]{1,0:T(8,128)S(1)} %copy.13.refs_0_, bf16[4,256,256]{2,1,0:T(8,128)(2,1)S(1)} %copy-done.32, f32[4,128,128]{2,1,0:T(8,128)S(1)} %copy-done.25, f32[2,384,128]{2,1,0:T(8,128)S(1)} %get-tuple-element.73.refs_3_.refs_0_, ...), custom_call_target="tpu_custom_call" | custom-call | flops 1207959552 | bytes 4063280 | tf_op jit(solution)/shard_map/pallas_call | solution.py:329
  87.5 2.5 %shard_map.74 = (f32[2,6,128,128]{3,2,1,0:T(8,128)S(1)}, f32[2,6,128,128]{3,2,1,0:T(8,128)S(1)}) custom-call(s32[6,2]{1,0:T(8,128)S(1)} %copy.13.refs_0_, bf16[4,256,256]{2,1,0:T(8,128)(2,1)S(1)} %copy-done.32, f32[4,128,128]{2,1,0:T(8,128)S(1)} %copy-done.25, f32[2,6,128,128]{3,2,1,0:T(8,128)S(1)} %get-tuple-element.75.refs_3_.refs_4_, ...), custom_call_target="tpu_custom_call" | custom-call | flops 1207959552 | bytes 4849712 | tf_op jit(solution)/shard_map/pallas_call | solution.py:329
  90.0 2.9 %shard_map.77 = (f32[2,384,128]{2,1,0:T(8,128)S(1)}, f32[2,256,128]{2,1,0:T(8,128)S(1)}, f32[2,128,128]{2,1,0:T(8,128)S(1)}, f32[2,384,128]{2,1,0:T(8,128)S(1)}, f32[2,6,128,128]{3,2,1,0:T(8,128)S(1)}) custom-call(s32[6,2]{1,0:T(8,128)S(1)} %copy.13.refs_0_, bf16[4,256,256]{2,1,0:T(8,128)(2,1)S(1)} %copy-done.32, f32[6,128,128]{2,1,0:T(8,128)S(1)} %bitcast.8, ...), custom_call_target="tpu_custom_call" | custom-call | flops 1207959552 | bytes 5374000 | tf_op jit(solution)/shard_map/pallas_call | solution.py:329
  92.9 3.8 %collective-permute-start.26 = (f32[2,384,128]{2,1,0:T(8,128)S(1)}, f32[2,384,128]{2,1,0:T(8,128)S(1)}, u32[]{:S(2)}, u32[]{:S(2)}) collective-permute-start(f32[2,384,128]{2,1,0:T(8,128)S(1)} %get-tuple-element.107), channel_id=1, source_target_pairs={{7,0},{0,1},{1,2},{2,3},{3,4},{4,5},{5,6},{6,7},{15,8},{8,9},{9,10... | collective-permute-start | bytes 1179656 | tf_op jit(solution)/shard_map/ppermute | solution.py:375
  96.7 2.7 %shard_map.78 = (f32[2,384,128]{2,1,0:T(8,128)S(1)}, f32[2,256,128]{2,1,0:T(8,128)S(1)}, f32[2,128,128]{2,1,0:T(8,128)S(1)}, f32[2,384,128]{2,1,0:T(8,128)S(1)}, f32[2,6,128,128]{3,2,1,0:T(8,128)S(1)}) custom-call(s32[6,2]{1,0:T(8,128)S(1)} %copy.13.refs_0_, bf16[4,256,256]{2,1,0:T(8,128)(2,1)S(1)} %copy-done.32, f32[4,128,128]{2,1,0:T(8,128)S(1)} %copy-done.25, ...), custom_call_target="tpu_custom_call" | custom-call | flops 1207959552 | bytes 5636144 | tf_op jit(solution)/shard_map/pallas_call | solution.py:329
  99.4 2.6 %shard_map.79 = (f32[2,384,128]{2,1,0:T(8,128)S(1)}, f32[2,256,128]{2,1,0:T(8,128)S(1)}, f32[2,128,128]{2,1,0:T(8,128)S(1)}, f32[2,384,128]{2,1,0:T(8,128)S(1)}) custom-call(s32[6,2]{1,0:T(8,128)S(1)} %copy.13.refs_0_, bf16[4,256,256]{2,1,0:T(8,128)(2,1)S(1)} %copy-done.32, f32[4,128,128]{2,1,0:T(8,128)S(1)} %copy-done.25, ...), custom_call_target="tpu_custom_call" | custom-call | flops 1207959552 | bytes 3276848 | tf_op jit(solution)/shard_map/pallas_call | solution.py:329
  105.7 4.2 %collective-permute-done.20.from_left.refs_4_ = f32[2,384,128]{2,1,0:T(8,128)S(1)} collective-permute-done((f32[2,384,128]{2,1,0:T(8,128)S(1)}, f32[2,384,128]{2,1,0:T(8,128)S(1)}, u32[]{:S(2)}, u32[]{:S(2)}) %collective-permute-start.20) | collective-permute-done | bytes 393248 | tf_op jit(solution)/shard_map/ppermute | solution.py:375
  109.9 2.4 %collective-permute-done.28.refs_6_ = f32[2,128,128]{2,1,0:T(8,128)S(1)} collective-permute-done((f32[2,128,128]{2,1,0:T(8,128)S(1)}, f32[2,128,128]{2,1,0:T(8,128)S(1)}, u32[]{:S(2)}, u32[]{:S(2)}) %collective-permute-start.28) | collective-permute-done | bytes 131104 | tf_op jit(solution)/shard_map/ppermute | solution.py:375
  112.3 8.4 %collective-permute-done.27.refs_5_ = f32[2,128,128]{2,1,0:T(8,128)S(1)} collective-permute-done((f32[2,128,128]{2,1,0:T(8,128)S(1)}, f32[2,128,128]{2,1,0:T(8,128)S(1)}, u32[]{:S(2)}, u32[]{:S(2)}) %collective-permute-start.27) | collective-permute-done | bytes 131104 | tf_op jit(solution)/shard_map/ppermute | solution.py:375
  (134 shorter events, 37.3 us)
Async XLA Ops:
  1.9 15.1 %collective-permute-start = (f32[2,128,256]{2,1,0:T(8,128)}, f32[2,128,256]{2,1,0:T(8,128)S(1)}, u32[]{:S(2)}, u32[]{:S(2)}) collective-permute-start(f32[2,128,256]{2,1,0:T(8,128)} %get-tuple-element.57), channel_id=1, source_target_pairs={{8,0},{16,8},{24,16},{32,24},{40,32},{48,40},{56,48},{64,56},{72,6... | collective-permute-start | bytes 786440 | tf_op jit(solution)/shard_map/ppermute | solution.py:375
  13.1 19.8 %collective-permute-start.4 = (f32[2,2,256,128]{3,2,1,0:T(8,128)}, f32[2,2,256,128]{3,2,1,0:T(8,128)S(1)}, u32[]{:S(2)}, u32[]{:S(2)}) collective-permute-start(f32[2,2,256,128]{3,2,1,0:T(8,128)} %get-tuple-element.61), channel_id=1, source_target_pairs={{1,0},{2,1},{3,2},{4,3},{5,4},{6,5},{7,6},{0,7},{9,8},{10,9},{11,1... | collective-permute-start | bytes 1572872 | tf_op jit(solution)/shard_map/ppermute | solution.py:375
  14.5 14.4 %collective-permute-start.1 = (f32[2,256,128]{2,1,0:T(8,128)}, f32[2,256,128]{2,1,0:T(8,128)S(1)}, u32[]{:S(2)}, u32[]{:S(2)}) collective-permute-start(f32[2,256,128]{2,1,0:T(8,128)} %get-tuple-element.58), channel_id=1, source_target_pairs={{1,0},{2,1},{3,2},{4,3},{5,4},{6,5},{7,6},{0,7},{9,8},{10,9},{11,1... | collective-permute-start | bytes 786440 | tf_op jit(solution)/shard_map/ppermute | solution.py:375
  16.7 10.6 %collective-permute-start.6 = (f32[2,128,256]{2,1,0:T(8,128)}, f32[2,128,256]{2,1,0:T(8,128)S(1)}, u32[]{:S(2)}, u32[]{:S(2)}) collective-permute-start(f32[2,128,256]{2,1,0:T(8,128)} %get-tuple-element.63), channel_id=1, source_target_pairs={{8,0},{16,8},{24,16},{32,24},{40,32},{48,40},{56,48},{64,56},{72,6... | collective-permute-start | bytes 786440 | tf_op jit(solution)/shard_map/ppermute | solution.py:375
  17.7 11.2 %collective-permute-start.2 = (f32[2,128,128]{2,1,0:T(8,128)}, f32[2,128,128]{2,1,0:T(8,128)}, u32[]{:S(2)}, u32[]{:S(2)}) collective-permute-start(f32[2,128,128]{2,1,0:T(8,128)} %slice.15), channel_id=1, source_target_pairs={{1,0},{2,1},{3,2},{4,3},{5,4},{6,5},{7,6},{0,7},{9,8},{10,9},{11,1... | collective-permute-start | bytes 393224 | tf_op jit(solution)/shard_map/ppermute | solution.py:375
  22.4 10.4 %collective-permute-start.5 = (f32[2,128,128]{2,1,0:T(8,128)}, f32[2,128,128]{2,1,0:T(8,128)S(1)}, u32[]{:S(2)}, u32[]{:S(2)}) collective-permute-start(f32[2,128,128]{2,1,0:T(8,128)} %slice.16), channel_id=1, source_target_pairs={{1,0},{2,1},{3,2},{4,3},{5,4},{6,5},{7,6},{0,7},{9,8},{10,9},{11,1... | collective-permute-start | bytes 393224 | tf_op jit(solution)/shard_map/ppermute | solution.py:375
  49.3 13.5 %collective-permute-start.16 = (f32[2,384,128]{2,1,0:T(8,128)}, f32[2,384,128]{2,1,0:T(8,128)S(1)}, u32[]{:S(2)}, u32[]{:S(2)}) collective-permute-start(f32[2,384,128]{2,1,0:T(8,128)} %get-tuple-element.89.right), channel_id=1, source_target_pairs={{7,0},{0,1},{1,2},{2,3},{3,4},{4,5},{5,6},{6,7},{15,8},{8,9},{9,10... | collective-permute-start | bytes 1179656 | tf_op jit(solution)/shard_map/ppermute | solution.py:375
  49.8 15.8 %collective-permute-start.12 = (f32[2,384,128]{2,1,0:T(8,128)}, f32[2,384,128]{2,1,0:T(8,128)}, u32[]{:S(2)}, u32[]{:S(2)}) collective-permute-start(f32[2,384,128]{2,1,0:T(8,128)} %get-tuple-element.79.right.refs_7_), channel_id=1, source_target_pairs={{7,0},{0,1},{1,2},{2,3},{3,4},{4,5},{5,6},{6,7},{15,8},{8,9},{9,10... | collective-permute-start | bytes 1179656 | tf_op jit(solution)/shard_map/ppermute | solution.py:375
  51.0 17.2 %collective-permute-start.13 = (f32[2,384,128]{2,1,0:T(8,128)S(1)}, f32[2,384,128]{2,1,0:T(8,128)}, u32[]{:S(2)}, u32[]{:S(2)}) collective-permute-start(f32[2,384,128]{2,1,0:T(8,128)S(1)} %get-tuple-element.76.left.refs_4_), channel_id=1, source_target_pairs={{1,0},{2,1},{3,2},{4,3},{5,4},{6,5},{7,6},{0,7},{9,8},{10,9},{11,1... | collective-permute-start | bytes 1179656 | tf_op jit(solution)/shard_map/ppermute | solution.py:375
  57.3 12.3 %collective-permute-start.10 = (f32[2,128,256]{2,1,0:T(8,128)S(1)}, f32[2,128,256]{2,1,0:T(8,128)S(1)}, u32[]{:S(2)}, u32[]{:S(2)}) collective-permute-start(f32[2,128,256]{2,1,0:T(8,128)S(1)} %get-tuple-element.72), channel_id=1, source_target_pairs={{0,248},{8,16},{16,8},{24,32},{32,24},{40,48},{48,40},{56,64},{64,... | collective-permute-start | bytes 786440 | tf_op jit(solution)/shard_map/ppermute | solution.py:383
  62.8 9.0 %collective-permute-start.9 = (f32[2,128,256]{2,1,0:T(8,128)S(1)}, f32[2,128,256]{2,1,0:T(8,128)S(1)}, u32[]{:S(2)}, u32[]{:S(2)}) collective-permute-start(f32[2,128,256]{2,1,0:T(8,128)S(1)} %get-tuple-element.71), channel_id=1, source_target_pairs={{0,8},{8,0},{16,24},{24,16},{32,40},{40,32},{48,56},{56,48},{64,72... | collective-permute-start | bytes 786440 | tf_op jit(solution)/shard_map/ppermute | solution.py:383
  64.0 14.5 %collective-permute-start.17 = (f32[2,128,256]{2,1,0:T(8,128)S(1)}, f32[2,128,256]{2,1,0:T(8,128)S(1)}, u32[]{:S(2)}, u32[]{:S(2)}) collective-permute-start(f32[2,128,256]{2,1,0:T(8,128)S(1)} %get-tuple-element.90), channel_id=1, source_target_pairs={{0,8},{8,0},{16,24},{24,16},{32,40},{40,32},{48,56},{56,48},{64,72... | collective-permute-start | bytes 786440 | tf_op jit(solution)/shard_map/ppermute | solution.py:383
  65.6 12.9 %collective-permute-start.18 = (f32[2,128,256]{2,1,0:T(8,128)S(1)}, f32[2,128,256]{2,1,0:T(8,128)S(1)}, u32[]{:S(2)}, u32[]{:S(2)}) collective-permute-start(f32[2,128,256]{2,1,0:T(8,128)S(1)} %get-tuple-element.91), channel_id=1, source_target_pairs={{0,248},{8,16},{16,8},{24,32},{32,24},{40,48},{48,40},{56,64},{64,... | collective-permute-start | bytes 786440 | tf_op jit(solution)/shard_map/ppermute | solution.py:383
  69.6 13.3 %collective-permute-start.14 = (f32[2,128,384]{2,1,0:T(8,128)S(1)}, f32[2,128,384]{2,1,0:T(8,128)S(1)}, u32[]{:S(2)}, u32[]{:S(2)}) collective-permute-start(f32[2,128,384]{2,1,0:T(8,128)S(1)} %get-tuple-element.80), channel_id=1, source_target_pairs={{0,8},{8,0},{16,24},{24,16},{32,40},{40,32},{48,56},{56,48},{64,72... | collective-permute-start | bytes 1179656 | tf_op jit(solution)/shard_map/ppermute | solution.py:383
  69.7 13.7 %collective-permute-start.15 = (f32[2,128,384]{2,1,0:T(8,128)S(1)}, f32[2,128,384]{2,1,0:T(8,128)S(1)}, u32[]{:S(2)}, u32[]{:S(2)}) collective-permute-start(f32[2,128,384]{2,1,0:T(8,128)S(1)} %get-tuple-element.81), channel_id=1, source_target_pairs={{0,248},{8,16},{16,8},{24,32},{32,24},{40,48},{48,40},{56,64},{64,... | collective-permute-start | bytes 1179656 | tf_op jit(solution)/shard_map/ppermute | solution.py:383
  72.1 12.8 %collective-permute-start.11 = (f32[2,384,128]{2,1,0:T(8,128)S(1)}, f32[2,384,128]{2,1,0:T(8,128)S(1)}, u32[]{:S(2)}, u32[]{:S(2)}) collective-permute-start(f32[2,384,128]{2,1,0:T(8,128)S(1)} %get-tuple-element.73.refs_3_.refs_0_), channel_id=1, source_target_pairs={{1,0},{2,1},{3,2},{4,3},{5,4},{6,5},{7,6},{0,7},{9,8},{10,9},{11,1... | collective-permute-start | bytes 1179656 | tf_op jit(solution)/shard_map/ppermute | solution.py:375
  78.7 11.2 %collective-permute-start.19 = (f32[2,384,128]{2,1,0:T(8,128)S(1)}, f32[2,384,128]{2,1,0:T(8,128)S(1)}, u32[]{:S(2)}, u32[]{:S(2)}) collective-permute-start(f32[2,384,128]{2,1,0:T(8,128)S(1)} %get-tuple-element.92.refs_4_.refs_0_), channel_id=1, source_target_pairs={{1,0},{2,1},{3,2},{4,3},{5,4},{6,5},{7,6},{0,7},{9,8},{10,9},{11,1... | collective-permute-start | bytes 1179656 | tf_op jit(solution)/shard_map/ppermute | solution.py:375
  92.9 10.6 %collective-permute-start.26 = (f32[2,384,128]{2,1,0:T(8,128)S(1)}, f32[2,384,128]{2,1,0:T(8,128)S(1)}, u32[]{:S(2)}, u32[]{:S(2)}) collective-permute-start(f32[2,384,128]{2,1,0:T(8,128)S(1)} %get-tuple-element.107), channel_id=1, source_target_pairs={{7,0},{0,1},{1,2},{2,3},{3,4},{4,5},{5,6},{6,7},{15,8},{8,9},{9,10... | collective-permute-start | bytes 1179656 | tf_op jit(solution)/shard_map/ppermute | solution.py:375
  103.5 8.8 %collective-permute-start.28 = (f32[2,128,128]{2,1,0:T(8,128)S(1)}, f32[2,128,128]{2,1,0:T(8,128)S(1)}, u32[]{:S(2)}, u32[]{:S(2)}) collective-permute-start(f32[2,128,128]{2,1,0:T(8,128)S(1)} %get-tuple-element.108), channel_id=1, source_target_pairs={{248,0},{0,8},{8,16},{16,24},{24,32},{32,40},{40,48},{48,56},{56,6... | collective-permute-start | bytes 393224 | tf_op jit(solution)/shard_map/ppermute | solution.py:375
  103.5 18.2 %collective-permute-start.25 = (f32[2,128,128]{2,1,0:T(8,128)S(1)}, f32[2,128,128]{2,1,0:T(8,128)S(1)}, u32[]{:S(2)}, u32[]{:S(2)}) collective-permute-start(f32[2,128,128]{2,1,0:T(8,128)S(1)} %get-tuple-element.104), channel_id=1, source_target_pairs={{248,0},{0,8},{8,16},{16,24},{24,32},{32,40},{40,48},{48,56},{56,6... | collective-permute-start | bytes 393224 | tf_op jit(solution)/shard_map/ppermute | solution.py:375
  103.5 21.0 %collective-permute-start.22 = (f32[2,128,128]{2,1,0:T(8,128)S(1)}, f32[2,128,128]{2,1,0:T(8,128)S(1)}, u32[]{:S(2)}, u32[]{:S(2)}) collective-permute-start(f32[2,128,128]{2,1,0:T(8,128)S(1)} %get-tuple-element.100), channel_id=1, source_target_pairs={{248,0},{0,8},{8,16},{16,24},{24,32},{32,40},{40,48},{48,56},{56,6... | collective-permute-start | bytes 393224 | tf_op jit(solution)/shard_map/ppermute | solution.py:375
  105.6 15.1 %collective-permute-start.27 = (f32[2,128,128]{2,1,0:T(8,128)S(1)}, f32[2,128,128]{2,1,0:T(8,128)S(1)}, u32[]{:S(2)}, u32[]{:S(2)}) collective-permute-start(f32[2,128,128]{2,1,0:T(8,128)S(1)} %shard_map.82), channel_id=1, source_target_pairs={{248,0},{0,8},{8,16},{16,24},{24,32},{32,40},{40,48},{48,56},{56,6... | collective-permute-start | bytes 393224 | tf_op jit(solution)/shard_map/ppermute | solution.py:375
  109.8 13.7 %collective-permute-start.24 = (f32[2,128,128]{2,1,0:T(8,128)S(1)}, f32[2,128,128]{2,1,0:T(8,128)S(1)}, u32[]{:S(2)}, u32[]{:S(2)}) collective-permute-start(f32[2,128,128]{2,1,0:T(8,128)S(1)} %shard_map.81), channel_id=1, source_target_pairs={{248,0},{0,8},{8,16},{16,24},{24,32},{32,40},{40,48},{48,56},{56,6... | collective-permute-start | bytes 393224 | tf_op jit(solution)/shard_map/ppermute | solution.py:375
  112.3 13.9 %collective-permute-start.21 = (f32[2,128,128]{2,1,0:T(8,128)S(1)}, f32[2,128,128]{2,1,0:T(8,128)S(1)}, u32[]{:S(2)}, u32[]{:S(2)}) collective-permute-start(f32[2,128,128]{2,1,0:T(8,128)S(1)} %shard_map.80), channel_id=1, source_target_pairs={{248,0},{0,8},{8,16},{16,24},{24,32},{32,40},{40,48},{48,56},{56,6... | collective-permute-start | bytes 393224 | tf_op jit(solution)/shard_map/ppermute | solution.py:375
  (40 other events, 306.2 us)

commit v2 on v1

--- a/solution.py
+++ b/solution.py
@@ -113,7 +113,7 @@
 
 
 def place(offset_ref, p):
-    row, col = offset_ref[p, 0], offset_ref[p, 1]
+    row, col = offset_ref[0, p], offset_ref[1, p]
     over = lax.rem(row, SUB)
     base = jnp.where(col >= PROBE, PROBE, 0)
     return pl.multiple_of(row - over, SUB), over, pl.multiple_of(base, PROBE), col - base
@@ -334,7 +334,7 @@
         out_shape=outs,
         scratch_shapes=scratch,
         cost_estimate=pl.CostEstimate(flops=flops, bytes_accessed=moved, transcendentals=0),
-        compiler_params=pltpu.CompilerParams(vmem_limit_bytes=40 * 2**20),
+        compiler_params=pltpu.CompilerParams(vmem_limit_bytes=14 * 2**20),
     )(*operands)
 
 
@@ -394,11 +394,10 @@
         out_shape=outs,
         input_output_aliases=aliases or {},
         cost_estimate=pl.CostEstimate(flops=0, bytes_accessed=2 * moved, transcendentals=0),
-        compiler_params=pltpu.CompilerParams(vmem_limit_bytes=24 * 2**20),
+        compiler_params=pltpu.CompilerParams(vmem_limit_bytes=8 * 2**20),
     )(*operands)
 
 
-IN_SMEM = pl.BlockSpec(memory_space=pltpu.SMEM)
 SIDE = shape(2, EXT, PROBE)
 
 
@@ -423,10 +422,24 @@
         scratch_shapes=[pltpu.SemaphoreType.DMA((len(outs),))],
         name="pack",
         cost_estimate=pl.CostEstimate(flops=0, bytes_accessed=4 * 2**18, transcendentals=0),
+        compiler_params=pltpu.CompilerParams(vmem_limit_bytes=4 * 2**20),
     )(object_field)
 
 
-def sums_kernel(wide, parity, left, middle, low, right, from_left, *refs):
+def prepare_kernel(probe, propagator, tables, phase, copied):
+    phase[:2] = probe[...]
+    phase[2] = jnp.cos(propagator[...])
+    phase[3] = jnp.sin(propagator[...])
+    copied[...] = tables[...]
+
+
+def prepare(probe, propagator):
+    tables = jnp.asarray(dft_tables())
+    outs = [shape(4, PROBE, PROBE), jax.ShapeDtypeStruct(tables.shape, BF16)]
+    return plain(prepare_kernel, outs, [probe, propagator, tables])
+
+
+def sums_kernel(wide, left, middle, low, right, from_left, *refs):
     h, t = PROBE, TILE
     from_right = refs[0] if wide else None
     even_out, odd_out = refs[-2:]
@@ -440,23 +453,25 @@
             down[:, :, t:] = right[:, t:] + from_right[:, t:]
             up[:, :, t:] = right[:, :h] + from_right[:, :h]
 
-    @pl.when(parity[0] == 0)
+    parity = lax.axis_index("row") & 1
+
+    @pl.when(parity == 0)
     def _():
         fill(even_out, odd_out)
 
-    @pl.when(parity[0] == 1)
+    @pl.when(parity == 1)
     def _():
         fill(odd_out, even_out)
 
 
-def sums(parity, grad, from_left, from_right):
+def sums(grad, from_left, from_right):
     wide = from_right is not None
-    operands = [parity, *grad, from_left] + ([from_right] if wide else [])
+    operands = [*grad, from_left] + ([from_right] if wide else [])
     outs = [shape(2, PROBE, EXT if wide else TILE)] * 2
-    return plain(functools.partial(sums_kernel, wide), outs, operands, {0: IN_SMEM})
-
-
-def update_kernel(wide, parity, *refs):
+    return plain(functools.partial(sums_kernel, wide), outs, operands)
+
+
+def update_kernel(wide, *refs):
     h, t = PROBE, TILE
     if wide:
         tile, low, side, corner, left, middle, bottom, right, from_left, from_right, even, odd = refs[:12]
@@ -466,7 +481,7 @@
     top, mid, end = slice(0, h), slice(h, t), slice(t, t + h)
     first, second, third = slice(0, h), slice(h, t), slice(t, t + h)
 
-    swap = parity[0] == 1
+    swap = (lax.axis_index("row") & 1) == 1
 
     class Chosen:
         def __init__(self, first, second):
@@ -490,14 +505,14 @@
     fill(Chosen(odd, even), Chosen(even, odd))
 
 
-def update(parity, layer, field, grad, from_left, from_right, even, odd):
+def update(layer, field, grad, from_left, from_right, even, odd):
     tile, low, side, corner = field
     if from_right is None:
-        operands = [parity, tile, low, *grad[:3], from_left, even, odd]
-        specs = {0: IN_SMEM, 1: tile_of(layer)}
+        operands = [tile, low, *grad[:3], from_left, even, odd]
+        specs = {0: tile_of(layer)}
         return plain(functools.partial(update_kernel, False), [SIDE] * 2, operands, specs)
-    operands = [parity, tile, low, side, corner, *grad, from_left, from_right, even, odd]
-    specs = {0: IN_SMEM, **field_specs(1, layer, fill_first)}
+    operands = [tile, low, side, corner, *grad, from_left, from_right, even, odd]
+    specs = field_specs(0, layer, fill_first)
     return plain(functools.partial(update_kernel, True), [SIDE] * 3, operands, specs)
 
 
@@ -533,11 +548,9 @@
 
 def on_device(object_field, probe, propagator, measured, offsets):
     h, t = PROBE, TILE
-    tables = jnp.asarray(dft_tables())
-    offsets = offsets.reshape(POS, 2)
+    phase, tables = prepare(probe, propagator)
+    offsets = jnp.swapaxes(offsets, 2, 3).reshape(2, POS)
     intensity = measured.reshape(POS, h, h)
-    phase = jnp.stack([probe[0], probe[1], jnp.cos(propagator), jnp.sin(propagator)])
-    parity = (lax.axis_index("row") & 1).astype(jnp.int32).reshape(1)
 
     top, all_rows, left, all_cols = pl.ds(0, h), pl.ds(0, t), pl.ds(0, h), pl.ds(0, t)
     rows_shape = shape(2, h, t)
@@ -572,10 +585,10 @@
         from_left = shifted(grad[3], "col", 1)
         if layer == 1:
             from_right = shifted(grad[0], "col", -1)
-        for_even, for_odd = sums(parity, grad, from_left, from_right)
+        for_even, for_odd = sums(grad, from_left, from_right)
         even = swapped(for_even, 0)
         odd = swapped(for_odd, 1)
-        new = update(parity, layer, fields[layer], grad, from_left, from_right, even, odd)
+        new = update(layer, fields[layer], grad, from_left, from_right, even, odd)
         if layer != 1:
             new = [*new, shifted(new[0], "col", -1)]
         renewed[layer] = list(new)

time: 127 us -> 117 us (0.921)
  the two profiles are of different devices: /device:TPU:1 before, /device:TPU:7 now
where the time goes in v2:
time: 117 us; the launch traced here: 115 us
  waiting for transfers between devices  44 us (38%)
  starting transfers between devices  39.2 us (34%)
  Pallas kernels  30.1 us (26%)
  local copies, waits for them, and re-layouts  1.47 us (1%)
    ppermute x23, waiting for transfers between devices, shifted(): lax.ppermute(block, axis, [((i - distance) % size, i) for i in range(size)])  35.9 us
    pallas_call x10, Pallas kernels, run(): pl.pallas_call(body, grid=(1,), in_specs=in_specs, out_specs=[whole(o) fo...  26 us
    ppermute x23, starting transfers between devices, shifted(): lax.ppermute(block, axis, [((i - distance) % size, i) for i in range(size)])  24.5 us
    ppermute x6, starting transfers between devices, swapped(): return lax.ppermute(block, 'row', sorted(route))  14.8 us
    ppermute x6, waiting for transfers between devices, swapped(): return lax.ppermute(block, 'row', sorted(route))  8.08 us
    pallas_call x13, Pallas kernels, plain(): pl.pallas_call(body, grid=(1,), in_specs=[specs.get(n, None) or whole(o)...  3.93 us
  transfers between devices with their start and end apart: 29, of which 14 were waited for; matrix products, arithmetic and copies ran while one was open for 0% of the time, Pallas kernels for 16%

profile of v2, /device:TPU:7, one launch (start us, length us, event | category | flops | bytes accessed | tf_op | source)
XLA Modules:
  0.0 115.1 jit_solution(11190538814228548317)
XLA Ops:
  2.3 8.1 %collective-permute-start = (f32[2,128,256]{2,1,0:T(8,128)S(1)}, f32[2,128,256]{2,1,0:T(8,128)S(1)}, u32[]{:S(2)}, u32[]{:S(2)}) collective-permute-start(f32[2,128,256]{2,1,0:T(8,128)S(1)} %get-tuple-element.59), channel_id=1, source_target_pairs={{8,0},{16,8},{24,16},{32,24},{40,32},{48,40},{56,48},{64,56},{72,6... | collective-permute-start | bytes 786440 | tf_op jit(solution)/shard_map/ppermute | solution.py:375
  12.1 3.7 %collective-permute-done.refs_4_.refs_1_ = f32[2,128,256]{2,1,0:T(8,128)S(1)} collective-permute-done((f32[2,128,256]{2,1,0:T(8,128)S(1)}, f32[2,128,256]{2,1,0:T(8,128)S(1)}, u32[]{:S(2)}, u32[]{:S(2)}) %collective-permute-start) | collective-permute-done | bytes 262176 | tf_op jit(solution)/shard_map/ppermute | solution.py:375
  17.7 3.7 %collective-permute-done.3.refs_5_.refs_1_ = f32[2,128,256]{2,1,0:T(8,128)S(1)} collective-permute-done((f32[2,128,256]{2,1,0:T(8,128)S(1)}, f32[2,128,256]{2,1,0:T(8,128)S(1)}, u32[]{:S(2)}, u32[]{:S(2)}) %collective-permute-start.3) | collective-permute-done | bytes 262176 | tf_op jit(solution)/shard_map/ppermute | solution.py:375
  23.7 3.3 %collective-permute-done.6.refs_5_.refs_1_ = f32[2,128,256]{2,1,0:T(8,128)S(1)} collective-permute-done((f32[2,128,256]{2,1,0:T(8,128)S(1)}, f32[2,128,256]{2,1,0:T(8,128)S(1)}, u32[]{:S(2)}, u32[]{:S(2)}) %collective-permute-start.6) | collective-permute-done | bytes 262176 | tf_op jit(solution)/shard_map/ppermute | solution.py:375
  28.2 2.4 %shard_map.65 = (f32[2,6,128,128]{3,2,1,0:T(8,128)}, f32[2,6,128,128]{3,2,1,0:T(8,128)S(1)}) custom-call(s32[2,6]{1,0:T(2,128)S(1)} %bitcast.6, bf16[4,256,256]{2,1,0:T(8,128)(2,1)S(1)} %get-tuple-element.60.refs_1_, f32[4,128,128]{2,1,0:T(8,128)S(1)} %get-tuple-element.61.refs_2_, f32[2,3,256,256]{3,2,1,0:T(8,128)S(1)} %copy-done.1, ...), custom_call_target="tpu_custom_call" | custom-call | flops 1207959552 | bytes 5111856 | tf_op jit(solution)/shard_map/pallas_call | solution.py:329
  30.7 2.4 %shard_map.66 = (f32[2,6,128,128]{3,2,1,0:T(8,128)S(1)}, f32[2,6,128,128]{3,2,1,0:T(8,128)S(1)}) custom-call(s32[2,6]{1,0:T(2,128)S(1)} %bitcast.7, bf16[4,256,256]{2,1,0:T(8,128)(2,1)S(1)} %get-tuple-element.60.refs_1_, f32[4,128,128]{2,1,0:T(8,128)S(1)} %get-tuple-element.61.refs_2_, f32[2,6,128,128]{3,2,1,0:T(8,128)S(1)} %get-tuple-element.63.refs_3_.refs_4_, ...), custom_call_target="tpu_custom_call" | custom-call | flops 1207959552 | bytes 6160432 | tf_op jit(solution)/shard_map/pallas_call | solution.py:329
  33.1 2.9 %shard_map.67 = (f32[2,384,128]{2,1,0:T(8,128)S(1)}, f32[2,256,128]{2,1,0:T(8,128)S(1)}, f32[2,128,128]{2,1,0:T(8,128)S(1)}, f32[2,384,128]{2,1,0:T(8,128)S(1)}, f32[2,6,128,128]{3,2,1,0:T(8,128)S(1)}) custom-call(s32[2,6]{1,0:T(2,128)S(1)} %bitcast.8, bf16[4,256,256]{2,1,0:T(8,128)(2,1)S(1)} %get-tuple-element.60.refs_1_, f32[6,128,128]{2,1,0:T(8,128)S(1)} %bitcast.4, ...), custom_call_target="tpu_custom_call" | custom-call | flops 1207959552 | bytes 6684720 | tf_op jit(solution)/shard_map/pallas_call | solution.py:329
  36.0 2.7 %shard_map.68 = (f32[2,384,128]{2,1,0:T(8,128)S(1)}, f32[2,256,128]{2,1,0:T(8,128)S(1)}, f32[2,128,128]{2,1,0:T(8,128)S(1)}, f32[2,384,128]{2,1,0:T(8,128)S(1)}, f32[2,6,128,128]{3,2,1,0:T(8,128)S(1)}) custom-call(s32[2,6]{1,0:T(2,128)S(1)} %bitcast.9, bf16[4,256,256]{2,1,0:T(8,128)(2,1)S(1)} %get-tuple-element.60.refs_1_, ...), custom_call_target="tpu_custom_call" | custom-call | flops 1207959552 | bytes 5636144 | tf_op jit(solution)/shard_map/pallas_call | solution.py:329
  38.7 2.6 %shard_map.69 = (f32[2,384,128]{2,1,0:T(8,128)S(1)}, f32[2,256,128]{2,1,0:T(8,128)S(1)}, f32[2,128,128]{2,1,0:T(8,128)S(1)}, f32[2,384,128]{2,1,0:T(8,128)S(1)}) custom-call(s32[2,6]{1,0:T(2,128)S(1)} %bitcast.10, bf16[4,256,256]{2,1,0:T(8,128)(2,1)S(1)} %get-tuple-element.60.refs_1_, f32[4,128,128]{2,1,0:T(8,128)S(1)} %get-tuple-element.61.refs_2_, ...), custom_call_target="tpu_custom_call" | custom-call | flops 1207959552 | bytes 3276848 | tf_op jit(solution)/shard_map/pallas_call | solution.py:329
  43.7 4.2 %collective-permute-done.8.from_left.refs_5_ = f32[2,384,128]{2,1,0:T(8,128)S(1)} collective-permute-done((f32[2,384,128]{2,1,0:T(8,128)S(1)}, f32[2,384,128]{2,1,0:T(8,128)S(1)}, u32[]{:S(2)}, u32[]{:S(2)}) %collective-permute-start.8) | collective-permute-done | bytes 393248 | tf_op jit(solution)/shard_map/ppermute | solution.py:375
  47.9 5.6 %collective-permute-start.10 = (f32[2,128,256]{2,1,0:T(8,128)S(1)}, f32[2,128,256]{2,1,0:T(8,128)S(1)}, u32[]{:S(2)}, u32[]{:S(2)}) collective-permute-start(f32[2,128,256]{2,1,0:T(8,128)S(1)} %get-tuple-element.76), channel_id=1, source_target_pairs={{0,248},{8,16},{16,8},{24,32},{32,24},{40,48},{48,40},{56,64},{64,... | collective-permute-start | bytes 786440 | tf_op jit(solution)/shard_map/ppermute | solution.py:383
  56.3 5.5 %collective-permute-start.18 = (f32[2,128,256]{2,1,0:T(8,128)S(1)}, f32[2,128,256]{2,1,0:T(8,128)S(1)}, u32[]{:S(2)}, u32[]{:S(2)}) collective-permute-start(f32[2,128,256]{2,1,0:T(8,128)S(1)} %get-tuple-element.95), channel_id=1, source_target_pairs={{0,248},{8,16},{16,8},{24,32},{32,24},{40,48},{48,40},{56,64},{64,... | collective-permute-start | bytes 786440 | tf_op jit(solution)/shard_map/ppermute | solution.py:383
  62.0 2.0 %collective-permute-start.15 = (f32[2,128,384]{2,1,0:T(8,128)S(1)}, f32[2,128,384]{2,1,0:T(8,128)S(1)}, u32[]{:S(2)}, u32[]{:S(2)}) collective-permute-start(f32[2,128,384]{2,1,0:T(8,128)S(1)} %get-tuple-element.85), channel_id=1, source_target_pairs={{0,248},{8,16},{16,8},{24,32},{32,24},{40,48},{48,40},{56,64},{64,... | collective-permute-start | bytes 1179656 | tf_op jit(solution)/shard_map/ppermute | solution.py:383
  69.8 4.6 %collective-permute-done.14.refs_10_ = f32[2,128,384]{2,1,0:T(8,128)S(1)} collective-permute-done((f32[2,128,384]{2,1,0:T(8,128)S(1)}, f32[2,128,384]{2,1,0:T(8,128)S(1)}, u32[]{:S(2)}, u32[]{:S(2)}) %collective-permute-start.14) | collective-permute-done | bytes 393248 | tf_op jit(solution)/shard_map/ppermute | solution.py:383
  76.5 2.4 %shard_map.72 = (f32[2,6,128,128]{3,2,1,0:T(8,128)}, f32[2,6,128,128]{3,2,1,0:T(8,128)S(1)}) custom-call(s32[2,6]{1,0:T(2,128)S(1)} %bitcast.11, bf16[4,256,256]{2,1,0:T(8,128)(2,1)S(1)} %get-tuple-element.60.refs_1_, f32[4,128,128]{2,1,0:T(8,128)S(1)} %get-tuple-element.61.refs_2_, f32[2,384,128]{2,1,0:T(8,128)S(1)} %get-tuple-element.77.refs_3_.refs_0_, ...), custom_call_target="tpu_custom_call" | custom-call | flops 1207959552 | bytes 4063280 | tf_op jit(solution)/shard_map/pallas_call | solution.py:329
  78.9 2.4 %shard_map.75 = (f32[2,6,128,128]{3,2,1,0:T(8,128)S(1)}, f32[2,6,128,128]{3,2,1,0:T(8,128)S(1)}) custom-call(s32[2,6]{1,0:T(2,128)S(1)} %bitcast.12, bf16[4,256,256]{2,1,0:T(8,128)(2,1)S(1)} %get-tuple-element.60.refs_1_, f32[4,128,128]{2,1,0:T(8,128)S(1)} %get-tuple-element.61.refs_2_, f32[2,6,128,128]{3,2,1,0:T(8,128)S(1)} %get-tuple-element.79.refs_3_.refs_4_, ...), custom_call_target="tpu_custom_call" | custom-call | flops 1207959552 | bytes 4849712 | tf_op jit(solution)/shard_map/pallas_call | solution.py:329
  81.4 2.9 %shard_map.78 = (f32[2,384,128]{2,1,0:T(8,128)S(1)}, f32[2,256,128]{2,1,0:T(8,128)S(1)}, f32[2,128,128]{2,1,0:T(8,128)S(1)}, f32[2,384,128]{2,1,0:T(8,128)S(1)}, f32[2,6,128,128]{3,2,1,0:T(8,128)S(1)}) custom-call(s32[2,6]{1,0:T(2,128)S(1)} %bitcast.13, bf16[4,256,256]{2,1,0:T(8,128)(2,1)S(1)} %get-tuple-element.60.refs_1_, f32[6,128,128]{2,1,0:T(8,128)S(1)} %bitcast.5, ...), custom_call_target="tpu_custom_call" | custom-call | flops 1207959552 | bytes 5374000 | tf_op jit(solution)/shard_map/pallas_call | solution.py:329
  84.3 2.4 %collective-permute-start.26 = (f32[2,384,128]{2,1,0:T(8,128)S(1)}, f32[2,384,128]{2,1,0:T(8,128)S(1)}, u32[]{:S(2)}, u32[]{:S(2)}) collective-permute-start(f32[2,384,128]{2,1,0:T(8,128)S(1)} %get-tuple-element.111), channel_id=1, source_target_pairs={{7,0},{0,1},{1,2},{2,3},{3,4},{4,5},{5,6},{6,7},{15,8},{8,9},{9,10... | collective-permute-start | bytes 1179656 | tf_op jit(solution)/shard_map/ppermute | solution.py:375
  86.7 2.7 %shard_map.79 = (f32[2,384,128]{2,1,0:T(8,128)S(1)}, f32[2,256,128]{2,1,0:T(8,128)S(1)}, f32[2,128,128]{2,1,0:T(8,128)S(1)}, f32[2,384,128]{2,1,0:T(8,128)S(1)}, f32[2,6,128,128]{3,2,1,0:T(8,128)S(1)}) custom-call(s32[2,6]{1,0:T(2,128)S(1)} %bitcast.14, bf16[4,256,256]{2,1,0:T(8,128)(2,1)S(1)} %get-tuple-element.60.refs_1_, ...), custom_call_target="tpu_custom_call" | custom-call | flops 1207959552 | bytes 5636144 | tf_op jit(solution)/shard_map/pallas_call | solution.py:329
  89.4 2.6 %shard_map.80 = (f32[2,384,128]{2,1,0:T(8,128)S(1)}, f32[2,256,128]{2,1,0:T(8,128)S(1)}, f32[2,128,128]{2,1,0:T(8,128)S(1)}, f32[2,384,128]{2,1,0:T(8,128)S(1)}) custom-call(s32[2,6]{1,0:T(2,128)S(1)} %bitcast.15, bf16[4,256,256]{2,1,0:T(8,128)(2,1)S(1)} %get-tuple-element.60.refs_1_, f32[4,128,128]{2,1,0:T(8,128)S(1)} %get-tuple-element.61.refs_2_, ...), custom_call_target="tpu_custom_call" | custom-call | flops 1207959552 | bytes 3276848 | tf_op jit(solution)/shard_map/pallas_call | solution.py:329
  92.5 3.1 %collective-permute-done.23.from_left.refs_4_ = f32[2,384,128]{2,1,0:T(8,128)S(1)} collective-permute-done((f32[2,384,128]{2,1,0:T(8,128)S(1)}, f32[2,384,128]{2,1,0:T(8,128)S(1)}, u32[]{:S(2)}, u32[]{:S(2)}) %collective-permute-start.23) | collective-permute-done | bytes 393248 | tf_op jit(solution)/shard_map/ppermute | solution.py:375
  95.6 4.2 %collective-permute-done.20.from_left.refs_4_ = f32[2,384,128]{2,1,0:T(8,128)S(1)} collective-permute-done((f32[2,384,128]{2,1,0:T(8,128)S(1)}, f32[2,384,128]{2,1,0:T(8,128)S(1)}, u32[]{:S(2)}, u32[]{:S(2)}) %collective-permute-start.20) | collective-permute-done | bytes 393248 | tf_op jit(solution)/shard_map/ppermute | solution.py:375
  100.2 8.4 %collective-permute-done.27.refs_5_ = f32[2,128,128]{2,1,0:T(8,128)S(1)} collective-permute-done((f32[2,128,128]{2,1,0:T(8,128)S(1)}, f32[2,128,128]{2,1,0:T(8,128)S(1)}, u32[]{:S(2)}, u32[]{:S(2)}) %collective-permute-start.27) | collective-permute-done | bytes 131104 | tf_op jit(solution)/shard_map/ppermute | solution.py:375
  109.5 1.9 %collective-permute-done.24.refs_5_ = f32[2,128,128]{2,1,0:T(8,128)S(1)} collective-permute-done((f32[2,128,128]{2,1,0:T(8,128)S(1)}, f32[2,128,128]{2,1,0:T(8,128)S(1)}, u32[]{:S(2)}, u32[]{:S(2)}) %collective-permute-start.24) | collective-permute-done | bytes 131104 | tf_op jit(solution)/shard_map/ppermute | solution.py:375
  (76 shorter events, 28.1 us)
Async XLA Ops:
  1.5 29.1 %collective-permute-start.4 = (f32[2,2,256,128]{3,2,1,0:T(8,128)S(1)}, f32[2,2,256,128]{3,2,1,0:T(8,128)S(1)}, u32[]{:S(2)}, u32[]{:S(2)}) collective-permute-start(f32[2,2,256,128]{3,2,1,0:T(8,128)S(1)} %get-tuple-element.65), channel_id=1, source_target_pairs={{1,0},{2,1},{3,2},{4,3},{5,4},{6,5},{7,6},{0,7},{9,8},{10,9},{11,1... | collective-permute-start | bytes 1572872 | tf_op jit(solution)/shard_map/ppermute | solution.py:375
  2.3 13.5 %collective-permute-start = (f32[2,128,256]{2,1,0:T(8,128)S(1)}, f32[2,128,256]{2,1,0:T(8,128)S(1)}, u32[]{:S(2)}, u32[]{:S(2)}) collective-permute-start(f32[2,128,256]{2,1,0:T(8,128)S(1)} %get-tuple-element.59), channel_id=1, source_target_pairs={{8,0},{16,8},{24,16},{32,24},{40,32},{48,40},{56,48},{64,56},{72,6... | collective-permute-start | bytes 786440 | tf_op jit(solution)/shard_map/ppermute | solution.py:375
  10.4 11.0 %collective-permute-start.3 = (f32[2,128,256]{2,1,0:T(8,128)S(1)}, f32[2,128,256]{2,1,0:T(8,128)S(1)}, u32[]{:S(2)}, u32[]{:S(2)}) collective-permute-start(f32[2,128,256]{2,1,0:T(8,128)S(1)} %get-tuple-element.64), channel_id=1, source_target_pairs={{8,0},{16,8},{24,16},{32,24},{40,32},{48,40},{56,48},{64,56},{72,6... | collective-permute-start | bytes 786440 | tf_op jit(solution)/shard_map/ppermute | solution.py:375
  10.9 16.2 %collective-permute-start.6 = (f32[2,128,256]{2,1,0:T(8,128)S(1)}, f32[2,128,256]{2,1,0:T(8,128)S(1)}, u32[]{:S(2)}, u32[]{:S(2)}) collective-permute-start(f32[2,128,256]{2,1,0:T(8,128)S(1)} %get-tuple-element.67), channel_id=1, source_target_pairs={{8,0},{16,8},{24,16},{32,24},{40,32},{48,40},{56,48},{64,56},{72,6... | collective-permute-start | bytes 786440 | tf_op jit(solution)/shard_map/ppermute | solution.py:375
  11.0 17.1 %collective-permute-start.1 = (f32[2,256,128]{2,1,0:T(8,128)S(1)}, f32[2,256,128]{2,1,0:T(8,128)S(1)}, u32[]{:S(2)}, u32[]{:S(2)}) collective-permute-start(f32[2,256,128]{2,1,0:T(8,128)S(1)} %get-tuple-element.62), channel_id=1, source_target_pairs={{1,0},{2,1},{3,2},{4,3},{5,4},{6,5},{7,6},{0,7},{9,8},{10,9},{11,1... | collective-permute-start | bytes 786440 | tf_op jit(solution)/shard_map/ppermute | solution.py:375
  15.8 12.4 %collective-permute-start.2 = (f32[2,128,128]{2,1,0:T(8,128)S(1)}, f32[2,128,128]{2,1,0:T(8,128)S(1)}, u32[]{:S(2)}, u32[]{:S(2)}) collective-permute-start(f32[2,128,128]{2,1,0:T(8,128)S(1)} %slice.12), channel_id=1, source_target_pairs={{1,0},{2,1},{3,2},{4,3},{5,4},{6,5},{7,6},{0,7},{9,8},{10,9},{11,1... | collective-permute-start | bytes 393224 | tf_op jit(solution)/shard_map/ppermute | solution.py:375
  21.4 9.2 %collective-permute-start.5 = (f32[2,128,128]{2,1,0:T(8,128)S(1)}, f32[2,128,128]{2,1,0:T(8,128)S(1)}, u32[]{:S(2)}, u32[]{:S(2)}) collective-permute-start(f32[2,128,128]{2,1,0:T(8,128)S(1)} %slice.13), channel_id=1, source_target_pairs={{1,0},{2,1},{3,2},{4,3},{5,4},{6,5},{7,6},{0,7},{9,8},{10,9},{11,1... | collective-permute-start | bytes 393224 | tf_op jit(solution)/shard_map/ppermute | solution.py:375
  43.1 10.4 %collective-permute-start.16 = (f32[2,384,128]{2,1,0:T(8,128)S(1)}, f32[2,384,128]{2,1,0:T(8,128)S(1)}, u32[]{:S(2)}, u32[]{:S(2)}) collective-permute-start(f32[2,384,128]{2,1,0:T(8,128)S(1)} %get-tuple-element.93.right), channel_id=1, source_target_pairs={{7,0},{0,1},{1,2},{2,3},{3,4},{4,5},{5,6},{6,7},{15,8},{8,9},{9,10... | collective-permute-start | bytes 1179656 | tf_op jit(solution)/shard_map/ppermute | solution.py:375
  43.1 13.1 %collective-permute-start.12 = (f32[2,384,128]{2,1,0:T(8,128)S(1)}, f32[2,384,128]{2,1,0:T(8,128)S(1)}, u32[]{:S(2)}, u32[]{:S(2)}) collective-permute-start(f32[2,384,128]{2,1,0:T(8,128)S(1)} %get-tuple-element.83.right.refs_7_), channel_id=1, source_target_pairs={{7,0},{0,1},{1,2},{2,3},{3,4},{4,5},{5,6},{6,7},{15,8},{8,9},{9,10... | collective-permute-start | bytes 1179656 | tf_op jit(solution)/shard_map/ppermute | solution.py:375
  43.2 18.6 %collective-permute-start.13 = (f32[2,384,128]{2,1,0:T(8,128)S(1)}, f32[2,384,128]{2,1,0:T(8,128)S(1)}, u32[]{:S(2)}, u32[]{:S(2)}) collective-permute-start(f32[2,384,128]{2,1,0:T(8,128)S(1)} %get-tuple-element.80.left.refs_4_), channel_id=1, source_target_pairs={{1,0},{2,1},{3,2},{4,3},{5,4},{6,5},{7,6},{0,7},{9,8},{10,9},{11,1... | collective-permute-start | bytes 1179656 | tf_op jit(solution)/shard_map/ppermute | solution.py:375
  47.9 14.1 %collective-permute-start.10 = (f32[2,128,256]{2,1,0:T(8,128)S(1)}, f32[2,128,256]{2,1,0:T(8,128)S(1)}, u32[]{:S(2)}, u32[]{:S(2)}) collective-permute-start(f32[2,128,256]{2,1,0:T(8,128)S(1)} %get-tuple-element.76), channel_id=1, source_target_pairs={{0,248},{8,16},{16,8},{24,32},{32,24},{40,48},{48,40},{56,64},{64,... | collective-permute-start | bytes 786440 | tf_op jit(solution)/shard_map/ppermute | solution.py:383
  53.5 10.5 %collective-permute-start.9 = (f32[2,128,256]{2,1,0:T(8,128)S(1)}, f32[2,128,256]{2,1,0:T(8,128)S(1)}, u32[]{:S(2)}, u32[]{:S(2)}) collective-permute-start(f32[2,128,256]{2,1,0:T(8,128)S(1)} %get-tuple-element.75), channel_id=1, source_target_pairs={{0,8},{8,0},{16,24},{24,16},{32,40},{40,32},{48,56},{56,48},{64,72... | collective-permute-start | bytes 786440 | tf_op jit(solution)/shard_map/ppermute | solution.py:383
  53.6 12.5 %collective-permute-start.17 = (f32[2,128,256]{2,1,0:T(8,128)S(1)}, f32[2,128,256]{2,1,0:T(8,128)S(1)}, u32[]{:S(2)}, u32[]{:S(2)}) collective-permute-start(f32[2,128,256]{2,1,0:T(8,128)S(1)} %get-tuple-element.94), channel_id=1, source_target_pairs={{0,8},{8,0},{16,24},{24,16},{32,40},{40,32},{48,56},{56,48},{64,72... | collective-permute-start | bytes 786440 | tf_op jit(solution)/shard_map/ppermute | solution.py:383
  56.3 11.5 %collective-permute-start.18 = (f32[2,128,256]{2,1,0:T(8,128)S(1)}, f32[2,128,256]{2,1,0:T(8,128)S(1)}, u32[]{:S(2)}, u32[]{:S(2)}) collective-permute-start(f32[2,128,256]{2,1,0:T(8,128)S(1)} %get-tuple-element.95), channel_id=1, source_target_pairs={{0,248},{8,16},{16,8},{24,32},{32,24},{40,48},{48,40},{56,64},{64,... | collective-permute-start | bytes 786440 | tf_op jit(solution)/shard_map/ppermute | solution.py:383
  61.9 12.5 %collective-permute-start.14 = (f32[2,128,384]{2,1,0:T(8,128)S(1)}, f32[2,128,384]{2,1,0:T(8,128)S(1)}, u32[]{:S(2)}, u32[]{:S(2)}) collective-permute-start(f32[2,128,384]{2,1,0:T(8,128)S(1)} %get-tuple-element.84), channel_id=1, source_target_pairs={{0,8},{8,0},{16,24},{24,16},{32,40},{40,32},{48,56},{56,48},{64,72... | collective-permute-start | bytes 1179656 | tf_op jit(solution)/shard_map/ppermute | solution.py:383
  62.0 14.2 %collective-permute-start.15 = (f32[2,128,384]{2,1,0:T(8,128)S(1)}, f32[2,128,384]{2,1,0:T(8,128)S(1)}, u32[]{:S(2)}, u32[]{:S(2)}) collective-permute-start(f32[2,128,384]{2,1,0:T(8,128)S(1)} %get-tuple-element.85), channel_id=1, source_target_pairs={{0,248},{8,16},{16,8},{24,32},{32,24},{40,48},{48,40},{56,64},{64,... | collective-permute-start | bytes 1179656 | tf_op jit(solution)/shard_map/ppermute | solution.py:383
  64.2 12.3 %collective-permute-start.11 = (f32[2,384,128]{2,1,0:T(8,128)S(1)}, f32[2,384,128]{2,1,0:T(8,128)S(1)}, u32[]{:S(2)}, u32[]{:S(2)}) collective-permute-start(f32[2,384,128]{2,1,0:T(8,128)S(1)} %get-tuple-element.77.refs_3_.refs_0_), channel_id=1, source_target_pairs={{1,0},{2,1},{3,2},{4,3},{5,4},{6,5},{7,6},{0,7},{9,8},{10,9},{11,1... | collective-permute-start | bytes 1179656 | tf_op jit(solution)/shard_map/ppermute | solution.py:375
  67.9 13.4 %collective-permute-start.19 = (f32[2,384,128]{2,1,0:T(8,128)S(1)}, f32[2,384,128]{2,1,0:T(8,128)S(1)}, u32[]{:S(2)}, u32[]{:S(2)}) collective-permute-start(f32[2,384,128]{2,1,0:T(8,128)S(1)} %get-tuple-element.96.refs_4_.refs_0_), channel_id=1, source_target_pairs={{1,0},{2,1},{3,2},{4,3},{5,4},{6,5},{7,6},{0,7},{9,8},{10,9},{11,1... | collective-permute-start | bytes 1179656 | tf_op jit(solution)/shard_map/ppermute | solution.py:375
  92.0 8.2 %collective-permute-start.28 = (f32[2,128,128]{2,1,0:T(8,128)S(1)}, f32[2,128,128]{2,1,0:T(8,128)S(1)}, u32[]{:S(2)}, u32[]{:S(2)}) collective-permute-start(f32[2,128,128]{2,1,0:T(8,128)S(1)} %get-tuple-element.112), channel_id=1, source_target_pairs={{248,0},{0,8},{8,16},{16,24},{24,32},{32,40},{40,48},{48,56},{56,6... | collective-permute-start | bytes 393224 | tf_op jit(solution)/shard_map/ppermute | solution.py:375
  92.3 17.2 %collective-permute-start.25 = (f32[2,128,128]{2,1,0:T(8,128)S(1)}, f32[2,128,128]{2,1,0:T(8,128)S(1)}, u32[]{:S(2)}, u32[]{:S(2)}) collective-permute-start(f32[2,128,128]{2,1,0:T(8,128)S(1)} %get-tuple-element.108), channel_id=1, source_target_pairs={{248,0},{0,8},{8,16},{16,24},{24,32},{32,40},{40,48},{48,56},{56,6... | collective-permute-start | bytes 393224 | tf_op jit(solution)/shard_map/ppermute | solution.py:375
  92.4 19.9 %collective-permute-start.22 = (f32[2,128,128]{2,1,0:T(8,128)S(1)}, f32[2,128,128]{2,1,0:T(8,128)S(1)}, u32[]{:S(2)}, u32[]{:S(2)}) collective-permute-start(f32[2,128,128]{2,1,0:T(8,128)S(1)} %get-tuple-element.104), channel_id=1, source_target_pairs={{248,0},{0,8},{8,16},{16,24},{24,32},{32,40},{40,48},{48,56},{56,6... | collective-permute-start | bytes 393224 | tf_op jit(solution)/shard_map/ppermute | solution.py:375
  95.6 13.0 %collective-permute-start.27 = (f32[2,128,128]{2,1,0:T(8,128)S(1)}, f32[2,128,128]{2,1,0:T(8,128)S(1)}, u32[]{:S(2)}, u32[]{:S(2)}) collective-permute-start(f32[2,128,128]{2,1,0:T(8,128)S(1)} %shard_map.83), channel_id=1, source_target_pairs={{248,0},{0,8},{8,16},{16,24},{24,32},{32,40},{40,48},{48,56},{56,6... | collective-permute-start | bytes 393224 | tf_op jit(solution)/shard_map/ppermute | solution.py:375
  99.8 11.6 %collective-permute-start.24 = (f32[2,128,128]{2,1,0:T(8,128)S(1)}, f32[2,128,128]{2,1,0:T(8,128)S(1)}, u32[]{:S(2)}, u32[]{:S(2)}) collective-permute-start(f32[2,128,128]{2,1,0:T(8,128)S(1)} %shard_map.82), channel_id=1, source_target_pairs={{248,0},{0,8},{8,16},{16,24},{24,32},{32,40},{40,48},{48,56},{56,6... | collective-permute-start | bytes 393224 | tf_op jit(solution)/shard_map/ppermute | solution.py:375
  100.2 14.0 %collective-permute-start.21 = (f32[2,128,128]{2,1,0:T(8,128)S(1)}, f32[2,128,128]{2,1,0:T(8,128)S(1)}, u32[]{:S(2)}, u32[]{:S(2)}) collective-permute-start(f32[2,128,128]{2,1,0:T(8,128)S(1)} %shard_map.81), channel_id=1, source_target_pairs={{248,0},{0,8},{8,16},{16,24},{24,32},{32,40},{40,48},{48,56},{56,6... | collective-permute-start | bytes 393224 | tf_op jit(solution)/shard_map/ppermute | solution.py:375
  (12 other events, 157.7 us)

commit v3 on v2

--- a/solution.py
+++ b/solution.py
@@ -26,12 +26,8 @@
     angle = (index[:, None] * index[None, :] % PROBE) * (-2.0 * math.pi / PROBE)
     cosines, sines = np.cos(angle) / math.sqrt(PROBE), np.sin(angle) / math.sqrt(PROBE)
     right = np.block([[cosines, sines], [-sines, cosines]]).astype(np.float32)
-    left = np.block([[cosines, -sines], [sines, cosines]]).astype(np.float32)
-    parts = []
-    for matrix in (right, left):
-        high = matrix.astype(BF16)
-        parts += [high, (matrix - high.astype(np.float32)).astype(BF16)]
-    return np.stack(parts)
+    high = right.astype(BF16)
+    return np.stack([high, (right - high.astype(np.float32)).astype(BF16)])
 
 
 def split(value):
@@ -430,28 +426,35 @@
     phase[:2] = probe[...]
     phase[2] = jnp.cos(propagator[...])
     phase[3] = jnp.sin(propagator[...])
-    copied[...] = tables[...]
+    h = PROBE
+    copied[:2] = tables[...]
+    copied[2:, :h, :h] = tables[:, :h, :h]
+    copied[2:, :h, h:] = tables[:, h:, :h]
+    copied[2:, h:, :h] = tables[:, :h, h:]
+    copied[2:, h:, h:] = tables[:, h:, h:]
 
 
 def prepare(probe, propagator):
     tables = jnp.asarray(dft_tables())
-    outs = [shape(4, PROBE, PROBE), jax.ShapeDtypeStruct(tables.shape, BF16)]
+    outs = [shape(4, PROBE, PROBE), jax.ShapeDtypeStruct((4, 2 * PROBE, 2 * PROBE), BF16)]
     return plain(prepare_kernel, outs, [probe, propagator, tables])
 
 
-def sums_kernel(wide, left, middle, low, right, from_left, *refs):
+def sums_kernel(summed, left, middle, low, right, *refs):
     h, t = PROBE, TILE
-    from_right = refs[0] if wide else None
     even_out, odd_out = refs[-2:]
+    from_left, from_right = refs[:2] if summed else (None, None)
+
+    def total(own, other, rows):
+        return own[:, rows] + other[:, rows] if summed else own[:, rows]
 
     def fill(down, up):
-        down[:, :, :h] = left[:, t:] + from_left[:, t:]
-        up[:, :, :h] = left[:, :h] + from_left[:, :h]
+        down[:, :, :h] = total(left, from_left, slice(t, t + h))
+        up[:, :, :h] = total(left, from_left, slice(0, h))
         down[:, :, h:t] = low[...]
         up[:, :, h:t] = middle[:, :h]
-        if wide:
-            down[:, :, t:] = right[:, t:] + from_right[:, t:]
-            up[:, :, t:] = right[:, :h] + from_right[:, :h]
+        down[:, :, t:] = total(right, from_right, slice(t, t + h))
+        up[:, :, t:] = total(right, from_right, slice(0, h))
 
     parity = lax.axis_index("row") & 1
 
@@ -464,60 +467,63 @@
         fill(odd_out, even_out)
 
 
-def sums(grad, from_left, from_right):
-    wide = from_right is not None
-    operands = [*grad, from_left] + ([from_right] if wide else [])
-    outs = [shape(2, PROBE, EXT if wide else TILE)] * 2
-    return plain(functools.partial(sums_kernel, wide), outs, operands)
-
-
-def update_kernel(wide, *refs):
+def sums(grad, columns):
+    body = functools.partial(sums_kernel, bool(columns))
+    return plain(body, [shape(2, PROBE, EXT)] * 2, [*grad, *columns])
+
+
+class Chosen:
+    def __init__(self, for_even, for_odd):
+        self.pair = for_even, for_odd
+
+    def __getitem__(self, where):
+        odd_row = (lax.axis_index("row") & 1) == 1
+        return jnp.where(odd_row, self.pair[1][where], self.pair[0][where])
+
+
+def edges_kernel(left, right, even, odd, west, east):
     h, t = PROBE, TILE
-    if wide:
-        tile, low, side, corner, left, middle, bottom, right, from_left, from_right, even, odd = refs[:12]
-        new_l, new_m, new_r = refs[12:]
-    else:
-        tile, low, left, middle, bottom, from_left, even, odd, new_l, new_m = refs
-    top, mid, end = slice(0, h), slice(h, t), slice(t, t + h)
+    above, below = Chosen(odd, even), Chosen(even, odd)
+    for out, own, cols in ((west, left, slice(0, h)), (east, right, slice(t, t + h))):
+        out[:, :h] = own[:, :h] + above[:, :, cols]
+        out[:, h:t] = own[:, h:t]
+        out[:, t:] = own[:, t:] + below[:, :, cols]
+
+
+def update_kernel(rows_first, tile, low, side, corner, left, middle, bottom, right, *refs):
+    from_left, from_right, even, odd, new_l, new_m, new_r = refs
+    h, t = PROBE, TILE
+    above, below = Chosen(odd, even), Chosen(even, odd)
     first, second, third = slice(0, h), slice(h, t), slice(t, t + h)
-
-    swap = (lax.axis_index("row") & 1) == 1
-
-    class Chosen:
-        def __init__(self, first, second):
-            self.first, self.second = first, second
-
-        def __getitem__(self, where):
-            return jnp.where(swap, self.second[where], self.first[where])
-
-    def fill(above, below):
-        new_l[:, top] = tile[:, 0, top, first] - STEP * (left[:, top] + from_left[:, top] + above[:, :, first])
-        new_l[:, mid] = tile[:, 0, mid, first] - STEP * (left[:, mid] + from_left[:, mid])
-        new_l[:, end] = low[:, :, first] - STEP * (left[:, end] + from_left[:, end] + below[:, :, first])
-        new_m[:, top] = tile[:, 0, top, second] - STEP * (middle[:, top] + above[:, :, second])
-        new_m[:, mid] = tile[:, 0, mid, second] - STEP * middle[:, mid]
-        new_m[:, end] = low[:, :, second] - STEP * (bottom[...] + below[:, :, second])
-        if wide:
-            new_r[:, top] = side[:, top] - STEP * (right[:, top] + from_right[:, top] + above[:, :, third])
-            new_r[:, mid] = side[:, mid] - STEP * (right[:, mid] + from_right[:, mid])
-            new_r[:, end] = corner[...] - STEP * (right[:, end] + from_right[:, end] + below[:, :, third])
-
-    fill(Chosen(odd, even), Chosen(even, odd))
-
-
-def update(layer, field, grad, from_left, from_right, even, odd):
-    tile, low, side, corner = field
-    if from_right is None:
-        operands = [tile, low, *grad[:3], from_left, even, odd]
-        specs = {0: tile_of(layer)}
-        return plain(functools.partial(update_kernel, False), [SIDE] * 2, operands, specs)
-    operands = [tile, low, side, corner, *grad, from_left, from_right, even, odd]
+    top, mid, end = first, second, third
+
+    def side_sum(own, other, rows, cols):
+        total = own[:, rows] + other[:, rows]
+        if rows_first or rows is mid:
+            return total
+        return total + (above if rows is top else below)[:, :, cols]
+
+    new_l[:, top] = tile[:, 0, top, first] - STEP * side_sum(left, from_left, top, first)
+    new_l[:, mid] = tile[:, 0, mid, first] - STEP * side_sum(left, from_left, mid, first)
+    new_l[:, end] = low[:, :, first] - STEP * side_sum(left, from_left, end, first)
+    new_m[:, top] = tile[:, 0, top, second] - STEP * (middle[:, top] + above[:, :, second])
+    new_m[:, mid] = tile[:, 0, mid, second] - STEP * middle[:, mid]
+    new_m[:, end] = low[:, :, second] - STEP * (bottom[...] + below[:, :, second])
+    new_r[:, top] = side[:, top] - STEP * side_sum(right, from_right, top, third)
+    new_r[:, mid] = side[:, mid] - STEP * side_sum(right, from_right, mid, third)
+    new_r[:, end] = corner[...] - STEP * side_sum(right, from_right, end, third)
+
+
+def update(layer, field, grad, columns, even, odd, rows_first):
+    operands = [*field, *grad, *columns, even, odd]
     specs = field_specs(0, layer, fill_first)
-    return plain(functools.partial(update_kernel, True), [SIDE] * 3, operands, specs)
+    body = functools.partial(update_kernel, rows_first)
+    return plain(body, [SIDE] * 3, operands, specs)
 
 
 def spill_kernel(left, from_left, down):
-    down[...] = left[:, TILE:] + from_left[:, TILE:]
+    rows = from_left.shape[1]
+    down[...] = left[:, TILE:] + from_left[:, rows - PROBE :]
 
 
 def last_kernel(n_alias, *refs):
@@ -580,25 +586,32 @@
 
     grads = gradients(fields, fill_first)
     renewed = [None] * SLICES
+
+    def columns(west, east):
+        from_left = shifted(east, "col", 1)
+        from_right = shifted(west, "col", -1)
+        return [from_left, from_right]
+
     for layer in (2, 0, 1):
-        grad, from_right = grads[layer], None
-        from_left = shifted(grad[3], "col", 1)
-        if layer == 1:
-            from_right = shifted(grad[0], "col", -1)
-        for_even, for_odd = sums(grad, from_left, from_right)
+        grad, rows_first = grads[layer], layer != 1
+        moved = [] if rows_first else columns(grad[0], grad[3])
+        for_even, for_odd = sums(grad, moved)
         even = swapped(for_even, 0)
         odd = swapped(for_odd, 1)
-        new = update(layer, fields[layer], grad, from_left, from_right, even, odd)
-        if layer != 1:
-            new = [*new, shifted(new[0], "col", -1)]
-        renewed[layer] = list(new)
+        if rows_first:
+            west, east = plain(edges_kernel, [SIDE] * 2, [grad[0], grad[3], even, odd])
+            moved = columns(west, east)
+            grad = [west, grad[1], grad[2], east]
+        renewed[layer] = list(update(layer, fields[layer], grad, moved, even, odd, rows_first))
     grads = gradients(renewed, fill_next)
     result = None
     for layer in (2, 1, 0):
         grad = grads[layer]
-        from_left = shifted(grad[3], "col", 1)
+        from_left = from_left_low = shifted(grad[3] if layer else grad[3][:, t:], "col", 1)
+        if layer == 0:
+            from_left = shifted(grad[3][:, :t], "col", 1)
         above_m = shifted(grad[2], "row", 1)
-        down = plain(spill_kernel, [shape(2, h, h)], [grad[0], from_left])[0]
+        down = plain(spill_kernel, [shape(2, h, h)], [grad[0], from_left_low])[0]
         above_l = shifted(down, "row", 1)
         result = last(result, layer, renewed[layer], grad, from_left, above_l, above_m)
     return result

time: 117 us -> 114 us (0.974)
  waiting for transfers between devices: 44 us -> 41.9 us
    ppermute x23 -> x24, waiting for transfers between devices: 35.9 us -> 27.9 us  [shifted(): lax.ppermute(block, axis, [((i - distance) % size, i) for i in range(size)])]
    ppermute x6, waiting for transfers between devices: 8.08 us -> 14.1 us  [swapped(): return lax.ppermute(block, 'row', sorted(route))]
    ppermute x23 -> x24, starting transfers between devices: 24.5 us -> 24.8 us  [shifted(): lax.ppermute(block, axis, [((i - distance) % size, i) for i in range(size)])]
    pallas_call x13 -> x15, Pallas kernels: 3.93 us -> 4.2 us  [plain(): pl.pallas_call(body, grid=(1,), in_specs=[specs.get(n, None) or whole(o)...]
  transfers between devices with their start and end apart: 29 -> 30, of which waited for: 14 -> 15; matrix products, arithmetic and copies ran while one was open for 0% -> 0% of each run, Pallas kernels for 16% -> 18%
where the time goes in v3:
time: 114 us; the launch traced here: 113 us
  waiting for transfers between devices  41.9 us (37%)
  starting transfers between devices  38.7 us (34%)
  Pallas kernels  30.3 us (27%)
  local copies, waits for them, and re-layouts  1.5 us (1%)
    ppermute x24, waiting for transfers between devices, shifted(): lax.ppermute(block, axis, [((i - distance) % size, i) for i in range(size)])  27.9 us
    pallas_call x10, Pallas kernels, run(): pl.pallas_call(body, grid=(1,), in_specs=in_specs, out_specs=[whole(o) fo...  26 us
    ppermute x24, starting transfers between devices, shifted(): lax.ppermute(block, axis, [((i - distance) % size, i) for i in range(size)])  24.8 us
    ppermute x6, waiting for transfers between devices, swapped(): return lax.ppermute(block, 'row', sorted(route))  14.1 us
    ppermute x6, starting transfers between devices, swapped(): return lax.ppermute(block, 'row', sorted(route))  13.9 us
    pallas_call x15, Pallas kernels, plain(): pl.pallas_call(body, grid=(1,), in_specs=[specs.get(n, None) or whole(o)...  4.2 us
  transfers between devices with their start and end apart: 30, of which 15 were waited for; matrix products, arithmetic and copies ran while one was open for 0% of the time, Pallas kernels for 18%

profile of v3, /device:TPU:7, one launch (start us, length us, event | category | flops | bytes accessed | tf_op | source)
XLA Modules:
  0.0 112.9 jit_solution(2235866663083017108)
XLA Ops:
  2.3 8.1 %collective-permute-start = (f32[2,128,256]{2,1,0:T(8,128)S(1)}, f32[2,128,256]{2,1,0:T(8,128)S(1)}, u32[]{:S(2)}, u32[]{:S(2)}) collective-permute-start(f32[2,128,256]{2,1,0:T(8,128)S(1)} %get-tuple-element.65), channel_id=1, source_target_pairs={{8,0},{16,8},{24,16},{32,24},{40,32},{48,40},{56,48},{64,56},{72,6... | collective-permute-start | bytes 786440 | tf_op jit(solution)/shard_map/ppermute | solution.py:371
  12.1 3.7 %collective-permute-done.refs_4_.low = f32[2,128,256]{2,1,0:T(8,128)S(1)} collective-permute-done((f32[2,128,256]{2,1,0:T(8,128)S(1)}, f32[2,128,256]{2,1,0:T(8,128)S(1)}, u32[]{:S(2)}, u32[]{:S(2)}) %collective-permute-start) | collective-permute-done | bytes 262176 | tf_op jit(solution)/shard_map/ppermute | solution.py:371
  17.7 3.7 %collective-permute-done.3.refs_5_.low = f32[2,128,256]{2,1,0:T(8,128)S(1)} collective-permute-done((f32[2,128,256]{2,1,0:T(8,128)S(1)}, f32[2,128,256]{2,1,0:T(8,128)S(1)}, u32[]{:S(2)}, u32[]{:S(2)}) %collective-permute-start.3) | collective-permute-done | bytes 262176 | tf_op jit(solution)/shard_map/ppermute | solution.py:371
  23.8 3.3 %collective-permute-done.6.refs_5_.low = f32[2,128,256]{2,1,0:T(8,128)S(1)} collective-permute-done((f32[2,128,256]{2,1,0:T(8,128)S(1)}, f32[2,128,256]{2,1,0:T(8,128)S(1)}, u32[]{:S(2)}, u32[]{:S(2)}) %collective-permute-start.6) | collective-permute-done | bytes 262176 | tf_op jit(solution)/shard_map/ppermute | solution.py:371
  33.1 2.9 %shard_map.67 = (f32[2,384,128]{2,1,0:T(8,128)S(1)}, f32[2,256,128]{2,1,0:T(8,128)S(1)}, f32[2,128,128]{2,1,0:T(8,128)S(1)}, f32[2,384,128]{2,1,0:T(8,128)S(1)}, f32[2,6,128,128]{3,2,1,0:T(8,128)S(1)}) custom-call(s32[2,6]{1,0:T(2,128)S(1)} %bitcast.8, bf16[4,256,256]{2,1,0:T(8,128)(2,1)S(1)} %get-tuple-element.67.refs_1_, f32[6,128,128]{2,1,0:T(8,128)S(1)} %bitcast.4, ...), custom_call_target="tpu_custom_call" | custom-call | flops 1207959552 | bytes 6684720 | tf_op jit(solution)/shard_map/pallas_call | solution.py:325
  36.0 2.6 %shard_map.68 = (f32[2,384,128]{2,1,0:T(8,128)S(1)}, f32[2,256,128]{2,1,0:T(8,128)S(1)}, f32[2,128,128]{2,1,0:T(8,128)S(1)}, f32[2,384,128]{2,1,0:T(8,128)S(1)}, f32[2,6,128,128]{3,2,1,0:T(8,128)S(1)}) custom-call(s32[2,6]{1,0:T(2,128)S(1)} %bitcast.9, bf16[4,256,256]{2,1,0:T(8,128)(2,1)S(1)} %get-tuple-element.67.refs_1_, ...), custom_call_target="tpu_custom_call" | custom-call | flops 1207959552 | bytes 5636144 | tf_op jit(solution)/shard_map/pallas_call | solution.py:325
  38.8 2.9 %collective-permute-start.12 = (f32[2,384,128]{2,1,0:T(8,128)S(1)}, f32[2,384,128]{2,1,0:T(8,128)S(1)}, u32[]{:S(2)}, u32[]{:S(2)}) collective-permute-start(f32[2,384,128]{2,1,0:T(8,128)S(1)} %get-tuple-element.92.right), channel_id=1, source_target_pairs={{7,0},{0,1},{1,2},{2,3},{3,4},{4,5},{5,6},{6,7},{15,8},{8,9},{9,10... | collective-permute-start | bytes 1179656 | tf_op jit(solution)/shard_map/ppermute | solution.py:371
  41.7 2.6 %shard_map.69 = (f32[2,384,128]{2,1,0:T(8,128)S(1)}, f32[2,256,128]{2,1,0:T(8,128)S(1)}, f32[2,128,128]{2,1,0:T(8,128)S(1)}, f32[2,384,128]{2,1,0:T(8,128)S(1)}) custom-call(s32[2,6]{1,0:T(2,128)S(1)} %bitcast.10, bf16[4,256,256]{2,1,0:T(8,128)(2,1)S(1)} %get-tuple-element.67.refs_1_, f32[4,128,128]{2,1,0:T(8,128)S(1)} %get-tuple-element.68.refs_2_, ...), custom_call_target="tpu_custom_call" | custom-call | flops 1207959552 | bytes 3276848 | tf_op jit(solution)/shard_map/pallas_call | solution.py:325
  44.4 5.6 %collective-permute-start.9 = (f32[2,128,384]{2,1,0:T(8,128)S(1)}, f32[2,128,384]{2,1,0:T(8,128)S(1)}, u32[]{:S(2)}, u32[]{:S(2)}) collective-permute-start(f32[2,128,384]{2,1,0:T(8,128)S(1)} %get-tuple-element.82), channel_id=1, source_target_pairs={{0,248},{8,16},{16,8},{24,32},{32,24},{40,48},{48,40},{56,64},{64,... | collective-permute-start | bytes 1179656 | tf_op jit(solution)/shard_map/ppermute | solution.py:379
  50.2 2.4 %collective-permute-start.17 = (f32[2,128,384]{2,1,0:T(8,128)S(1)}, f32[2,128,384]{2,1,0:T(8,128)S(1)}, u32[]{:S(2)}, u32[]{:S(2)}) collective-permute-start(f32[2,128,384]{2,1,0:T(8,128)S(1)} %get-tuple-element.104), channel_id=1, source_target_pairs={{0,248},{8,16},{16,8},{24,32},{32,24},{40,48},{48,40},{56,64},{64,... | collective-permute-start | bytes 1179656 | tf_op jit(solution)/shard_map/ppermute | solution.py:379
  52.8 2.7 %collective-permute-done.8.even.refs_2_ = f32[2,128,384]{2,1,0:T(8,128)S(1)} collective-permute-done((f32[2,128,384]{2,1,0:T(8,128)S(1)}, f32[2,128,384]{2,1,0:T(8,128)S(1)}, u32[]{:S(2)}, u32[]{:S(2)}) %collective-permute-start.8) | collective-permute-done | bytes 393248 | tf_op jit(solution)/shard_map/ppermute | solution.py:379
  55.5 5.5 %collective-permute-start.15 = (f32[2,128,384]{2,1,0:T(8,128)S(1)}, f32[2,128,384]{2,1,0:T(8,128)S(1)}, u32[]{:S(2)}, u32[]{:S(2)}) collective-permute-start(f32[2,128,384]{2,1,0:T(8,128)S(1)} %get-tuple-element.94), channel_id=1, source_target_pairs={{0,248},{8,16},{16,8},{24,32},{32,24},{40,48},{48,40},{56,64},{64,... | collective-permute-start | bytes 1179656 | tf_op jit(solution)/shard_map/ppermute | solution.py:379
  61.2 2.8 %collective-permute-done.16.even.refs_2_ = f32[2,128,384]{2,1,0:T(8,128)S(1)} collective-permute-done((f32[2,128,384]{2,1,0:T(8,128)S(1)}, f32[2,128,384]{2,1,0:T(8,128)S(1)}, u32[]{:S(2)}, u32[]{:S(2)}) %collective-permute-start.16) | collective-permute-done | bytes 393248 | tf_op jit(solution)/shard_map/ppermute | solution.py:379
  64.8 3.3 %collective-permute-done.17.odd.refs_3_ = f32[2,128,384]{2,1,0:T(8,128)S(1)} collective-permute-done((f32[2,128,384]{2,1,0:T(8,128)S(1)}, f32[2,128,384]{2,1,0:T(8,128)S(1)}, u32[]{:S(2)}, u32[]{:S(2)}) %collective-permute-start.17) | collective-permute-done | bytes 393248 | tf_op jit(solution)/shard_map/ppermute | solution.py:379
  68.2 2.6 %collective-permute-done.14.refs_2_ = f32[2,128,384]{2,1,0:T(8,128)S(1)} collective-permute-done((f32[2,128,384]{2,1,0:T(8,128)S(1)}, f32[2,128,384]{2,1,0:T(8,128)S(1)}, u32[]{:S(2)}, u32[]{:S(2)}) %collective-permute-start.14) | collective-permute-done | bytes 393248 | tf_op jit(solution)/shard_map/ppermute | solution.py:379
  71.7 2.8 %collective-permute-done.15.refs_3_ = f32[2,128,384]{2,1,0:T(8,128)S(1)} collective-permute-done((f32[2,128,384]{2,1,0:T(8,128)S(1)}, f32[2,128,384]{2,1,0:T(8,128)S(1)}, u32[]{:S(2)}, u32[]{:S(2)}) %collective-permute-start.15) | collective-permute-done | bytes 393248 | tf_op jit(solution)/shard_map/ppermute | solution.py:379
  80.0 2.9 %shard_map.80 = (f32[2,384,128]{2,1,0:T(8,128)S(1)}, f32[2,256,128]{2,1,0:T(8,128)S(1)}, f32[2,128,128]{2,1,0:T(8,128)S(1)}, f32[2,384,128]{2,1,0:T(8,128)S(1)}, f32[2,6,128,128]{3,2,1,0:T(8,128)S(1)}) custom-call(s32[2,6]{1,0:T(2,128)S(1)} %bitcast.13, bf16[4,256,256]{2,1,0:T(8,128)(2,1)S(1)} %get-tuple-element.67.refs_1_, f32[6,128,128]{2,1,0:T(8,128)S(1)} %bitcast.5, ...), custom_call_target="tpu_custom_call" | custom-call | flops 1207959552 | bytes 5374000 | tf_op jit(solution)/shard_map/pallas_call | solution.py:325
  84.4 2.6 %shard_map.81 = (f32[2,384,128]{2,1,0:T(8,128)S(1)}, f32[2,256,128]{2,1,0:T(8,128)S(1)}, f32[2,128,128]{2,1,0:T(8,128)S(1)}, f32[2,384,128]{2,1,0:T(8,128)S(1)}, f32[2,6,128,128]{3,2,1,0:T(8,128)S(1)}) custom-call(s32[2,6]{1,0:T(2,128)S(1)} %bitcast.14, bf16[4,256,256]{2,1,0:T(8,128)(2,1)S(1)} %get-tuple-element.67.refs_1_, ...), custom_call_target="tpu_custom_call" | custom-call | flops 1207959552 | bytes 5636144 | tf_op jit(solution)/shard_map/pallas_call | solution.py:325
  87.0 2.6 %shard_map.82 = (f32[2,384,128]{2,1,0:T(8,128)S(1)}, f32[2,256,128]{2,1,0:T(8,128)S(1)}, f32[2,128,128]{2,1,0:T(8,128)S(1)}, f32[2,384,128]{2,1,0:T(8,128)S(1)}) custom-call(s32[2,6]{1,0:T(2,128)S(1)} %bitcast.15, bf16[4,256,256]{2,1,0:T(8,128)(2,1)S(1)} %get-tuple-element.67.refs_1_, f32[4,128,128]{2,1,0:T(8,128)S(1)} %get-tuple-element.68.refs_2_, ...), custom_call_target="tpu_custom_call" | custom-call | flops 1207959552 | bytes 3276848 | tf_op jit(solution)/shard_map/pallas_call | solution.py:325
  90.2 2.8 %collective-permute-start.20 = (f32[2,256,128]{2,1,0:T(8,128)S(1)}, f32[2,256,128]{2,1,0:T(8,128)S(1)}, u32[]{:S(2)}, u32[]{:S(2)}) collective-permute-start(f32[2,256,128]{2,1,0:T(8,128)S(1)} %slice.18), channel_id=1, source_target_pairs={{7,0},{0,1},{1,2},{2,3},{3,4},{4,5},{5,6},{6,7},{15,8},{8,9},{9,10... | collective-permute-start | bytes 786440 | tf_op jit(solution)/shard_map/ppermute | solution.py:371
  94.9 3.0 %collective-permute-done.29.refs_6_ = f32[2,128,128]{2,1,0:T(8,128)S(1)} collective-permute-done((f32[2,128,128]{2,1,0:T(8,128)S(1)}, f32[2,128,128]{2,1,0:T(8,128)S(1)}, u32[]{:S(2)}, u32[]{:S(2)}) %collective-permute-start.29) | collective-permute-done | bytes 131104 | tf_op jit(solution)/shard_map/ppermute | solution.py:371
  97.9 2.8 %collective-permute-done.28.refs_5_ = f32[2,128,128]{2,1,0:T(8,128)S(1)} collective-permute-done((f32[2,128,128]{2,1,0:T(8,128)S(1)}, f32[2,128,128]{2,1,0:T(8,128)S(1)}, u32[]{:S(2)}, u32[]{:S(2)}) %collective-permute-start.28) | collective-permute-done | bytes 131104 | tf_op jit(solution)/shard_map/ppermute | solution.py:371
  103.6 2.8 %collective-permute-done.25.refs_5_ = f32[2,128,128]{2,1,0:T(8,128)S(1)} collective-permute-done((f32[2,128,128]{2,1,0:T(8,128)S(1)}, f32[2,128,128]{2,1,0:T(8,128)S(1)}, u32[]{:S(2)}, u32[]{:S(2)}) %collective-permute-start.25) | collective-permute-done | bytes 131104 | tf_op jit(solution)/shard_map/ppermute | solution.py:371
  109.2 2.8 %collective-permute-done.22.refs_5_ = f32[2,128,128]{2,1,0:T(8,128)S(1)} collective-permute-done((f32[2,128,128]{2,1,0:T(8,128)S(1)}, f32[2,128,128]{2,1,0:T(8,128)S(1)}, u32[]{:S(2)}, u32[]{:S(2)}) %collective-permute-start.22) | collective-permute-done | bytes 131104 | tf_op jit(solution)/shard_map/ppermute | solution.py:371
  (82 shorter events, 32.7 us)
Async XLA Ops:
  1.5 29.1 %collective-permute-start.4 = (f32[2,2,256,128]{3,2,1,0:T(8,128)S(1)}, f32[2,2,256,128]{3,2,1,0:T(8,128)S(1)}, u32[]{:S(2)}, u32[]{:S(2)}) collective-permute-start(f32[2,2,256,128]{3,2,1,0:T(8,128)S(1)} %get-tuple-element.71), channel_id=1, source_target_pairs={{1,0},{2,1},{3,2},{4,3},{5,4},{6,5},{7,6},{0,7},{9,8},{10,9},{11,1... | collective-permute-start | bytes 1572872 | tf_op jit(solution)/shard_map/ppermute | solution.py:371
  2.3 13.5 %collective-permute-start = (f32[2,128,256]{2,1,0:T(8,128)S(1)}, f32[2,128,256]{2,1,0:T(8,128)S(1)}, u32[]{:S(2)}, u32[]{:S(2)}) collective-permute-start(f32[2,128,256]{2,1,0:T(8,128)S(1)} %get-tuple-element.65), channel_id=1, source_target_pairs={{8,0},{16,8},{24,16},{32,24},{40,32},{48,40},{56,48},{64,56},{72,6... | collective-permute-start | bytes 786440 | tf_op jit(solution)/shard_map/ppermute | solution.py:371
  10.4 11.0 %collective-permute-start.3 = (f32[2,128,256]{2,1,0:T(8,128)S(1)}, f32[2,128,256]{2,1,0:T(8,128)S(1)}, u32[]{:S(2)}, u32[]{:S(2)}) collective-permute-start(f32[2,128,256]{2,1,0:T(8,128)S(1)} %get-tuple-element.70), channel_id=1, source_target_pairs={{8,0},{16,8},{24,16},{32,24},{40,32},{48,40},{56,48},{64,56},{72,6... | collective-permute-start | bytes 786440 | tf_op jit(solution)/shard_map/ppermute | solution.py:371
  10.9 16.2 %collective-permute-start.6 = (f32[2,128,256]{2,1,0:T(8,128)S(1)}, f32[2,128,256]{2,1,0:T(8,128)S(1)}, u32[]{:S(2)}, u32[]{:S(2)}) collective-permute-start(f32[2,128,256]{2,1,0:T(8,128)S(1)} %get-tuple-element.73), channel_id=1, source_target_pairs={{8,0},{16,8},{24,16},{32,24},{40,32},{48,40},{56,48},{64,56},{72,6... | collective-permute-start | bytes 786440 | tf_op jit(solution)/shard_map/ppermute | solution.py:371
  11.0 17.1 %collective-permute-start.1 = (f32[2,256,128]{2,1,0:T(8,128)S(1)}, f32[2,256,128]{2,1,0:T(8,128)S(1)}, u32[]{:S(2)}, u32[]{:S(2)}) collective-permute-start(f32[2,256,128]{2,1,0:T(8,128)S(1)} %get-tuple-element.66), channel_id=1, source_target_pairs={{1,0},{2,1},{3,2},{4,3},{5,4},{6,5},{7,6},{0,7},{9,8},{10,9},{11,1... | collective-permute-start | bytes 786440 | tf_op jit(solution)/shard_map/ppermute | solution.py:371
  15.8 12.4 %collective-permute-start.2 = (f32[2,128,128]{2,1,0:T(8,128)S(1)}, f32[2,128,128]{2,1,0:T(8,128)S(1)}, u32[]{:S(2)}, u32[]{:S(2)}) collective-permute-start(f32[2,128,128]{2,1,0:T(8,128)S(1)} %slice.20), channel_id=1, source_target_pairs={{1,0},{2,1},{3,2},{4,3},{5,4},{6,5},{7,6},{0,7},{9,8},{10,9},{11,1... | collective-permute-start | bytes 393224 | tf_op jit(solution)/shard_map/ppermute | solution.py:371
  21.4 9.2 %collective-permute-start.5 = (f32[2,128,128]{2,1,0:T(8,128)S(1)}, f32[2,128,128]{2,1,0:T(8,128)S(1)}, u32[]{:S(2)}, u32[]{:S(2)}) collective-permute-start(f32[2,128,128]{2,1,0:T(8,128)S(1)} %slice.21), channel_id=1, source_target_pairs={{1,0},{2,1},{3,2},{4,3},{5,4},{6,5},{7,6},{0,7},{9,8},{10,9},{11,1... | collective-permute-start | bytes 393224 | tf_op jit(solution)/shard_map/ppermute | solution.py:371
  38.7 11.5 %collective-permute-start.13 = (f32[2,384,128]{2,1,0:T(8,128)S(1)}, f32[2,384,128]{2,1,0:T(8,128)S(1)}, u32[]{:S(2)}, u32[]{:S(2)}) collective-permute-start(f32[2,384,128]{2,1,0:T(8,128)S(1)} %get-tuple-element.89.left), channel_id=1, source_target_pairs={{1,0},{2,1},{3,2},{4,3},{5,4},{6,5},{7,6},{0,7},{9,8},{10,9},{11,1... | collective-permute-start | bytes 1179656 | tf_op jit(solution)/shard_map/ppermute | solution.py:371
  38.8 13.9 %collective-permute-start.12 = (f32[2,384,128]{2,1,0:T(8,128)S(1)}, f32[2,384,128]{2,1,0:T(8,128)S(1)}, u32[]{:S(2)}, u32[]{:S(2)}) collective-permute-start(f32[2,384,128]{2,1,0:T(8,128)S(1)} %get-tuple-element.92.right), channel_id=1, source_target_pairs={{7,0},{0,1},{1,2},{2,3},{3,4},{4,5},{5,6},{6,7},{15,8},{8,9},{9,10... | collective-permute-start | bytes 1179656 | tf_op jit(solution)/shard_map/ppermute | solution.py:371
  44.3 11.2 %collective-permute-start.8 = (f32[2,128,384]{2,1,0:T(8,128)S(1)}, f32[2,128,384]{2,1,0:T(8,128)S(1)}, u32[]{:S(2)}, u32[]{:S(2)}) collective-permute-start(f32[2,128,384]{2,1,0:T(8,128)S(1)} %get-tuple-element.81), channel_id=1, source_target_pairs={{0,8},{8,0},{16,24},{24,16},{32,40},{40,32},{48,56},{56,48},{64,72... | collective-permute-start | bytes 1179656 | tf_op jit(solution)/shard_map/ppermute | solution.py:379
  44.4 16.7 %collective-permute-start.9 = (f32[2,128,384]{2,1,0:T(8,128)S(1)}, f32[2,128,384]{2,1,0:T(8,128)S(1)}, u32[]{:S(2)}, u32[]{:S(2)}) collective-permute-start(f32[2,128,384]{2,1,0:T(8,128)S(1)} %get-tuple-element.82), channel_id=1, source_target_pairs={{0,248},{8,16},{16,8},{24,32},{32,24},{40,48},{48,40},{56,64},{64,... | collective-permute-start | bytes 1179656 | tf_op jit(solution)/shard_map/ppermute | solution.py:379
  50.1 13.9 %collective-permute-start.16 = (f32[2,128,384]{2,1,0:T(8,128)S(1)}, f32[2,128,384]{2,1,0:T(8,128)S(1)}, u32[]{:S(2)}, u32[]{:S(2)}) collective-permute-start(f32[2,128,384]{2,1,0:T(8,128)S(1)} %get-tuple-element.103), channel_id=1, source_target_pairs={{0,8},{8,0},{16,24},{24,16},{32,40},{40,32},{48,56},{56,48},{64,72... | collective-permute-start | bytes 1179656 | tf_op jit(solution)/shard_map/ppermute | solution.py:379
  50.2 17.9 %collective-permute-start.17 = (f32[2,128,384]{2,1,0:T(8,128)S(1)}, f32[2,128,384]{2,1,0:T(8,128)S(1)}, u32[]{:S(2)}, u32[]{:S(2)}) collective-permute-start(f32[2,128,384]{2,1,0:T(8,128)S(1)} %get-tuple-element.104), channel_id=1, source_target_pairs={{0,248},{8,16},{16,8},{24,32},{32,24},{40,48},{48,40},{56,64},{64,... | collective-permute-start | bytes 1179656 | tf_op jit(solution)/shard_map/ppermute | solution.py:379
  52.7 18.1 %collective-permute-start.14 = (f32[2,128,384]{2,1,0:T(8,128)S(1)}, f32[2,128,384]{2,1,0:T(8,128)S(1)}, u32[]{:S(2)}, u32[]{:S(2)}) collective-permute-start(f32[2,128,384]{2,1,0:T(8,128)S(1)} %get-tuple-element.93), channel_id=1, source_target_pairs={{0,8},{8,0},{16,24},{24,16},{32,40},{40,32},{48,56},{56,48},{64,72... | collective-permute-start | bytes 1179656 | tf_op jit(solution)/shard_map/ppermute | solution.py:379
  55.5 18.9 %collective-permute-start.15 = (f32[2,128,384]{2,1,0:T(8,128)S(1)}, f32[2,128,384]{2,1,0:T(8,128)S(1)}, u32[]{:S(2)}, u32[]{:S(2)}) collective-permute-start(f32[2,128,384]{2,1,0:T(8,128)S(1)} %get-tuple-element.94), channel_id=1, source_target_pairs={{0,248},{8,16},{16,8},{24,32},{32,24},{40,48},{48,40},{56,64},{64,... | collective-permute-start | bytes 1179656 | tf_op jit(solution)/shard_map/ppermute | solution.py:379
  61.2 13.5 %collective-permute-start.11 = (f32[2,384,128]{2,1,0:T(8,128)S(1)}, f32[2,384,128]{2,1,0:T(8,128)S(1)}, u32[]{:S(2)}, u32[]{:S(2)}) collective-permute-start(f32[2,384,128]{2,1,0:T(8,128)S(1)} %get-tuple-element.83.left), channel_id=1, source_target_pairs={{1,0},{2,1},{3,2},{4,3},{5,4},{6,5},{7,6},{0,7},{9,8},{10,9},{11,1... | collective-permute-start | bytes 1179656 | tf_op jit(solution)/shard_map/ppermute | solution.py:371
  63.9 10.8 %collective-permute-start.10 = (f32[2,384,128]{2,1,0:T(8,128)S(1)}, f32[2,384,128]{2,1,0:T(8,128)S(1)}, u32[]{:S(2)}, u32[]{:S(2)}) collective-permute-start(f32[2,384,128]{2,1,0:T(8,128)S(1)} %get-tuple-element.84.right), channel_id=1, source_target_pairs={{7,0},{0,1},{1,2},{2,3},{3,4},{4,5},{5,6},{6,7},{15,8},{8,9},{9,10... | collective-permute-start | bytes 1179656 | tf_op jit(solution)/shard_map/ppermute | solution.py:371
  68.2 11.6 %collective-permute-start.19 = (f32[2,384,128]{2,1,0:T(8,128)S(1)}, f32[2,384,128]{2,1,0:T(8,128)S(1)}, u32[]{:S(2)}, u32[]{:S(2)}) collective-permute-start(f32[2,384,128]{2,1,0:T(8,128)S(1)} %get-tuple-element.105.left), channel_id=1, source_target_pairs={{1,0},{2,1},{3,2},{4,3},{5,4},{6,5},{7,6},{0,7},{9,8},{10,9},{11,1... | collective-permute-start | bytes 1179656 | tf_op jit(solution)/shard_map/ppermute | solution.py:371
  70.8 9.0 %collective-permute-start.18 = (f32[2,384,128]{2,1,0:T(8,128)S(1)}, f32[2,384,128]{2,1,0:T(8,128)S(1)}, u32[]{:S(2)}, u32[]{:S(2)}) collective-permute-start(f32[2,384,128]{2,1,0:T(8,128)S(1)} %get-tuple-element.106.right), channel_id=1, source_target_pairs={{7,0},{0,1},{1,2},{2,3},{3,4},{4,5},{5,6},{6,7},{15,8},{8,9},{9,10... | collective-permute-start | bytes 1179656 | tf_op jit(solution)/shard_map/ppermute | solution.py:371
  90.1 10.7 %collective-permute-start.28 = (f32[2,128,128]{2,1,0:T(8,128)S(1)}, f32[2,128,128]{2,1,0:T(8,128)S(1)}, u32[]{:S(2)}, u32[]{:S(2)}) collective-permute-start(f32[2,128,128]{2,1,0:T(8,128)S(1)} %shard_map.85), channel_id=1, source_target_pairs={{248,0},{0,8},{8,16},{16,24},{24,32},{32,40},{40,48},{48,56},{56,6... | collective-permute-start | bytes 393224 | tf_op jit(solution)/shard_map/ppermute | solution.py:371
  90.2 21.8 %collective-permute-start.20 = (f32[2,256,128]{2,1,0:T(8,128)S(1)}, f32[2,256,128]{2,1,0:T(8,128)S(1)}, u32[]{:S(2)}, u32[]{:S(2)}) collective-permute-start(f32[2,256,128]{2,1,0:T(8,128)S(1)} %slice.18), channel_id=1, source_target_pairs={{7,0},{0,1},{1,2},{2,3},{3,4},{4,5},{5,6},{6,7},{15,8},{8,9},{9,10... | collective-permute-start | bytes 786440 | tf_op jit(solution)/shard_map/ppermute | solution.py:371
  94.8 11.6 %collective-permute-start.25 = (f32[2,128,128]{2,1,0:T(8,128)S(1)}, f32[2,128,128]{2,1,0:T(8,128)S(1)}, u32[]{:S(2)}, u32[]{:S(2)}) collective-permute-start(f32[2,128,128]{2,1,0:T(8,128)S(1)} %shard_map.84), channel_id=1, source_target_pairs={{248,0},{0,8},{8,16},{16,24},{24,32},{32,40},{40,48},{48,56},{56,6... | collective-permute-start | bytes 393224 | tf_op jit(solution)/shard_map/ppermute | solution.py:371
  97.9 11.3 %collective-permute-start.23 = (f32[2,128,128]{2,1,0:T(8,128)S(1)}, f32[2,128,128]{2,1,0:T(8,128)S(1)}, u32[]{:S(2)}, u32[]{:S(2)}) collective-permute-start(f32[2,128,128]{2,1,0:T(8,128)S(1)} %get-tuple-element.116), channel_id=1, source_target_pairs={{248,0},{0,8},{8,16},{16,24},{24,32},{32,40},{40,48},{48,56},{56,6... | collective-permute-start | bytes 393224 | tf_op jit(solution)/shard_map/ppermute | solution.py:371
  100.7 11.3 %collective-permute-start.22 = (f32[2,128,128]{2,1,0:T(8,128)S(1)}, f32[2,128,128]{2,1,0:T(8,128)S(1)}, u32[]{:S(2)}, u32[]{:S(2)}) collective-permute-start(f32[2,128,128]{2,1,0:T(8,128)S(1)} %shard_map.83), channel_id=1, source_target_pairs={{248,0},{0,8},{8,16},{16,24},{24,32},{32,40},{40,48},{48,56},{56,6... | collective-permute-start | bytes 393224 | tf_op jit(solution)/shard_map/ppermute | solution.py:371
  (13 other events, 165.8 us)

commit v4 on v3

--- a/solution.py
+++ b/solution.py
@@ -521,34 +521,44 @@
     return plain(body, [SIDE] * 3, operands, specs)
 
 
-def spill_kernel(left, from_left, down):
-    rows = from_left.shape[1]
-    down[...] = left[:, TILE:] + from_left[:, rows - PROBE :]
-
-
-def last_kernel(n_alias, *refs):
-    old_l, old_m, left, middle, from_left, above_l, above_m = refs[:7]
-    out = refs[7 + n_alias]
-    h, t = PROBE, TILE
-    out[:, 0, :h, :h] = old_l[:, :h] - STEP * (left[:, :h] + from_left[:, :h] + above_l[...])
-    out[:, 0, h:, :h] = old_l[:, h:t] - STEP * (left[:, h:t] + from_left[:, h:t])
-    out[:, 0, :h, h:] = old_m[:, :h] - STEP * (middle[:, :h] + above_m[...])
-    out[:, 0, h:, h:] = old_m[:, h:t] - STEP * middle[:, h:t]
-
-
-def last(result, layer, field, grad, from_left, above_l, above_m):
-    operands = [field[0], field[1], grad[0], grad[1], from_left, above_l, above_m]
+def spill_kernel(*refs):
+    down = refs[-1]
+    for n in range(down.shape[0]):
+        left, from_left = refs[2 * n : 2 * n + 2]
+        rows = from_left.shape[1]
+        down[n] = left[:, TILE:] + from_left[:, rows - PROBE :]
+
+
+def spill(*pairs):
+    operands = [array for pair in pairs for array in pair]
+    return plain(spill_kernel, [shape(len(pairs), 2, PROBE, PROBE)], operands)[0]
+
+
+def last_kernel(layers, place, *refs):
+    out, h, t = refs[-1], PROBE, TILE
+    above_l = refs[6 * layers]
+    for n in range(layers):
+        old_l, old_m, left, middle, from_left, above_m = refs[6 * n : 6 * n + 6]
+        top_l = left[:, :h] + from_left[:, :h] + above_l[n]
+        out[:, place + n, :h, :h] = old_l[:, :h] - STEP * top_l
+        out[:, place + n, h:, :h] = old_l[:, h:t] - STEP * (left[:, h:t] + from_left[:, h:t])
+        out[:, place + n, :h, h:] = old_m[:, :h] - STEP * (middle[:, :h] + above_m[...])
+        out[:, place + n, h:, h:] = old_m[:, h:t] - STEP * middle[:, h:t]
+
+
+def last(pieces, above_l, spec, result):
+    operands = [array for piece in pieces for array in piece] + [above_l]
     specs, aliases = {}, {}
     if result is not None:
+        specs, aliases = {len(operands): pl.BlockSpec(memory_space=pl.ANY)}, {len(operands): 0}
         operands.append(result)
-        specs, aliases = {7: pl.BlockSpec(memory_space=pl.ANY)}, {7: 0}
     return plain(
-        functools.partial(last_kernel, len(operands) - 7),
+        functools.partial(last_kernel, len(pieces), 0 if result is not None else 1),
         [shape(2, SLICES, TILE, TILE)],
         operands,
         specs,
         aliases,
-        [tile_of(layer)],
+        [spec],
     )[0]
 
 
@@ -592,8 +602,8 @@
         from_right = shifted(west, "col", -1)
         return [from_left, from_right]
 
-    for layer in (2, 0, 1):
-        grad, rows_first = grads[layer], layer != 1
+    for layer in (2, 1, 0):
+        grad, rows_first = grads[layer], layer != 0
         moved = [] if rows_first else columns(grad[0], grad[3])
         for_even, for_odd = sums(grad, moved)
         even = swapped(for_even, 0)
@@ -604,17 +614,22 @@
             grad = [west, grad[1], grad[2], east]
         renewed[layer] = list(update(layer, fields[layer], grad, moved, even, odd, rows_first))
     grads = gradients(renewed, fill_next)
-    result = None
+    from_left, above_m = {}, {}
     for layer in (2, 1, 0):
-        grad = grads[layer]
-        from_left = from_left_low = shifted(grad[3] if layer else grad[3][:, t:], "col", 1)
-        if layer == 0:
-            from_left = shifted(grad[3][:, :t], "col", 1)
-        above_m = shifted(grad[2], "row", 1)
-        down = plain(spill_kernel, [shape(2, h, h)], [grad[0], from_left_low])[0]
-        above_l = shifted(down, "row", 1)
-        result = last(result, layer, renewed[layer], grad, from_left, above_l, above_m)
-    return result
+        right = grads[layer][3]
+        from_left[layer] = shifted(right if layer else right[:, t:], "col", 1)
+        above_m[layer] = shifted(grads[layer][2], "row", 1)
+    down = spill((grads[1][0], from_left[1]), (grads[2][0], from_left[2]))
+    above_l12 = shifted(down, "row", 1)
+    down = spill((grads[0][0], from_left[0]))
+    above_l0 = shifted(down, "row", 1)
+    from_left[0] = shifted(grads[0][3][:, :t], "col", 1)
+    pieces = [
+        (renewed[n][0], renewed[n][1], grads[n][0], grads[n][1], from_left[n], above_m[n])
+        for n in range(SLICES)
+    ]
+    result = last(pieces[1:], above_l12, whole(shape(2, SLICES, TILE, TILE)), None)
+    return last(pieces[:1], above_l0, tile_of(0), result)
 
 
 def solution(mesh):

time: 114 us -> 122 us (1.070)
  the two profiles are of different devices: /device:TPU:7 before, /device:TPU:0 now
where the time goes in v4:
time: 122 us
  waiting for transfers between devices  54.9 us (45%)
  starting transfers between devices  35.2 us (29%)
  Pallas kernels  29.8 us (24%)
  local copies, waits for them, and re-layouts  1.5 us (1%)
    ppermute x23, waiting for transfers between devices, shifted(): lax.ppermute(block, axis, [((i - distance) % size, i) for i in range(size)])  44.9 us
    pallas_call x10, Pallas kernels, run(): pl.pallas_call(body, grid=(1,), in_specs=in_specs, out_specs=[whole(o) fo...  26 us
    ppermute x23, starting transfers between devices, shifted(): lax.ppermute(block, axis, [((i - distance) % size, i) for i in range(size)])  18.3 us
    ppermute x6, starting transfers between devices, swapped(): return lax.ppermute(block, 'row', sorted(route))  16.9 us
    ppermute x6, waiting for transfers between devices, swapped(): return lax.ppermute(block, 'row', sorted(route))  10 us
    pallas_call x13, Pallas kernels, plain(): pl.pallas_call(body, grid=(1,), in_specs=[specs.get(n, None) or whole(o)...  3.68 us
  transfers between devices with their start and end apart: 29, of which 15 were waited for; matrix products, arithmetic and copies ran while one was open for 0% of the time, Pallas kernels for 12%

profile of v4, /device:TPU:0, one launch (start us, length us, event | category | flops | bytes accessed | tf_op | source)
XLA Modules:
  0.0 121.8 jit_solution(917341879555202695)
XLA Ops:
  2.1 8.4 %collective-permute-start = (f32[2,128,256]{2,1,0:T(8,128)S(1)}, f32[2,128,256]{2,1,0:T(8,128)S(1)}, u32[]{:S(2)}, u32[]{:S(2)}) collective-permute-start(f32[2,128,256]{2,1,0:T(8,128)S(1)} %get-tuple-element.65), channel_id=1, source_target_pairs={{8,0},{16,8},{24,16},{32,24},{40,32},{48,40},{56,48},{64,56},{72,6... | collective-permute-start | bytes 786440 | tf_op jit(solution)/shard_map/ppermute | solution.py:371
  11.7 5.5 %collective-permute-done.refs_4_.low = f32[2,128,256]{2,1,0:T(8,128)S(1)} collective-permute-done((f32[2,128,256]{2,1,0:T(8,128)S(1)}, f32[2,128,256]{2,1,0:T(8,128)S(1)}, u32[]{:S(2)}, u32[]{:S(2)}) %collective-permute-start) | collective-permute-done | bytes 262176 | tf_op jit(solution)/shard_map/ppermute | solution.py:371
  17.2 5.6 %collective-permute-done.3.refs_5_.low = f32[2,128,256]{2,1,0:T(8,128)S(1)} collective-permute-done((f32[2,128,256]{2,1,0:T(8,128)S(1)}, f32[2,128,256]{2,1,0:T(8,128)S(1)}, u32[]{:S(2)}, u32[]{:S(2)}) %collective-permute-start.3) | collective-permute-done | bytes 262176 | tf_op jit(solution)/shard_map/ppermute | solution.py:371
  23.3 2.4 %collective-permute-done.6.refs_5_.low = f32[2,128,256]{2,1,0:T(8,128)S(1)} collective-permute-done((f32[2,128,256]{2,1,0:T(8,128)S(1)}, f32[2,128,256]{2,1,0:T(8,128)S(1)}, u32[]{:S(2)}, u32[]{:S(2)}) %collective-permute-start.6) | collective-permute-done | bytes 262176 | tf_op jit(solution)/shard_map/ppermute | solution.py:371
  27.6 2.4 %shard_map.65 = (f32[2,6,128,128]{3,2,1,0:T(8,128)}, f32[2,6,128,128]{3,2,1,0:T(8,128)S(1)}) custom-call(s32[2,6]{1,0:T(2,128)S(1)} %bitcast.6, bf16[4,256,256]{2,1,0:T(8,128)(2,1)S(1)} %get-tuple-element.67.refs_1_, f32[4,128,128]{2,1,0:T(8,128)S(1)} %get-tuple-element.68.refs_2_, f32[2,3,256,256]{3,2,1,0:T(8,128)S(1)} %copy-done.1, ...), custom_call_target="tpu_custom_call" | custom-call | flops 1207959552 | bytes 5111856 | tf_op jit(solution)/shard_map/pallas_call | solution.py:325
  30.0 2.4 %shard_map.66 = (f32[2,6,128,128]{3,2,1,0:T(8,128)S(1)}, f32[2,6,128,128]{3,2,1,0:T(8,128)S(1)}) custom-call(s32[2,6]{1,0:T(2,128)S(1)} %bitcast.7, bf16[4,256,256]{2,1,0:T(8,128)(2,1)S(1)} %get-tuple-element.67.refs_1_, f32[4,128,128]{2,1,0:T(8,128)S(1)} %get-tuple-element.68.refs_2_, f32[2,6,128,128]{3,2,1,0:T(8,128)S(1)} %get-tuple-element.69.refs_3_.refs_4_, ...), custom_call_target="tpu_custom_call" | custom-call | flops 1207959552 | bytes 6160432 | tf_op jit(solution)/shard_map/pallas_call | solution.py:325
  32.5 2.9 %shard_map.67 = (f32[2,384,128]{2,1,0:T(8,128)S(1)}, f32[2,256,128]{2,1,0:T(8,128)S(1)}, f32[2,128,128]{2,1,0:T(8,128)S(1)}, f32[2,384,128]{2,1,0:T(8,128)S(1)}, f32[2,6,128,128]{3,2,1,0:T(8,128)S(1)}) custom-call(s32[2,6]{1,0:T(2,128)S(1)} %bitcast.8, bf16[4,256,256]{2,1,0:T(8,128)(2,1)S(1)} %get-tuple-element.67.refs_1_, f32[6,128,128]{2,1,0:T(8,128)S(1)} %bitcast.4, ...), custom_call_target="tpu_custom_call" | custom-call | flops 1207959552 | bytes 6684720 | tf_op jit(solution)/shard_map/pallas_call | solution.py:325
  35.4 2.7 %shard_map.68 = (f32[2,384,128]{2,1,0:T(8,128)S(1)}, f32[2,256,128]{2,1,0:T(8,128)S(1)}, f32[2,128,128]{2,1,0:T(8,128)S(1)}, f32[2,384,128]{2,1,0:T(8,128)S(1)}, f32[2,6,128,128]{3,2,1,0:T(8,128)S(1)}) custom-call(s32[2,6]{1,0:T(2,128)S(1)} %bitcast.9, bf16[4,256,256]{2,1,0:T(8,128)(2,1)S(1)} %get-tuple-element.67.refs_1_, ...), custom_call_target="tpu_custom_call" | custom-call | flops 1207959552 | bytes 5636144 | tf_op jit(solution)/shard_map/pallas_call | solution.py:325
  38.1 2.6 %shard_map.69 = (f32[2,384,128]{2,1,0:T(8,128)S(1)}, f32[2,256,128]{2,1,0:T(8,128)S(1)}, f32[2,128,128]{2,1,0:T(8,128)S(1)}, f32[2,384,128]{2,1,0:T(8,128)S(1)}) custom-call(s32[2,6]{1,0:T(2,128)S(1)} %bitcast.10, bf16[4,256,256]{2,1,0:T(8,128)(2,1)S(1)} %get-tuple-element.67.refs_1_, f32[4,128,128]{2,1,0:T(8,128)S(1)} %get-tuple-element.68.refs_2_, ...), custom_call_target="tpu_custom_call" | custom-call | flops 1207959552 | bytes 3276848 | tf_op jit(solution)/shard_map/pallas_call | solution.py:325
  41.9 5.9 %collective-permute-start.13 = (f32[2,128,384]{2,1,0:T(8,128)S(1)}, f32[2,128,384]{2,1,0:T(8,128)S(1)}, u32[]{:S(2)}, u32[]{:S(2)}) collective-permute-start(f32[2,128,384]{2,1,0:T(8,128)S(1)} %get-tuple-element.92), channel_id=1, source_target_pairs={{0,248},{8,16},{16,8},{24,32},{32,24},{40,48},{48,40},{56,64},{64,... | collective-permute-start | bytes 1179656 | tf_op jit(solution)/shard_map/ppermute | solution.py:379
  48.0 4.9 %collective-permute-start.17 = (f32[2,128,384]{2,1,0:T(8,128)S(1)}, f32[2,128,384]{2,1,0:T(8,128)S(1)}, u32[]{:S(2)}, u32[]{:S(2)}) collective-permute-start(f32[2,128,384]{2,1,0:T(8,128)S(1)} %get-tuple-element.104), channel_id=1, source_target_pairs={{0,248},{8,16},{16,8},{24,32},{32,24},{40,48},{48,40},{56,64},{64,... | collective-permute-start | bytes 1179656 | tf_op jit(solution)/shard_map/ppermute | solution.py:379
  53.9 5.8 %collective-permute-start.11 = (f32[2,128,384]{2,1,0:T(8,128)S(1)}, f32[2,128,384]{2,1,0:T(8,128)S(1)}, u32[]{:S(2)}, u32[]{:S(2)}) collective-permute-start(f32[2,128,384]{2,1,0:T(8,128)S(1)} %get-tuple-element.82), channel_id=1, source_target_pairs={{0,248},{8,16},{16,8},{24,32},{32,24},{40,48},{48,40},{56,64},{64,... | collective-permute-start | bytes 1179656 | tf_op jit(solution)/shard_map/ppermute | solution.py:379
  62.3 3.9 %collective-permute-done.17.odd.refs_3_ = f32[2,128,384]{2,1,0:T(8,128)S(1)} collective-permute-done((f32[2,128,384]{2,1,0:T(8,128)S(1)}, f32[2,128,384]{2,1,0:T(8,128)S(1)}, u32[]{:S(2)}, u32[]{:S(2)}) %collective-permute-start.17) | collective-permute-done | bytes 393248 | tf_op jit(solution)/shard_map/ppermute | solution.py:379
  66.3 2.4 %collective-permute-start.19 = (f32[2,384,128]{2,1,0:T(8,128)S(1)}, f32[2,384,128]{2,1,0:T(8,128)S(1)}, u32[]{:S(2)}, u32[]{:S(2)}) collective-permute-start(f32[2,384,128]{2,1,0:T(8,128)S(1)} %get-tuple-element.105.left), channel_id=1, source_target_pairs={{1,0},{2,1},{3,2},{4,3},{5,4},{6,5},{7,6},{0,7},{9,8},{10,9},{11,1... | collective-permute-start | bytes 1179656 | tf_op jit(solution)/shard_map/ppermute | solution.py:371
  69.2 4.2 %collective-permute-done.11.refs_3_ = f32[2,128,384]{2,1,0:T(8,128)S(1)} collective-permute-done((f32[2,128,384]{2,1,0:T(8,128)S(1)}, f32[2,128,384]{2,1,0:T(8,128)S(1)}, u32[]{:S(2)}, u32[]{:S(2)}) %collective-permute-start.11) | collective-permute-done | bytes 393248 | tf_op jit(solution)/shard_map/ppermute | solution.py:379
  73.9 2.4 %shard_map.72 = (f32[2,6,128,128]{3,2,1,0:T(8,128)}, f32[2,6,128,128]{3,2,1,0:T(8,128)S(1)}) custom-call(s32[2,6]{1,0:T(2,128)S(1)} %bitcast.11, bf16[4,256,256]{2,1,0:T(8,128)(2,1)S(1)} %get-tuple-element.67.refs_1_, f32[4,128,128]{2,1,0:T(8,128)S(1)} %get-tuple-element.68.refs_2_, f32[2,384,128]{2,1,0:T(8,128)S(1)} %get-tuple-element.83.refs_3_.refs_0_, ...), custom_call_target="tpu_custom_call" | custom-call | flops 1207959552 | bytes 4063280 | tf_op jit(solution)/shard_map/pallas_call | solution.py:325
  76.3 2.4 %shard_map.76 = (f32[2,6,128,128]{3,2,1,0:T(8,128)S(1)}, f32[2,6,128,128]{3,2,1,0:T(8,128)S(1)}) custom-call(s32[2,6]{1,0:T(2,128)S(1)} %bitcast.12, bf16[4,256,256]{2,1,0:T(8,128)(2,1)S(1)} %get-tuple-element.67.refs_1_, f32[4,128,128]{2,1,0:T(8,128)S(1)} %get-tuple-element.68.refs_2_, f32[2,6,128,128]{3,2,1,0:T(8,128)S(1)} %get-tuple-element.86.refs_3_.refs_4_, ...), custom_call_target="tpu_custom_call" | custom-call | flops 1207959552 | bytes 4849712 | tf_op jit(solution)/shard_map/pallas_call | solution.py:325
  78.9 2.9 %shard_map.80 = (f32[2,384,128]{2,1,0:T(8,128)S(1)}, f32[2,256,128]{2,1,0:T(8,128)S(1)}, f32[2,128,128]{2,1,0:T(8,128)S(1)}, f32[2,384,128]{2,1,0:T(8,128)S(1)}, f32[2,6,128,128]{3,2,1,0:T(8,128)S(1)}) custom-call(s32[2,6]{1,0:T(2,128)S(1)} %bitcast.13, bf16[4,256,256]{2,1,0:T(8,128)(2,1)S(1)} %get-tuple-element.67.refs_1_, f32[6,128,128]{2,1,0:T(8,128)S(1)} %bitcast.5, ...), custom_call_target="tpu_custom_call" | custom-call | flops 1207959552 | bytes 5374000 | tf_op jit(solution)/shard_map/pallas_call | solution.py:325
  81.9 2.6 %shard_map.81 = (f32[2,384,128]{2,1,0:T(8,128)S(1)}, f32[2,256,128]{2,1,0:T(8,128)S(1)}, f32[2,128,128]{2,1,0:T(8,128)S(1)}, f32[2,384,128]{2,1,0:T(8,128)S(1)}, f32[2,6,128,128]{3,2,1,0:T(8,128)S(1)}) custom-call(s32[2,6]{1,0:T(2,128)S(1)} %bitcast.14, bf16[4,256,256]{2,1,0:T(8,128)(2,1)S(1)} %get-tuple-element.67.refs_1_, ...), custom_call_target="tpu_custom_call" | custom-call | flops 1207959552 | bytes 5636144 | tf_op jit(solution)/shard_map/pallas_call | solution.py:325
  84.6 2.6 %shard_map.82 = (f32[2,384,128]{2,1,0:T(8,128)S(1)}, f32[2,256,128]{2,1,0:T(8,128)S(1)}, f32[2,128,128]{2,1,0:T(8,128)S(1)}, f32[2,384,128]{2,1,0:T(8,128)S(1)}) custom-call(s32[2,6]{1,0:T(2,128)S(1)} %bitcast.15, bf16[4,256,256]{2,1,0:T(8,128)(2,1)S(1)} %get-tuple-element.67.refs_1_, f32[4,128,128]{2,1,0:T(8,128)S(1)} %get-tuple-element.68.refs_2_, ...), custom_call_target="tpu_custom_call" | custom-call | flops 1207959552 | bytes 3276848 | tf_op jit(solution)/shard_map/pallas_call | solution.py:325
  87.7 5.3 %collective-permute-done.24.refs_1_.refs_4_ = f32[2,384,128]{2,1,0:T(8,128)S(1)} collective-permute-done((f32[2,384,128]{2,1,0:T(8,128)S(1)}, f32[2,384,128]{2,1,0:T(8,128)S(1)}, u32[]{:S(2)}, u32[]{:S(2)}) %collective-permute-start.24) | collective-permute-done | bytes 393248 | tf_op jit(solution)/shard_map/ppermute | solution.py:371
  93.0 4.2 %collective-permute-done.26.refs_3_.refs_10_ = f32[2,384,128]{2,1,0:T(8,128)S(1)} collective-permute-done((f32[2,384,128]{2,1,0:T(8,128)S(1)}, f32[2,384,128]{2,1,0:T(8,128)S(1)}, u32[]{:S(2)}, u32[]{:S(2)}) %collective-permute-start.26) | collective-permute-done | bytes 393248 | tf_op jit(solution)/shard_map/ppermute | solution.py:371
  98.6 14.1 %collective-permute-done.25.refs_5_ = f32[2,128,128]{2,1,0:T(8,128)S(1)} collective-permute-done((f32[2,128,128]{2,1,0:T(8,128)S(1)}, f32[2,128,128]{2,1,0:T(8,128)S(1)}, u32[]{:S(2)}, u32[]{:S(2)}) %collective-permute-start.25) | collective-permute-done | bytes 131104 | tf_op jit(solution)/shard_map/ppermute | solution.py:371
  115.6 5.4 %collective-permute-done.23.refs_6_ = f32[1,2,128,128]{3,2,1,0:T(8,128)S(1)} collective-permute-done((f32[1,2,128,128]{3,2,1,0:T(8,128)S(1)}, f32[1,2,128,128]{3,2,1,0:T(8,128)S(1)}, u32[]{:S(2)}, u32[]{:S(2)}) %collective-permute-start.23) | collective-permute-done | bytes 131104 | tf_op jit(solution)/shard_map/ppermute | solution.py:371
  (78 shorter events, 17.5 us)
Async XLA Ops:
  1.5 28.5 %collective-permute-start.4 = (f32[2,2,256,128]{3,2,1,0:T(8,128)S(1)}, f32[2,2,256,128]{3,2,1,0:T(8,128)S(1)}, u32[]{:S(2)}, u32[]{:S(2)}) collective-permute-start(f32[2,2,256,128]{3,2,1,0:T(8,128)S(1)} %get-tuple-element.71), channel_id=1, source_target_pairs={{1,0},{2,1},{3,2},{4,3},{5,4},{6,5},{7,6},{0,7},{9,8},{10,9},{11,1... | collective-permute-start | bytes 1572872 | tf_op jit(solution)/shard_map/ppermute | solution.py:371
  2.1 15.1 %collective-permute-start = (f32[2,128,256]{2,1,0:T(8,128)S(1)}, f32[2,128,256]{2,1,0:T(8,128)S(1)}, u32[]{:S(2)}, u32[]{:S(2)}) collective-permute-start(f32[2,128,256]{2,1,0:T(8,128)S(1)} %get-tuple-element.65), channel_id=1, source_target_pairs={{8,0},{16,8},{24,16},{32,24},{40,32},{48,40},{56,48},{64,56},{72,6... | collective-permute-start | bytes 786440 | tf_op jit(solution)/shard_map/ppermute | solution.py:371
  10.5 12.3 %collective-permute-start.3 = (f32[2,128,256]{2,1,0:T(8,128)S(1)}, f32[2,128,256]{2,1,0:T(8,128)S(1)}, u32[]{:S(2)}, u32[]{:S(2)}) collective-permute-start(f32[2,128,256]{2,1,0:T(8,128)S(1)} %get-tuple-element.70), channel_id=1, source_target_pairs={{8,0},{16,8},{24,16},{32,24},{40,32},{48,40},{56,48},{64,56},{72,6... | collective-permute-start | bytes 786440 | tf_op jit(solution)/shard_map/ppermute | solution.py:371
  11.2 14.5 %collective-permute-start.6 = (f32[2,128,256]{2,1,0:T(8,128)S(1)}, f32[2,128,256]{2,1,0:T(8,128)S(1)}, u32[]{:S(2)}, u32[]{:S(2)}) collective-permute-start(f32[2,128,256]{2,1,0:T(8,128)S(1)} %get-tuple-element.73), channel_id=1, source_target_pairs={{8,0},{16,8},{24,16},{32,24},{40,32},{48,40},{56,48},{64,56},{72,6... | collective-permute-start | bytes 786440 | tf_op jit(solution)/shard_map/ppermute | solution.py:371
  11.7 15.9 %collective-permute-start.1 = (f32[2,256,128]{2,1,0:T(8,128)S(1)}, f32[2,256,128]{2,1,0:T(8,128)S(1)}, u32[]{:S(2)}, u32[]{:S(2)}) collective-permute-start(f32[2,256,128]{2,1,0:T(8,128)S(1)} %get-tuple-element.66), channel_id=1, source_target_pairs={{1,0},{2,1},{3,2},{4,3},{5,4},{6,5},{7,6},{0,7},{9,8},{10,9},{11,1... | collective-permute-start | bytes 786440 | tf_op jit(solution)/shard_map/ppermute | solution.py:371
  17.2 10.3 %collective-permute-start.2 = (f32[2,128,128]{2,1,0:T(8,128)S(1)}, f32[2,128,128]{2,1,0:T(8,128)S(1)}, u32[]{:S(2)}, u32[]{:S(2)}) collective-permute-start(f32[2,128,128]{2,1,0:T(8,128)S(1)} %slice.20), channel_id=1, source_target_pairs={{1,0},{2,1},{3,2},{4,3},{5,4},{6,5},{7,6},{0,7},{9,8},{10,9},{11,1... | collective-permute-start | bytes 393224 | tf_op jit(solution)/shard_map/ppermute | solution.py:371
  41.8 11.1 %collective-permute-start.8 = (f32[2,384,128]{2,1,0:T(8,128)S(1)}, f32[2,384,128]{2,1,0:T(8,128)S(1)}, u32[]{:S(2)}, u32[]{:S(2)}) collective-permute-start(f32[2,384,128]{2,1,0:T(8,128)S(1)} %get-tuple-element.80.right), channel_id=1, source_target_pairs={{7,0},{0,1},{1,2},{2,3},{3,4},{4,5},{5,6},{6,7},{15,8},{8,9},{9,10... | collective-permute-start | bytes 1179656 | tf_op jit(solution)/shard_map/ppermute | solution.py:371
  41.8 12.1 %collective-permute-start.12 = (f32[2,128,384]{2,1,0:T(8,128)S(1)}, f32[2,128,384]{2,1,0:T(8,128)S(1)}, u32[]{:S(2)}, u32[]{:S(2)}) collective-permute-start(f32[2,128,384]{2,1,0:T(8,128)S(1)} %get-tuple-element.91), channel_id=1, source_target_pairs={{0,8},{8,0},{16,24},{24,16},{32,40},{40,32},{48,56},{56,48},{64,72... | collective-permute-start | bytes 1179656 | tf_op jit(solution)/shard_map/ppermute | solution.py:379
  41.9 17.8 %collective-permute-start.13 = (f32[2,128,384]{2,1,0:T(8,128)S(1)}, f32[2,128,384]{2,1,0:T(8,128)S(1)}, u32[]{:S(2)}, u32[]{:S(2)}) collective-permute-start(f32[2,128,384]{2,1,0:T(8,128)S(1)} %get-tuple-element.92), channel_id=1, source_target_pairs={{0,248},{8,16},{16,8},{24,32},{32,24},{40,48},{48,40},{56,64},{64,... | collective-permute-start | bytes 1179656 | tf_op jit(solution)/shard_map/ppermute | solution.py:379
  47.9 14.4 %collective-permute-start.16 = (f32[2,128,384]{2,1,0:T(8,128)S(1)}, f32[2,128,384]{2,1,0:T(8,128)S(1)}, u32[]{:S(2)}, u32[]{:S(2)}) collective-permute-start(f32[2,128,384]{2,1,0:T(8,128)S(1)} %get-tuple-element.103), channel_id=1, source_target_pairs={{0,8},{8,0},{16,24},{24,16},{32,40},{40,32},{48,56},{56,48},{64,72... | collective-permute-start | bytes 1179656 | tf_op jit(solution)/shard_map/ppermute | solution.py:379
  48.0 18.2 %collective-permute-start.17 = (f32[2,128,384]{2,1,0:T(8,128)S(1)}, f32[2,128,384]{2,1,0:T(8,128)S(1)}, u32[]{:S(2)}, u32[]{:S(2)}) collective-permute-start(f32[2,128,384]{2,1,0:T(8,128)S(1)} %get-tuple-element.104), channel_id=1, source_target_pairs={{0,248},{8,16},{16,8},{24,32},{32,24},{40,48},{48,40},{56,64},{64,... | collective-permute-start | bytes 1179656 | tf_op jit(solution)/shard_map/ppermute | solution.py:379
  53.0 16.2 %collective-permute-start.10 = (f32[2,128,384]{2,1,0:T(8,128)S(1)}, f32[2,128,384]{2,1,0:T(8,128)S(1)}, u32[]{:S(2)}, u32[]{:S(2)}) collective-permute-start(f32[2,128,384]{2,1,0:T(8,128)S(1)} %get-tuple-element.81), channel_id=1, source_target_pairs={{0,8},{8,0},{16,24},{24,16},{32,40},{40,32},{48,56},{56,48},{64,72... | collective-permute-start | bytes 1179656 | tf_op jit(solution)/shard_map/ppermute | solution.py:379
  53.9 19.5 %collective-permute-start.11 = (f32[2,128,384]{2,1,0:T(8,128)S(1)}, f32[2,128,384]{2,1,0:T(8,128)S(1)}, u32[]{:S(2)}, u32[]{:S(2)}) collective-permute-start(f32[2,128,384]{2,1,0:T(8,128)S(1)} %get-tuple-element.82), channel_id=1, source_target_pairs={{0,248},{8,16},{16,8},{24,32},{32,24},{40,48},{48,40},{56,64},{64,... | collective-permute-start | bytes 1179656 | tf_op jit(solution)/shard_map/ppermute | solution.py:379
  59.8 13.8 %collective-permute-start.15 = (f32[2,384,128]{2,1,0:T(8,128)S(1)}, f32[2,384,128]{2,1,0:T(8,128)S(1)}, u32[]{:S(2)}, u32[]{:S(2)}) collective-permute-start(f32[2,384,128]{2,1,0:T(8,128)S(1)} %get-tuple-element.93.left), channel_id=1, source_target_pairs={{1,0},{2,1},{3,2},{4,3},{5,4},{6,5},{7,6},{0,7},{9,8},{10,9},{11,1... | collective-permute-start | bytes 1179656 | tf_op jit(solution)/shard_map/ppermute | solution.py:371
  62.3 11.3 %collective-permute-start.14 = (f32[2,384,128]{2,1,0:T(8,128)S(1)}, f32[2,384,128]{2,1,0:T(8,128)S(1)}, u32[]{:S(2)}, u32[]{:S(2)}) collective-permute-start(f32[2,384,128]{2,1,0:T(8,128)S(1)} %get-tuple-element.94.right), channel_id=1, source_target_pairs={{7,0},{0,1},{1,2},{2,3},{3,4},{4,5},{5,6},{6,7},{15,8},{8,9},{9,10... | collective-permute-start | bytes 1179656 | tf_op jit(solution)/shard_map/ppermute | solution.py:371
  66.3 12.4 %collective-permute-start.19 = (f32[2,384,128]{2,1,0:T(8,128)S(1)}, f32[2,384,128]{2,1,0:T(8,128)S(1)}, u32[]{:S(2)}, u32[]{:S(2)}) collective-permute-start(f32[2,384,128]{2,1,0:T(8,128)S(1)} %get-tuple-element.105.left), channel_id=1, source_target_pairs={{1,0},{2,1},{3,2},{4,3},{5,4},{6,5},{7,6},{0,7},{9,8},{10,9},{11,1... | collective-permute-start | bytes 1179656 | tf_op jit(solution)/shard_map/ppermute | solution.py:371
  69.2 9.6 %collective-permute-start.18 = (f32[2,384,128]{2,1,0:T(8,128)S(1)}, f32[2,384,128]{2,1,0:T(8,128)S(1)}, u32[]{:S(2)}, u32[]{:S(2)}) collective-permute-start(f32[2,384,128]{2,1,0:T(8,128)S(1)} %get-tuple-element.106.right), channel_id=1, source_target_pairs={{7,0},{0,1},{1,2},{2,3},{3,4},{4,5},{5,6},{6,7},{15,8},{8,9},{9,10... | collective-permute-start | bytes 1179656 | tf_op jit(solution)/shard_map/ppermute | solution.py:371
  84.6 12.6 %collective-permute-start.26 = (f32[2,384,128]{2,1,0:T(8,128)S(1)}, f32[2,384,128]{2,1,0:T(8,128)S(1)}, u32[]{:S(2)}, u32[]{:S(2)}) collective-permute-start(f32[2,384,128]{2,1,0:T(8,128)S(1)} %get-tuple-element.123), channel_id=1, source_target_pairs={{7,0},{0,1},{1,2},{2,3},{3,4},{4,5},{5,6},{6,7},{15,8},{8,9},{9,10... | collective-permute-start | bytes 1179656 | tf_op jit(solution)/shard_map/ppermute | solution.py:371
  87.2 11.4 %collective-permute-start.22 = (f32[2,128,128]{2,1,0:T(8,128)S(1)}, f32[2,128,128]{2,1,0:T(8,128)S(1)}, u32[]{:S(2)}, u32[]{:S(2)}) collective-permute-start(f32[2,128,128]{2,1,0:T(8,128)S(1)} %slice.19), channel_id=1, source_target_pairs={{7,0},{0,1},{1,2},{2,3},{3,4},{4,5},{5,6},{6,7},{15,8},{8,9},{9,10... | collective-permute-start | bytes 393224 | tf_op jit(solution)/shard_map/ppermute | solution.py:371
  97.2 17.0 %collective-permute-start.28 = (f32[2,2,128,128]{3,2,1,0:T(8,128)S(1)}, f32[2,2,128,128]{3,2,1,0:T(8,128)S(1)}, u32[]{:S(2)}, u32[]{:S(2)}) collective-permute-start(f32[2,2,128,128]{3,2,1,0:T(8,128)S(1)} %shard_map.84), channel_id=1, source_target_pairs={{248,0},{0,8},{8,16},{16,24},{24,32},{32,40},{40,48},{48,56},{56,6... | collective-permute-start | bytes 786440 | tf_op jit(solution)/shard_map/ppermute | solution.py:371
  97.6 15.1 %collective-permute-start.25 = (f32[2,128,128]{2,1,0:T(8,128)S(1)}, f32[2,128,128]{2,1,0:T(8,128)S(1)}, u32[]{:S(2)}, u32[]{:S(2)}) collective-permute-start(f32[2,128,128]{2,1,0:T(8,128)S(1)} %get-tuple-element.120), channel_id=1, source_target_pairs={{248,0},{0,8},{8,16},{16,24},{24,32},{32,40},{40,48},{48,56},{56,6... | collective-permute-start | bytes 393224 | tf_op jit(solution)/shard_map/ppermute | solution.py:371
  97.7 23.3 %collective-permute-start.20 = (f32[2,256,128]{2,1,0:T(8,128)S(1)}, f32[2,256,128]{2,1,0:T(8,128)S(1)}, u32[]{:S(2)}, u32[]{:S(2)}) collective-permute-start(f32[2,256,128]{2,1,0:T(8,128)S(1)} %slice.18), channel_id=1, source_target_pairs={{7,0},{0,1},{1,2},{2,3},{3,4},{4,5},{5,6},{6,7},{15,8},{8,9},{9,10... | collective-permute-start | bytes 786440 | tf_op jit(solution)/shard_map/ppermute | solution.py:371
  97.7 16.5 %collective-permute-start.27 = (f32[2,128,128]{2,1,0:T(8,128)S(1)}, f32[2,128,128]{2,1,0:T(8,128)S(1)}, u32[]{:S(2)}, u32[]{:S(2)}) collective-permute-start(f32[2,128,128]{2,1,0:T(8,128)S(1)} %get-tuple-element.124), channel_id=1, source_target_pairs={{248,0},{0,8},{8,16},{16,24},{24,32},{32,40},{40,48},{48,56},{56,6... | collective-permute-start | bytes 393224 | tf_op jit(solution)/shard_map/ppermute | solution.py:371
  98.6 17.0 %collective-permute-start.21 = (f32[2,128,128]{2,1,0:T(8,128)S(1)}, f32[2,128,128]{2,1,0:T(8,128)S(1)}, u32[]{:S(2)}, u32[]{:S(2)}) collective-permute-start(f32[2,128,128]{2,1,0:T(8,128)S(1)} %get-tuple-element.116), channel_id=1, source_target_pairs={{248,0},{0,8},{8,16},{16,24},{24,32},{32,40},{40,48},{48,56},{56,6... | collective-permute-start | bytes 393224 | tf_op jit(solution)/shard_map/ppermute | solution.py:371
  (12 other events, 158.2 us)

commit v5 on v4

--- a/solution.py
+++ b/solution.py
@@ -160,10 +160,11 @@
 
 
 def fill_first(ext, refs):
-    tile, low, right, corner = refs
-    t = TILE
+    tile, low_left, low_right, right, corner = refs
+    t, h = TILE, PROBE
     ext[:, :t, :t] = tile[:, 0]
-    ext[:, t:, :t] = low[...]
+    ext[:, t:, :h] = low_left[...]
+    ext[:, t:, h:t] = low_right[...]
     ext[:, :t, t:] = right[...]
     ext[:, t:, t:] = corner[...]
 
@@ -337,10 +338,14 @@
 def field_specs(start, layer, fill):
     if fill is not fill_first:
         return {}
-    specs = {start: tile_of(layer)}
-    if layer > 0:
-        specs[start + 2] = pl.BlockSpec((2, None, TILE, PROBE), lambda i: (0, layer - 1, 0, 0))
-    return specs
+    h, t = PROBE, TILE
+    if layer == 0:
+        lows = [pl.BlockSpec((2, h, h), lambda i: (0, 0, 0)), pl.BlockSpec((2, h, h), lambda i: (0, 0, 1))]
+        sides = [None, None]
+    else:
+        low = pl.BlockSpec((2, None, h, h), lambda i: (0, layer - 1, 0, 0))
+        lows, sides = [low, low], [pl.BlockSpec((2, None, t, h), lambda i: (0, layer - 1, 0, 0)), low]
+    return {start + n: spec for n, spec in enumerate([tile_of(layer), *lows, *sides])}
 
 
 def forward(offsets, tables, phase, wave, field, layer, fill):
@@ -490,7 +495,7 @@
         out[:, t:] = own[:, t:] + below[:, :, cols]
 
 
-def update_kernel(rows_first, tile, low, side, corner, left, middle, bottom, right, *refs):
+def update_kernel(rows_first, tile, low_left, low_right, side, corner, left, middle, bottom, right, *refs):
     from_left, from_right, even, odd, new_l, new_m, new_r = refs
     h, t = PROBE, TILE
     above, below = Chosen(odd, even), Chosen(even, odd)
@@ -505,10 +510,10 @@
 
     new_l[:, top] = tile[:, 0, top, first] - STEP * side_sum(left, from_left, top, first)
     new_l[:, mid] = tile[:, 0, mid, first] - STEP * side_sum(left, from_left, mid, first)
-    new_l[:, end] = low[:, :, first] - STEP * side_sum(left, from_left, end, first)
+    new_l[:, end] = low_left[...] - STEP * side_sum(left, from_left, end, first)
     new_m[:, top] = tile[:, 0, top, second] - STEP * (middle[:, top] + above[:, :, second])
     new_m[:, mid] = tile[:, 0, mid, second] - STEP * middle[:, mid]
-    new_m[:, end] = low[:, :, second] - STEP * (bottom[...] + below[:, :, second])
+    new_m[:, end] = low_right[...] - STEP * (bottom[...] + below[:, :, second])
     new_r[:, top] = side[:, top] - STEP * side_sum(right, from_right, top, third)
     new_r[:, mid] = side[:, mid] - STEP * side_sum(right, from_right, mid, third)
     new_r[:, end] = corner[...] - STEP * side_sum(right, from_right, end, third)
@@ -568,23 +573,25 @@
     offsets = jnp.swapaxes(offsets, 2, 3).reshape(2, POS)
     intensity = measured.reshape(POS, h, h)
 
-    top, all_rows, left, all_cols = pl.ds(0, h), pl.ds(0, t), pl.ds(0, h), pl.ds(0, t)
-    rows_shape = shape(2, h, t)
-    rows0, cols0 = pack(
-        object_field, [(0, top, all_cols), (0, all_rows, left)], [rows_shape, shape(2, t, h)]
+    top, all_rows, west_half, east_half, rest = pl.ds(0, h), pl.ds(0, t), pl.ds(0, h), pl.ds(h, h), pl.ds(1, 2)
+    rows0 = object_field[:, 0, :h]
+    cols0, west_rows, east_rows, cols12 = pack(
+        object_field,
+        [(0, all_rows, west_half), (rest, top, west_half), (rest, top, east_half), (rest, all_rows, west_half)],
+        [shape(2, t, h), shape(2, 2, h, h), shape(2, 2, h, h), shape(2, 2, t, h)],
     )
-    rows1, rows2, cols12 = pack(
-        object_field,
-        [(1, top, all_cols), (2, top, all_cols), (pl.ds(1, 2), all_rows, left)],
-        [rows_shape, rows_shape, shape(2, 2, t, h)],
-    )
+    low0 = shifted(rows0, "row", -1)
+    low_west = shifted(west_rows, "row", -1)
+    low_east = shifted(east_rows, "row", -1)
     right0 = shifted(cols0, "col", -1)
     right12 = shifted(cols12, "col", -1)
-    fields = []
-    for layer, rows in enumerate((rows0, rows1, rows2)):
-        low = shifted(rows, "row", -1)
-        corner = shifted(low[:, :, :h], "col", -1)
-        fields.append([object_field, low, right0 if layer == 0 else right12, corner])
+    corner0 = shifted(low0[:, :, :h], "col", -1)
+    corner12 = shifted(low_west, "col", -1)
+    fields = [
+        [object_field, low0, low0, right0, corner0],
+        [object_field, low_west, low_east, right12, corner12],
+        [object_field, low_west, low_east, right12, corner12],
+    ]
 
     def gradients(fields, fill):
         _, wave1 = forward(offsets, tables, phase, None, fields[0], 0, fill)

time: 122 us -> 121 us (level)
  waiting for transfers between devices: 54.9 us -> 53.3 us
    ppermute x23 -> x22, waiting for transfers between devices: 44.9 us -> 42.1 us  [shifted(): lax.ppermute(block, axis, [((i - distance) % size, i) for i in range(size)])]
    ppermute x23 -> x22, starting transfers between devices: 18.3 us -> 19.4 us  [shifted(): lax.ppermute(block, axis, [((i - distance) % size, i) for i in range(size)])]
  transfers between devices with their start and end apart: 29 -> 28, of which waited for: 15 -> 15; matrix products, arithmetic and copies ran while one was open for 0% -> 0% of each run, Pallas kernels for 12% -> 10%
where the time goes in v5:
time: 121 us
  waiting for transfers between devices  53.3 us (44%)
  starting transfers between devices  35.7 us (30%)
  Pallas kernels  29.9 us (25%)
  local copies, waits for them, and re-layouts  1.49 us (1%)
    ppermute x22, waiting for transfers between devices, shifted(): lax.ppermute(block, axis, [((i - distance) % size, i) for i in range(size)])  42.1 us
    pallas_call x10, Pallas kernels, run(): pl.pallas_call(body, grid=(1,), in_specs=in_specs, out_specs=[whole(o) fo...  26 us
    ppermute x22, starting transfers between devices, shifted(): lax.ppermute(block, axis, [((i - distance) % size, i) for i in range(size)])  19.4 us
    ppermute x6, starting transfers between devices, swapped(): return lax.ppermute(block, 'row', sorted(route))  16.2 us
    ppermute x6, waiting for transfers between devices, swapped(): return lax.ppermute(block, 'row', sorted(route))  11.2 us
    pallas_call x13, Pallas kernels, plain(): pl.pallas_call(body, grid=(1,), in_specs=[specs.get(n, None) or whole(o)...  3.77 us
  transfers between devices with their start and end apart: 28, of which 15 were waited for; matrix products, arithmetic and copies ran while one was open for 0% of the time, Pallas kernels for 10%

profile of v5, /device:TPU:0, one launch (start us, length us, event | category | flops | bytes accessed | tf_op | source)
XLA Modules:
  0.0 120.7 jit_solution(12324912536011447696)
XLA Ops:
  1.6 6.7 %collective-permute-start.3 = (f32[2,2,128,128]{3,2,1,0:T(8,128)S(1)}, f32[2,2,128,128]{3,2,1,0:T(8,128)S(1)}, u32[]{:S(2)}, u32[]{:S(2)}) collective-permute-start(f32[2,2,128,128]{3,2,1,0:T(8,128)S(1)} %get-tuple-element.68), channel_id=1, source_target_pairs={{8,0},{16,8},{24,16},{32,24},{40,32},{48,40},{56,48},{64,56},{72,6... | collective-permute-start | bytes 786440 | tf_op jit(solution)/shard_map/ppermute | solution.py:376
  12.2 2.8 %collective-permute-done.3.refs_5_.low_left = f32[2,2,128,128]{3,2,1,0:T(8,128)S(1)} collective-permute-done((f32[2,2,128,128]{3,2,1,0:T(8,128)S(1)}, f32[2,2,128,128]{3,2,1,0:T(8,128)S(1)}, u32[]{:S(2)}, u32[]{:S(2)}) %collective-permute-start.3) | collective-permute-done | bytes 262176 | tf_op jit(solution)/shard_map/ppermute | solution.py:376
  15.2 5.4 %collective-permute-done.refs_4_.refs_5_.low_left.low_right = f32[2,128,256]{2,1,0:T(8,128)S(1)} collective-permute-done((f32[2,128,256]{2,1,0:T(8,128)S(1)}, f32[2,128,256]{2,1,0:T(8,128)S(1)}, u32[]{:S(2)}, u32[]{:S(2)}) %collective-permute-start) | collective-permute-done | bytes 262176 | tf_op jit(solution)/shard_map/ppermute | solution.py:376
  21.3 2.6 %collective-permute-done.2.refs_7_.corner = f32[2,128,128]{2,1,0:T(8,128)S(1)} collective-permute-done((f32[2,128,128]{2,1,0:T(8,128)S(1)}, f32[2,128,128]{2,1,0:T(8,128)S(1)}, u32[]{:S(2)}, u32[]{:S(2)}) %collective-permute-start.2) | collective-permute-done | bytes 131104 | tf_op jit(solution)/shard_map/ppermute | solution.py:376
  23.9 2.4 %shard_map.65 = (f32[2,6,128,128]{3,2,1,0:T(8,128)}, f32[2,6,128,128]{3,2,1,0:T(8,128)S(1)}) custom-call(s32[2,6]{1,0:T(2,128)S(1)} %bitcast.10, bf16[4,256,256]{2,1,0:T(8,128)(2,1)S(1)} %get-tuple-element.65.refs_1_, f32[4,128,128]{2,1,0:T(8,128)S(1)} %get-tuple-element.66.refs_2_, f32[2,3,256,256]{3,2,1,0:T(8,128)S(1)} %copy-done.1, ...), custom_call_target="tpu_custom_call" | custom-call | flops 1207959552 | bytes 5374000 | tf_op jit(solution)/shard_map/pallas_call | solution.py:326
  26.4 2.4 %shard_map.66 = (f32[2,6,128,128]{3,2,1,0:T(8,128)S(1)}, f32[2,6,128,128]{3,2,1,0:T(8,128)S(1)}) custom-call(s32[2,6]{1,0:T(2,128)S(1)} %bitcast.11, bf16[4,256,256]{2,1,0:T(8,128)(2,1)S(1)} %get-tuple-element.65.refs_1_, f32[4,128,128]{2,1,0:T(8,128)S(1)} %get-tuple-element.66.refs_2_, f32[2,6,128,128]{3,2,1,0:T(8,128)S(1)} %get-tuple-element.67.refs_3_.refs_4_, ...), custom_call_target="tpu_custom_call" | custom-call | flops 1207959552 | bytes 6553648 | tf_op jit(solution)/shard_map/pallas_call | solution.py:326
  28.8 2.9 %shard_map.67 = (f32[2,384,128]{2,1,0:T(8,128)S(1)}, f32[2,256,128]{2,1,0:T(8,128)S(1)}, f32[2,128,128]{2,1,0:T(8,128)S(1)}, f32[2,384,128]{2,1,0:T(8,128)S(1)}, f32[2,6,128,128]{3,2,1,0:T(8,128)S(1)}) custom-call(s32[2,6]{1,0:T(2,128)S(1)} %bitcast.12, bf16[4,256,256]{2,1,0:T(8,128)(2,1)S(1)} %get-tuple-element.65.refs_1_, f32[6,128,128]{2,1,0:T(8,128)S(1)} %bitcast.8, ...), custom_call_target="tpu_custom_call" | custom-call | flops 1207959552 | bytes 7077936 | tf_op jit(solution)/shard_map/pallas_call | solution.py:326
  31.8 2.6 %shard_map.68 = (f32[2,384,128]{2,1,0:T(8,128)S(1)}, f32[2,256,128]{2,1,0:T(8,128)S(1)}, f32[2,128,128]{2,1,0:T(8,128)S(1)}, f32[2,384,128]{2,1,0:T(8,128)S(1)}, f32[2,6,128,128]{3,2,1,0:T(8,128)S(1)}) custom-call(s32[2,6]{1,0:T(2,128)S(1)} %bitcast.13, bf16[4,256,256]{2,1,0:T(8,128)(2,1)S(1)} %get-tuple-element.65.refs_1_, ...), custom_call_target="tpu_custom_call" | custom-call | flops 1207959552 | bytes 5636144 | tf_op jit(solution)/shard_map/pallas_call | solution.py:326
  34.4 2.6 %shard_map.69 = (f32[2,384,128]{2,1,0:T(8,128)S(1)}, f32[2,256,128]{2,1,0:T(8,128)S(1)}, f32[2,128,128]{2,1,0:T(8,128)S(1)}, f32[2,384,128]{2,1,0:T(8,128)S(1)}) custom-call(s32[2,6]{1,0:T(2,128)S(1)} %bitcast.14, bf16[4,256,256]{2,1,0:T(8,128)(2,1)S(1)} %get-tuple-element.65.refs_1_, f32[4,128,128]{2,1,0:T(8,128)S(1)} %get-tuple-element.66.refs_2_, ...), custom_call_target="tpu_custom_call" | custom-call | flops 1207959552 | bytes 3276848 | tf_op jit(solution)/shard_map/pallas_call | solution.py:326
  37.0 3.1 %collective-permute-start.8 = (f32[2,384,128]{2,1,0:T(8,128)S(1)}, f32[2,384,128]{2,1,0:T(8,128)S(1)}, u32[]{:S(2)}, u32[]{:S(2)}) collective-permute-start(f32[2,384,128]{2,1,0:T(8,128)S(1)} %get-tuple-element.75.left), channel_id=1, source_target_pairs={{1,0},{2,1},{3,2},{4,3},{5,4},{6,5},{7,6},{0,7},{9,8},{10,9},{11,1... | collective-permute-start | bytes 1179656 | tf_op jit(solution)/shard_map/ppermute | solution.py:376
  40.3 5.6 %collective-permute-start.12 = (f32[2,128,384]{2,1,0:T(8,128)S(1)}, f32[2,128,384]{2,1,0:T(8,128)S(1)}, u32[]{:S(2)}, u32[]{:S(2)}) collective-permute-start(f32[2,128,384]{2,1,0:T(8,128)S(1)} %get-tuple-element.90), channel_id=1, source_target_pairs={{0,248},{8,16},{16,8},{24,32},{32,24},{40,48},{48,40},{56,64},{64,... | collective-permute-start | bytes 1179656 | tf_op jit(solution)/shard_map/ppermute | solution.py:384
  46.1 4.9 %collective-permute-start.16 = (f32[2,128,384]{2,1,0:T(8,128)S(1)}, f32[2,128,384]{2,1,0:T(8,128)S(1)}, u32[]{:S(2)}, u32[]{:S(2)}) collective-permute-start(f32[2,128,384]{2,1,0:T(8,128)S(1)} %get-tuple-element.102), channel_id=1, source_target_pairs={{0,248},{8,16},{16,8},{24,32},{32,24},{40,48},{48,40},{56,64},{64,... | collective-permute-start | bytes 1179656 | tf_op jit(solution)/shard_map/ppermute | solution.py:384
  52.3 5.5 %collective-permute-start.10 = (f32[2,128,384]{2,1,0:T(8,128)S(1)}, f32[2,128,384]{2,1,0:T(8,128)S(1)}, u32[]{:S(2)}, u32[]{:S(2)}) collective-permute-start(f32[2,128,384]{2,1,0:T(8,128)S(1)} %get-tuple-element.80), channel_id=1, source_target_pairs={{0,248},{8,16},{16,8},{24,32},{32,24},{40,48},{48,40},{56,64},{64,... | collective-permute-start | bytes 1179656 | tf_op jit(solution)/shard_map/ppermute | solution.py:384
  60.7 3.6 %collective-permute-done.16.odd.refs_3_ = f32[2,128,384]{2,1,0:T(8,128)S(1)} collective-permute-done((f32[2,128,384]{2,1,0:T(8,128)S(1)}, f32[2,128,384]{2,1,0:T(8,128)S(1)}, u32[]{:S(2)}, u32[]{:S(2)}) %collective-permute-start.16) | collective-permute-done | bytes 393248 | tf_op jit(solution)/shard_map/ppermute | solution.py:384
  67.8 4.5 %collective-permute-done.10.refs_3_ = f32[2,128,384]{2,1,0:T(8,128)S(1)} collective-permute-done((f32[2,128,384]{2,1,0:T(8,128)S(1)}, f32[2,128,384]{2,1,0:T(8,128)S(1)}, u32[]{:S(2)}, u32[]{:S(2)}) %collective-permute-start.10) | collective-permute-done | bytes 393248 | tf_op jit(solution)/shard_map/ppermute | solution.py:384
  72.7 2.4 %shard_map.72 = (f32[2,6,128,128]{3,2,1,0:T(8,128)}, f32[2,6,128,128]{3,2,1,0:T(8,128)S(1)}) custom-call(s32[2,6]{1,0:T(2,128)S(1)} %bitcast.15, bf16[4,256,256]{2,1,0:T(8,128)(2,1)S(1)} %get-tuple-element.65.refs_1_, f32[4,128,128]{2,1,0:T(8,128)S(1)} %get-tuple-element.66.refs_2_, f32[2,384,128]{2,1,0:T(8,128)S(1)} %get-tuple-element.81.refs_3_.refs_0_, ...), custom_call_target="tpu_custom_call" | custom-call | flops 1207959552 | bytes 4063280 | tf_op jit(solution)/shard_map/pallas_call | solution.py:326
  75.2 2.4 %shard_map.76 = (f32[2,6,128,128]{3,2,1,0:T(8,128)S(1)}, f32[2,6,128,128]{3,2,1,0:T(8,128)S(1)}) custom-call(s32[2,6]{1,0:T(2,128)S(1)} %bitcast.16, bf16[4,256,256]{2,1,0:T(8,128)(2,1)S(1)} %get-tuple-element.65.refs_1_, f32[4,128,128]{2,1,0:T(8,128)S(1)} %get-tuple-element.66.refs_2_, f32[2,6,128,128]{3,2,1,0:T(8,128)S(1)} %get-tuple-element.84.refs_3_.refs_4_, ...), custom_call_target="tpu_custom_call" | custom-call | flops 1207959552 | bytes 4849712 | tf_op jit(solution)/shard_map/pallas_call | solution.py:326
  77.8 2.9 %shard_map.80 = (f32[2,384,128]{2,1,0:T(8,128)S(1)}, f32[2,256,128]{2,1,0:T(8,128)S(1)}, f32[2,128,128]{2,1,0:T(8,128)S(1)}, f32[2,384,128]{2,1,0:T(8,128)S(1)}, f32[2,6,128,128]{3,2,1,0:T(8,128)S(1)}) custom-call(s32[2,6]{1,0:T(2,128)S(1)} %bitcast.17, bf16[4,256,256]{2,1,0:T(8,128)(2,1)S(1)} %get-tuple-element.65.refs_1_, f32[6,128,128]{2,1,0:T(8,128)S(1)} %bitcast.9, ...), custom_call_target="tpu_custom_call" | custom-call | flops 1207959552 | bytes 5374000 | tf_op jit(solution)/shard_map/pallas_call | solution.py:326
  80.7 2.6 %shard_map.81 = (f32[2,384,128]{2,1,0:T(8,128)S(1)}, f32[2,256,128]{2,1,0:T(8,128)S(1)}, f32[2,128,128]{2,1,0:T(8,128)S(1)}, f32[2,384,128]{2,1,0:T(8,128)S(1)}, f32[2,6,128,128]{3,2,1,0:T(8,128)S(1)}) custom-call(s32[2,6]{1,0:T(2,128)S(1)} %bitcast.18, bf16[4,256,256]{2,1,0:T(8,128)(2,1)S(1)} %get-tuple-element.65.refs_1_, ...), custom_call_target="tpu_custom_call" | custom-call | flops 1207959552 | bytes 5636144 | tf_op jit(solution)/shard_map/pallas_call | solution.py:326
  83.4 2.6 %shard_map.82 = (f32[2,384,128]{2,1,0:T(8,128)S(1)}, f32[2,256,128]{2,1,0:T(8,128)S(1)}, f32[2,128,128]{2,1,0:T(8,128)S(1)}, f32[2,384,128]{2,1,0:T(8,128)S(1)}) custom-call(s32[2,6]{1,0:T(2,128)S(1)} %bitcast.19, bf16[4,256,256]{2,1,0:T(8,128)(2,1)S(1)} %get-tuple-element.65.refs_1_, f32[4,128,128]{2,1,0:T(8,128)S(1)} %get-tuple-element.66.refs_2_, ...), custom_call_target="tpu_custom_call" | custom-call | flops 1207959552 | bytes 3276848 | tf_op jit(solution)/shard_map/pallas_call | solution.py:326
  86.5 5.3 %collective-permute-done.23.refs_1_.refs_4_ = f32[2,384,128]{2,1,0:T(8,128)S(1)} collective-permute-done((f32[2,384,128]{2,1,0:T(8,128)S(1)}, f32[2,384,128]{2,1,0:T(8,128)S(1)}, u32[]{:S(2)}, u32[]{:S(2)}) %collective-permute-start.23) | collective-permute-done | bytes 393248 | tf_op jit(solution)/shard_map/ppermute | solution.py:376
  91.8 4.2 %collective-permute-done.25.refs_3_.refs_10_ = f32[2,384,128]{2,1,0:T(8,128)S(1)} collective-permute-done((f32[2,384,128]{2,1,0:T(8,128)S(1)}, f32[2,384,128]{2,1,0:T(8,128)S(1)}, u32[]{:S(2)}, u32[]{:S(2)}) %collective-permute-start.25) | collective-permute-done | bytes 393248 | tf_op jit(solution)/shard_map/ppermute | solution.py:376
  97.4 14.1 %collective-permute-done.24.refs_5_ = f32[2,128,128]{2,1,0:T(8,128)S(1)} collective-permute-done((f32[2,128,128]{2,1,0:T(8,128)S(1)}, f32[2,128,128]{2,1,0:T(8,128)S(1)}, u32[]{:S(2)}, u32[]{:S(2)}) %collective-permute-start.24) | collective-permute-done | bytes 131104 | tf_op jit(solution)/shard_map/ppermute | solution.py:376
  114.4 5.4 %collective-permute-done.22.refs_6_ = f32[1,2,128,128]{3,2,1,0:T(8,128)S(1)} collective-permute-done((f32[1,2,128,128]{3,2,1,0:T(8,128)S(1)}, f32[1,2,128,128]{3,2,1,0:T(8,128)S(1)}, u32[]{:S(2)}, u32[]{:S(2)}) %collective-permute-start.22) | collective-permute-done | bytes 131104 | tf_op jit(solution)/shard_map/ppermute | solution.py:376
  (74 shorter events, 20.8 us)
Async XLA Ops:
  1.6 13.4 %collective-permute-start.3 = (f32[2,2,128,128]{3,2,1,0:T(8,128)S(1)}, f32[2,2,128,128]{3,2,1,0:T(8,128)S(1)}, u32[]{:S(2)}, u32[]{:S(2)}) collective-permute-start(f32[2,2,128,128]{3,2,1,0:T(8,128)S(1)} %get-tuple-element.68), channel_id=1, source_target_pairs={{8,0},{16,8},{24,16},{32,24},{40,32},{48,40},{56,48},{64,56},{72,6... | collective-permute-start | bytes 786440 | tf_op jit(solution)/shard_map/ppermute | solution.py:376
  8.2 18.1 %collective-permute-start.5 = (f32[2,2,256,128]{3,2,1,0:T(8,128)S(1)}, f32[2,2,256,128]{3,2,1,0:T(8,128)S(1)}, u32[]{:S(2)}, u32[]{:S(2)}) collective-permute-start(f32[2,2,256,128]{3,2,1,0:T(8,128)S(1)} %get-tuple-element.70), channel_id=1, source_target_pairs={{1,0},{2,1},{3,2},{4,3},{5,4},{6,5},{7,6},{0,7},{9,8},{10,9},{11,1... | collective-permute-start | bytes 1572872 | tf_op jit(solution)/shard_map/ppermute | solution.py:376
  10.2 10.4 %collective-permute-start = (f32[2,128,256]{2,1,0:T(8,128)S(1)}, f32[2,128,256]{2,1,0:T(8,128)S(1)}, u32[]{:S(2)}, u32[]{:S(2)}) collective-permute-start(f32[2,128,256]{2,1,0:T(8,128)S(1)} %slice_bitcast_fusion), channel_id=1, source_target_pairs={{8,0},{16,8},{24,16},{32,24},{40,32},{48,40},{56,48},{64,56},{72,6... | collective-permute-start | bytes 786440 | tf_op jit(solution)/shard_map/ppermute | solution.py:376
  11.0 10.3 %collective-permute-start.1 = (f32[2,256,128]{2,1,0:T(8,128)S(1)}, f32[2,256,128]{2,1,0:T(8,128)S(1)}, u32[]{:S(2)}, u32[]{:S(2)}) collective-permute-start(f32[2,256,128]{2,1,0:T(8,128)S(1)} %get-tuple-element.64), channel_id=1, source_target_pairs={{1,0},{2,1},{3,2},{4,3},{5,4},{6,5},{7,6},{0,7},{9,8},{10,9},{11,1... | collective-permute-start | bytes 786440 | tf_op jit(solution)/shard_map/ppermute | solution.py:376
  11.7 14.7 %collective-permute-start.4 = (f32[2,2,128,128]{3,2,1,0:T(8,128)S(1)}, f32[2,2,128,128]{3,2,1,0:T(8,128)S(1)}, u32[]{:S(2)}, u32[]{:S(2)}) collective-permute-start(f32[2,2,128,128]{3,2,1,0:T(8,128)S(1)} %get-tuple-element.69), channel_id=1, source_target_pairs={{8,0},{16,8},{24,16},{32,24},{40,32},{48,40},{56,48},{64,56},{72,6... | collective-permute-start | bytes 786440 | tf_op jit(solution)/shard_map/ppermute | solution.py:376
  14.9 11.4 %collective-permute-start.6 = (f32[2,2,128,128]{3,2,1,0:T(8,128)S(1)}, f32[2,2,128,128]{3,2,1,0:T(8,128)S(1)}, u32[]{:S(2)}, u32[]{:S(2)}) collective-permute-start(f32[2,2,128,128]{3,2,1,0:T(8,128)S(1)} %collective-permute-done.3.refs_5_.low_left), channel_id=1, source_target_pairs={{1,0},{2,1},{3,2},{4,3},{5,4},{6,5},{7,6},{0,7},{9,8},{10,9},{11,1... | collective-permute-start | bytes 786440 | tf_op jit(solution)/shard_map/ppermute | solution.py:376
  40.1 10.8 %collective-permute-start.7 = (f32[2,384,128]{2,1,0:T(8,128)S(1)}, f32[2,384,128]{2,1,0:T(8,128)S(1)}, u32[]{:S(2)}, u32[]{:S(2)}) collective-permute-start(f32[2,384,128]{2,1,0:T(8,128)S(1)} %get-tuple-element.78.right), channel_id=1, source_target_pairs={{7,0},{0,1},{1,2},{2,3},{3,4},{4,5},{5,6},{6,7},{15,8},{8,9},{9,10... | collective-permute-start | bytes 1179656 | tf_op jit(solution)/shard_map/ppermute | solution.py:376
  40.2 12.1 %collective-permute-start.11 = (f32[2,128,384]{2,1,0:T(8,128)S(1)}, f32[2,128,384]{2,1,0:T(8,128)S(1)}, u32[]{:S(2)}, u32[]{:S(2)}) collective-permute-start(f32[2,128,384]{2,1,0:T(8,128)S(1)} %get-tuple-element.89), channel_id=1, source_target_pairs={{0,8},{8,0},{16,24},{24,16},{32,40},{40,32},{48,56},{56,48},{64,72... | collective-permute-start | bytes 1179656 | tf_op jit(solution)/shard_map/ppermute | solution.py:384
  40.3 17.5 %collective-permute-start.12 = (f32[2,128,384]{2,1,0:T(8,128)S(1)}, f32[2,128,384]{2,1,0:T(8,128)S(1)}, u32[]{:S(2)}, u32[]{:S(2)}) collective-permute-start(f32[2,128,384]{2,1,0:T(8,128)S(1)} %get-tuple-element.90), channel_id=1, source_target_pairs={{0,248},{8,16},{16,8},{24,32},{32,24},{40,48},{48,40},{56,64},{64,... | collective-permute-start | bytes 1179656 | tf_op jit(solution)/shard_map/ppermute | solution.py:384
  45.9 14.8 %collective-permute-start.15 = (f32[2,128,384]{2,1,0:T(8,128)S(1)}, f32[2,128,384]{2,1,0:T(8,128)S(1)}, u32[]{:S(2)}, u32[]{:S(2)}) collective-permute-start(f32[2,128,384]{2,1,0:T(8,128)S(1)} %get-tuple-element.101), channel_id=1, source_target_pairs={{0,8},{8,0},{16,24},{24,16},{32,40},{40,32},{48,56},{56,48},{64,72... | collective-permute-start | bytes 1179656 | tf_op jit(solution)/shard_map/ppermute | solution.py:384
  46.1 18.2 %collective-permute-start.16 = (f32[2,128,384]{2,1,0:T(8,128)S(1)}, f32[2,128,384]{2,1,0:T(8,128)S(1)}, u32[]{:S(2)}, u32[]{:S(2)}) collective-permute-start(f32[2,128,384]{2,1,0:T(8,128)S(1)} %get-tuple-element.102), channel_id=1, source_target_pairs={{0,248},{8,16},{16,8},{24,32},{32,24},{40,48},{48,40},{56,64},{64,... | collective-permute-start | bytes 1179656 | tf_op jit(solution)/shard_map/ppermute | solution.py:384
  51.0 16.7 %collective-permute-start.9 = (f32[2,128,384]{2,1,0:T(8,128)S(1)}, f32[2,128,384]{2,1,0:T(8,128)S(1)}, u32[]{:S(2)}, u32[]{:S(2)}) collective-permute-start(f32[2,128,384]{2,1,0:T(8,128)S(1)} %get-tuple-element.79), channel_id=1, source_target_pairs={{0,8},{8,0},{16,24},{24,16},{32,40},{40,32},{48,56},{56,48},{64,72... | collective-permute-start | bytes 1179656 | tf_op jit(solution)/shard_map/ppermute | solution.py:384
  52.3 19.9 %collective-permute-start.10 = (f32[2,128,384]{2,1,0:T(8,128)S(1)}, f32[2,128,384]{2,1,0:T(8,128)S(1)}, u32[]{:S(2)}, u32[]{:S(2)}) collective-permute-start(f32[2,128,384]{2,1,0:T(8,128)S(1)} %get-tuple-element.80), channel_id=1, source_target_pairs={{0,248},{8,16},{16,8},{24,32},{32,24},{40,48},{48,40},{56,64},{64,... | collective-permute-start | bytes 1179656 | tf_op jit(solution)/shard_map/ppermute | solution.py:384
  57.9 14.6 %collective-permute-start.14 = (f32[2,384,128]{2,1,0:T(8,128)S(1)}, f32[2,384,128]{2,1,0:T(8,128)S(1)}, u32[]{:S(2)}, u32[]{:S(2)}) collective-permute-start(f32[2,384,128]{2,1,0:T(8,128)S(1)} %get-tuple-element.91.left), channel_id=1, source_target_pairs={{1,0},{2,1},{3,2},{4,3},{5,4},{6,5},{7,6},{0,7},{9,8},{10,9},{11,1... | collective-permute-start | bytes 1179656 | tf_op jit(solution)/shard_map/ppermute | solution.py:376
  60.7 11.8 %collective-permute-start.13 = (f32[2,384,128]{2,1,0:T(8,128)S(1)}, f32[2,384,128]{2,1,0:T(8,128)S(1)}, u32[]{:S(2)}, u32[]{:S(2)}) collective-permute-start(f32[2,384,128]{2,1,0:T(8,128)S(1)} %get-tuple-element.92.right), channel_id=1, source_target_pairs={{7,0},{0,1},{1,2},{2,3},{3,4},{4,5},{5,6},{6,7},{15,8},{8,9},{9,10... | collective-permute-start | bytes 1179656 | tf_op jit(solution)/shard_map/ppermute | solution.py:376
  64.4 13.2 %collective-permute-start.18 = (f32[2,384,128]{2,1,0:T(8,128)S(1)}, f32[2,384,128]{2,1,0:T(8,128)S(1)}, u32[]{:S(2)}, u32[]{:S(2)}) collective-permute-start(f32[2,384,128]{2,1,0:T(8,128)S(1)} %get-tuple-element.103.left), channel_id=1, source_target_pairs={{1,0},{2,1},{3,2},{4,3},{5,4},{6,5},{7,6},{0,7},{9,8},{10,9},{11,1... | collective-permute-start | bytes 1179656 | tf_op jit(solution)/shard_map/ppermute | solution.py:376
  67.7 9.9 %collective-permute-start.17 = (f32[2,384,128]{2,1,0:T(8,128)S(1)}, f32[2,384,128]{2,1,0:T(8,128)S(1)}, u32[]{:S(2)}, u32[]{:S(2)}) collective-permute-start(f32[2,384,128]{2,1,0:T(8,128)S(1)} %get-tuple-element.104.right), channel_id=1, source_target_pairs={{7,0},{0,1},{1,2},{2,3},{3,4},{4,5},{5,6},{6,7},{15,8},{8,9},{9,10... | collective-permute-start | bytes 1179656 | tf_op jit(solution)/shard_map/ppermute | solution.py:376
  83.4 12.6 %collective-permute-start.25 = (f32[2,384,128]{2,1,0:T(8,128)S(1)}, f32[2,384,128]{2,1,0:T(8,128)S(1)}, u32[]{:S(2)}, u32[]{:S(2)}) collective-permute-start(f32[2,384,128]{2,1,0:T(8,128)S(1)} %get-tuple-element.121), channel_id=1, source_target_pairs={{7,0},{0,1},{1,2},{2,3},{3,4},{4,5},{5,6},{6,7},{15,8},{8,9},{9,10... | collective-permute-start | bytes 1179656 | tf_op jit(solution)/shard_map/ppermute | solution.py:376
  86.0 11.4 %collective-permute-start.21 = (f32[2,128,128]{2,1,0:T(8,128)S(1)}, f32[2,128,128]{2,1,0:T(8,128)S(1)}, u32[]{:S(2)}, u32[]{:S(2)}) collective-permute-start(f32[2,128,128]{2,1,0:T(8,128)S(1)} %slice.15), channel_id=1, source_target_pairs={{7,0},{0,1},{1,2},{2,3},{3,4},{4,5},{5,6},{6,7},{15,8},{8,9},{9,10... | collective-permute-start | bytes 393224 | tf_op jit(solution)/shard_map/ppermute | solution.py:376
  96.0 17.0 %collective-permute-start.27 = (f32[2,2,128,128]{3,2,1,0:T(8,128)S(1)}, f32[2,2,128,128]{3,2,1,0:T(8,128)S(1)}, u32[]{:S(2)}, u32[]{:S(2)}) collective-permute-start(f32[2,2,128,128]{3,2,1,0:T(8,128)S(1)} %shard_map.84), channel_id=1, source_target_pairs={{248,0},{0,8},{8,16},{16,24},{24,32},{32,40},{40,48},{48,56},{56,6... | collective-permute-start | bytes 786440 | tf_op jit(solution)/shard_map/ppermute | solution.py:376
  96.4 15.1 %collective-permute-start.24 = (f32[2,128,128]{2,1,0:T(8,128)S(1)}, f32[2,128,128]{2,1,0:T(8,128)S(1)}, u32[]{:S(2)}, u32[]{:S(2)}) collective-permute-start(f32[2,128,128]{2,1,0:T(8,128)S(1)} %get-tuple-element.118), channel_id=1, source_target_pairs={{248,0},{0,8},{8,16},{16,24},{24,32},{32,40},{40,48},{48,56},{56,6... | collective-permute-start | bytes 393224 | tf_op jit(solution)/shard_map/ppermute | solution.py:376
  96.5 23.3 %collective-permute-start.19 = (f32[2,256,128]{2,1,0:T(8,128)S(1)}, f32[2,256,128]{2,1,0:T(8,128)S(1)}, u32[]{:S(2)}, u32[]{:S(2)}) collective-permute-start(f32[2,256,128]{2,1,0:T(8,128)S(1)} %slice.14), channel_id=1, source_target_pairs={{7,0},{0,1},{1,2},{2,3},{3,4},{4,5},{5,6},{6,7},{15,8},{8,9},{9,10... | collective-permute-start | bytes 786440 | tf_op jit(solution)/shard_map/ppermute | solution.py:376
  96.5 16.5 %collective-permute-start.26 = (f32[2,128,128]{2,1,0:T(8,128)S(1)}, f32[2,128,128]{2,1,0:T(8,128)S(1)}, u32[]{:S(2)}, u32[]{:S(2)}) collective-permute-start(f32[2,128,128]{2,1,0:T(8,128)S(1)} %get-tuple-element.122), channel_id=1, source_target_pairs={{248,0},{0,8},{8,16},{16,24},{24,32},{32,40},{40,48},{48,56},{56,6... | collective-permute-start | bytes 393224 | tf_op jit(solution)/shard_map/ppermute | solution.py:376
  97.4 17.0 %collective-permute-start.20 = (f32[2,128,128]{2,1,0:T(8,128)S(1)}, f32[2,128,128]{2,1,0:T(8,128)S(1)}, u32[]{:S(2)}, u32[]{:S(2)}) collective-permute-start(f32[2,128,128]{2,1,0:T(8,128)S(1)} %get-tuple-element.114), channel_id=1, source_target_pairs={{248,0},{0,8},{8,16},{16,24},{24,32},{32,40},{40,48},{48,56},{56,6... | collective-permute-start | bytes 393224 | tf_op jit(solution)/shard_map/ppermute | solution.py:376
  (11 other events, 122.3 us)

commit v6 on v5

--- a/solution.py
+++ b/solution.py
@@ -445,13 +445,13 @@
     return plain(prepare_kernel, outs, [probe, propagator, tables])
 
 
-def sums_kernel(summed, left, middle, low, right, *refs):
+def sums_kernel(count, left, middle, low, right, *refs):
     h, t = PROBE, TILE
     even_out, odd_out = refs[-2:]
-    from_left, from_right = refs[:2] if summed else (None, None)
+    from_left, from_right = refs[:count] if count else (None, None)
 
     def total(own, other, rows):
-        return own[:, rows] + other[:, rows] if summed else own[:, rows]
+        return own[:, rows] if other is None else own[:, rows] + other[:, rows]
 
     def fill(down, up):
         down[:, :, :h] = total(left, from_left, slice(t, t + h))
@@ -473,7 +473,7 @@
 
 
 def sums(grad, columns):
-    body = functools.partial(sums_kernel, bool(columns))
+    body = functools.partial(sums_kernel, len(columns))
     return plain(body, [shape(2, PROBE, EXT)] * 2, [*grad, *columns])
 
 
@@ -526,44 +526,50 @@
     return plain(body, [SIDE] * 3, operands, specs)
 
 
-def spill_kernel(*refs):
-    down = refs[-1]
-    for n in range(down.shape[0]):
-        left, from_left = refs[2 * n : 2 * n + 2]
-        rows = from_left.shape[1]
-        down[n] = left[:, TILE:] + from_left[:, rows - PROBE :]
-
-
-def spill(*pairs):
-    operands = [array for pair in pairs for array in pair]
-    return plain(spill_kernel, [shape(len(pairs), 2, PROBE, PROBE)], operands)[0]
-
-
-def last_kernel(layers, place, *refs):
+def spill_kernel(left, from_left, down):
+    rows = from_left.shape[1]
+    down[...] = left[:, TILE:] + from_left[:, rows - PROBE :]
+
+
+def join_kernel(left, low, right, down):
+    h, t = PROBE, TILE
+    down[:, :, :h] = left[:, t:]
+    down[:, :, h:t] = low[...]
+    down[:, :, t:] = right[:, t:]
+
+
+def east_kernel(right, above, east):
+    h, t = PROBE, TILE
+    east[:, :h] = right[:, :h] + above[:, :, t:]
+    east[:, h:] = right[:, h:t]
+
+
+def last_kernel(whole_rows, *refs):
+    old_l, old_m, left, middle, from_left = refs[:5]
     out, h, t = refs[-1], PROBE, TILE
-    above_l = refs[6 * layers]
-    for n in range(layers):
-        old_l, old_m, left, middle, from_left, above_m = refs[6 * n : 6 * n + 6]
-        top_l = left[:, :h] + from_left[:, :h] + above_l[n]
-        out[:, place + n, :h, :h] = old_l[:, :h] - STEP * top_l
-        out[:, place + n, h:, :h] = old_l[:, h:t] - STEP * (left[:, h:t] + from_left[:, h:t])
-        out[:, place + n, :h, h:] = old_m[:, :h] - STEP * (middle[:, :h] + above_m[...])
-        out[:, place + n, h:, h:] = old_m[:, h:t] - STEP * middle[:, h:t]
-
-
-def last(pieces, above_l, spec, result):
-    operands = [array for piece in pieces for array in piece] + [above_l]
+    if whole_rows:
+        above_l, above_m = refs[5][:, :, :h], refs[5][:, :, h:t]
+    else:
+        above_l, above_m = refs[5][...], refs[6][...]
+    out[:, 0, :h, :h] = old_l[:, :h] - STEP * (left[:, :h] + from_left[:, :h] + above_l)
+    out[:, 0, h:, :h] = old_l[:, h:t] - STEP * (left[:, h:t] + from_left[:, h:t])
+    out[:, 0, :h, h:] = old_m[:, :h] - STEP * (middle[:, :h] + above_m)
+    out[:, 0, h:, h:] = old_m[:, h:t] - STEP * middle[:, h:t]
+
+
+def last(layer, piece, above, result):
+    operands = [*piece, *above]
     specs, aliases = {}, {}
     if result is not None:
         specs, aliases = {len(operands): pl.BlockSpec(memory_space=pl.ANY)}, {len(operands): 0}
         operands.append(result)
     return plain(
-        functools.partial(last_kernel, len(pieces), 0 if result is not None else 1),
+        functools.partial(last_kernel, len(above) == 1),
         [shape(2, SLICES, TILE, TILE)],
         operands,
         specs,
         aliases,
-        [spec],
+        [tile_of(layer)],
     )[0]
 
 
@@ -609,8 +615,8 @@
         from_right = shifted(west, "col", -1)
         return [from_left, from_right]
 
-    for layer in (2, 1, 0):
-        grad, rows_first = grads[layer], layer != 0
+    for layer in (1, 0, 2):
+        grad, rows_first = grads[layer], layer == 1
         moved = [] if rows_first else columns(grad[0], grad[3])
         for_even, for_odd = sums(grad, moved)
         even = swapped(for_even, 0)
@@ -621,22 +627,22 @@
             grad = [west, grad[1], grad[2], east]
         renewed[layer] = list(update(layer, fields[layer], grad, moved, even, odd, rows_first))
     grads = gradients(renewed, fill_next)
-    from_left, above_m = {}, {}
-    for layer in (2, 1, 0):
+    from_left, above_m, above_l = {}, {}, {}
+    down = plain(join_kernel, [shape(2, h, EXT)], [grads[2][0], grads[2][2], grads[2][3]])[0]
+    above2 = shifted(down, "row", 1)
+    east = plain(east_kernel, [shape(2, t, h)], [grads[2][3], above2])[0]
+    from_left[2] = shifted(east, "col", 1)
+    for layer in (1, 0):
         right = grads[layer][3]
         from_left[layer] = shifted(right if layer else right[:, t:], "col", 1)
         above_m[layer] = shifted(grads[layer][2], "row", 1)
-    down = spill((grads[1][0], from_left[1]), (grads[2][0], from_left[2]))
-    above_l12 = shifted(down, "row", 1)
-    down = spill((grads[0][0], from_left[0]))
-    above_l0 = shifted(down, "row", 1)
+        down = plain(spill_kernel, [shape(2, h, h)], [grads[layer][0], from_left[layer]])[0]
+        above_l[layer] = shifted(down, "row", 1)
     from_left[0] = shifted(grads[0][3][:, :t], "col", 1)
-    pieces = [
-        (renewed[n][0], renewed[n][1], grads[n][0], grads[n][1], from_left[n], above_m[n])
-        for n in range(SLICES)
-    ]
-    result = last(pieces[1:], above_l12, whole(shape(2, SLICES, TILE, TILE)), None)
-    return last(pieces[:1], above_l0, tile_of(0), result)
+    pieces = [(renewed[n][0], renewed[n][1], grads[n][0], grads[n][1], from_left[n]) for n in range(SLICES)]
+    result = last(2, pieces[2], [above2], None)
+    result = last(1, pieces[1], [above_l[1], above_m[1]], result)
+    return last(0, pieces[0], [above_l[0], above_m[0]], result)
 
 
 def solution(mesh):

time: 121 us -> 118 us (0.975)
  the two profiles are of different devices: /device:TPU:0 before, /device:TPU:1 now
where the time goes in v6:
time: 118 us
  starting transfers between devices  48.2 us (41%)
  waiting for transfers between devices  37.9 us (32%)
  Pallas kernels  30.4 us (26%)
  local copies, waits for them, and re-layouts  1.49 us (1%)
    ppermute x22, starting transfers between devices, shifted(): lax.ppermute(block, axis, [((i - distance) % size, i) for i in range(size)])  33.8 us
    ppermute x22, waiting for transfers between devices, shifted(): lax.ppermute(block, axis, [((i - distance) % size, i) for i in range(size)])  26.7 us
    pallas_call x10, Pallas kernels, run(): pl.pallas_call(body, grid=(1,), in_specs=in_specs, out_specs=[whole(o) fo...  26 us
    ppermute x6, starting transfers between devices, swapped(): return lax.ppermute(block, 'row', sorted(route))  14.4 us
    ppermute x6, waiting for transfers between devices, swapped(): return lax.ppermute(block, 'row', sorted(route))  11.2 us
    pallas_call x15, Pallas kernels, plain(): pl.pallas_call(body, grid=(1,), in_specs=[specs.get(n, None) or whole(o)...  4.24 us
  transfers between devices with their start and end apart: 28, of which 14 were waited for; matrix products, arithmetic and copies ran while one was open for 0% of the time, Pallas kernels for 15%

profile of v6, /device:TPU:1, one launch (start us, length us, event | category | flops | bytes accessed | tf_op | source)
XLA Modules:
  0.0 118.3 jit_solution(16368981516724743721)
XLA Ops:
  1.6 8.9 %collective-permute-start.3 = (f32[2,2,128,128]{3,2,1,0:T(8,128)S(1)}, f32[2,2,128,128]{3,2,1,0:T(8,128)S(1)}, u32[]{:S(2)}, u32[]{:S(2)}) collective-permute-start(f32[2,2,128,128]{3,2,1,0:T(8,128)S(1)} %get-tuple-element.66), channel_id=1, source_target_pairs={{8,0},{16,8},{24,16},{32,24},{40,32},{48,40},{56,48},{64,56},{72,6... | collective-permute-start | bytes 786440 | tf_op jit(solution)/shard_map/ppermute | solution.py:376
  15.5 2.7 %collective-permute-start.6 = (f32[2,2,128,128]{3,2,1,0:T(8,128)S(1)}, f32[2,2,128,128]{3,2,1,0:T(8,128)S(1)}, u32[]{:S(2)}, u32[]{:S(2)}) collective-permute-start(f32[2,2,128,128]{3,2,1,0:T(8,128)S(1)} %collective-permute-done.3.refs_5_.low_left), channel_id=1, source_target_pairs={{1,0},{2,1},{3,2},{4,3},{5,4},{6,5},{7,6},{0,7},{9,8},{10,9},{11,1... | collective-permute-start | bytes 786440 | tf_op jit(solution)/shard_map/ppermute | solution.py:376
  18.1 3.0 %collective-permute-done.refs_4_.refs_5_.low_left.low_right = f32[2,128,256]{2,1,0:T(8,128)S(1)} collective-permute-done((f32[2,128,256]{2,1,0:T(8,128)S(1)}, f32[2,128,256]{2,1,0:T(8,128)S(1)}, u32[]{:S(2)}, u32[]{:S(2)}) %collective-permute-start) | collective-permute-done | bytes 262176 | tf_op jit(solution)/shard_map/ppermute | solution.py:376
  21.1 2.7 %collective-permute-start.2 = (f32[2,128,128]{2,1,0:T(8,128)S(1)}, f32[2,128,128]{2,1,0:T(8,128)S(1)}, u32[]{:S(2)}, u32[]{:S(2)}) collective-permute-start(f32[2,128,128]{2,1,0:T(8,128)S(1)} %slice.16), channel_id=1, source_target_pairs={{1,0},{2,1},{3,2},{4,3},{5,4},{6,5},{7,6},{0,7},{9,8},{10,9},{11,1... | collective-permute-start | bytes 393224 | tf_op jit(solution)/shard_map/ppermute | solution.py:376
  24.3 3.3 %collective-permute-done.2.refs_7_.corner = f32[2,128,128]{2,1,0:T(8,128)S(1)} collective-permute-done((f32[2,128,128]{2,1,0:T(8,128)S(1)}, f32[2,128,128]{2,1,0:T(8,128)S(1)}, u32[]{:S(2)}, u32[]{:S(2)}) %collective-permute-start.2) | collective-permute-done | bytes 131104 | tf_op jit(solution)/shard_map/ppermute | solution.py:376
  27.5 2.4 %shard_map.65 = (f32[2,6,128,128]{3,2,1,0:T(8,128)}, f32[2,6,128,128]{3,2,1,0:T(8,128)S(1)}) custom-call(s32[2,6]{1,0:T(2,128)S(1)} %bitcast.10, bf16[4,256,256]{2,1,0:T(8,128)(2,1)S(1)} %get-tuple-element.63.refs_1_, f32[4,128,128]{2,1,0:T(8,128)S(1)} %get-tuple-element.64.refs_2_, f32[2,3,256,256]{3,2,1,0:T(8,128)S(1)} %copy-done.1, ...), custom_call_target="tpu_custom_call" | custom-call | flops 1207959552 | bytes 5374000 | tf_op jit(solution)/shard_map/pallas_call | solution.py:326
  30.0 2.4 %shard_map.66 = (f32[2,6,128,128]{3,2,1,0:T(8,128)S(1)}, f32[2,6,128,128]{3,2,1,0:T(8,128)S(1)}) custom-call(s32[2,6]{1,0:T(2,128)S(1)} %bitcast.11, bf16[4,256,256]{2,1,0:T(8,128)(2,1)S(1)} %get-tuple-element.63.refs_1_, f32[4,128,128]{2,1,0:T(8,128)S(1)} %get-tuple-element.64.refs_2_, f32[2,6,128,128]{3,2,1,0:T(8,128)S(1)} %get-tuple-element.65.refs_3_.refs_4_, ...), custom_call_target="tpu_custom_call" | custom-call | flops 1207959552 | bytes 6553648 | tf_op jit(solution)/shard_map/pallas_call | solution.py:326
  32.5 2.9 %shard_map.67 = (f32[2,384,128]{2,1,0:T(8,128)S(1)}, f32[2,256,128]{2,1,0:T(8,128)S(1)}, f32[2,128,128]{2,1,0:T(8,128)S(1)}, f32[2,384,128]{2,1,0:T(8,128)S(1)}, f32[2,6,128,128]{3,2,1,0:T(8,128)S(1)}) custom-call(s32[2,6]{1,0:T(2,128)S(1)} %bitcast.12, bf16[4,256,256]{2,1,0:T(8,128)(2,1)S(1)} %get-tuple-element.63.refs_1_, f32[6,128,128]{2,1,0:T(8,128)S(1)} %bitcast.8, ...), custom_call_target="tpu_custom_call" | custom-call | flops 1207959552 | bytes 7077936 | tf_op jit(solution)/shard_map/pallas_call | solution.py:326
  35.4 2.7 %shard_map.68 = (f32[2,384,128]{2,1,0:T(8,128)S(1)}, f32[2,256,128]{2,1,0:T(8,128)S(1)}, f32[2,128,128]{2,1,0:T(8,128)S(1)}, f32[2,384,128]{2,1,0:T(8,128)S(1)}, f32[2,6,128,128]{3,2,1,0:T(8,128)S(1)}) custom-call(s32[2,6]{1,0:T(2,128)S(1)} %bitcast.13, bf16[4,256,256]{2,1,0:T(8,128)(2,1)S(1)} %get-tuple-element.63.refs_1_, ...), custom_call_target="tpu_custom_call" | custom-call | flops 1207959552 | bytes 5636144 | tf_op jit(solution)/shard_map/pallas_call | solution.py:326
  38.3 6.1 %collective-permute-start.12 = (f32[2,128,384]{2,1,0:T(8,128)S(1)}, f32[2,128,384]{2,1,0:T(8,128)S(1)}, u32[]{:S(2)}, u32[]{:S(2)}) collective-permute-start(f32[2,128,384]{2,1,0:T(8,128)S(1)} %get-tuple-element.88), channel_id=1, source_target_pairs={{0,248},{8,16},{16,8},{24,32},{32,24},{40,48},{48,40},{56,64},{64,... | collective-permute-start | bytes 1179656 | tf_op jit(solution)/shard_map/ppermute | solution.py:384
  44.4 2.6 %shard_map.69 = (f32[2,384,128]{2,1,0:T(8,128)S(1)}, f32[2,256,128]{2,1,0:T(8,128)S(1)}, f32[2,128,128]{2,1,0:T(8,128)S(1)}, f32[2,384,128]{2,1,0:T(8,128)S(1)}) custom-call(s32[2,6]{1,0:T(2,128)S(1)} %bitcast.14, bf16[4,256,256]{2,1,0:T(8,128)(2,1)S(1)} %get-tuple-element.63.refs_1_, f32[4,128,128]{2,1,0:T(8,128)S(1)} %get-tuple-element.64.refs_2_, ...), custom_call_target="tpu_custom_call" | custom-call | flops 1207959552 | bytes 3276848 | tf_op jit(solution)/shard_map/pallas_call | solution.py:326
  49.8 2.9 %collective-permute-done.12.odd.refs_3_ = f32[2,128,384]{2,1,0:T(8,128)S(1)} collective-permute-done((f32[2,128,384]{2,1,0:T(8,128)S(1)}, f32[2,128,384]{2,1,0:T(8,128)S(1)}, u32[]{:S(2)}, u32[]{:S(2)}) %collective-permute-start.12) | collective-permute-done | bytes 393248 | tf_op jit(solution)/shard_map/ppermute | solution.py:384
  54.6 3.9 %collective-permute-start.10 = (f32[2,128,384]{2,1,0:T(8,128)S(1)}, f32[2,128,384]{2,1,0:T(8,128)S(1)}, u32[]{:S(2)}, u32[]{:S(2)}) collective-permute-start(f32[2,128,384]{2,1,0:T(8,128)S(1)} %get-tuple-element.78), channel_id=1, source_target_pairs={{0,248},{8,16},{16,8},{24,32},{32,24},{40,48},{48,40},{56,64},{64,... | collective-permute-start | bytes 1179656 | tf_op jit(solution)/shard_map/ppermute | solution.py:384
  60.1 2.9 %collective-permute-start.18 = (f32[2,128,384]{2,1,0:T(8,128)S(1)}, f32[2,128,384]{2,1,0:T(8,128)S(1)}, u32[]{:S(2)}, u32[]{:S(2)}) collective-permute-start(f32[2,128,384]{2,1,0:T(8,128)S(1)} %get-tuple-element.100), channel_id=1, source_target_pairs={{0,248},{8,16},{16,8},{24,32},{32,24},{40,48},{48,40},{56,64},{64,... | collective-permute-start | bytes 1179656 | tf_op jit(solution)/shard_map/ppermute | solution.py:384
  63.3 4.3 %collective-permute-done.10.refs_3_ = f32[2,128,384]{2,1,0:T(8,128)S(1)} collective-permute-done((f32[2,128,384]{2,1,0:T(8,128)S(1)}, f32[2,128,384]{2,1,0:T(8,128)S(1)}, u32[]{:S(2)}, u32[]{:S(2)}) %collective-permute-start.10) | collective-permute-done | bytes 393248 | tf_op jit(solution)/shard_map/ppermute | solution.py:384
  70.3 2.4 %shard_map.76 = (f32[2,6,128,128]{3,2,1,0:T(8,128)S(1)}, f32[2,6,128,128]{3,2,1,0:T(8,128)S(1)}) custom-call(s32[2,6]{1,0:T(2,128)S(1)} %bitcast.16, bf16[4,256,256]{2,1,0:T(8,128)(2,1)S(1)} %get-tuple-element.63.refs_1_, f32[4,128,128]{2,1,0:T(8,128)S(1)} %get-tuple-element.64.refs_2_, f32[2,6,128,128]{3,2,1,0:T(8,128)S(1)} %get-tuple-element.82.refs_3_.refs_4_, ...), custom_call_target="tpu_custom_call" | custom-call | flops 1207959552 | bytes 4849712 | tf_op jit(solution)/shard_map/pallas_call | solution.py:326
  76.3 2.9 %shard_map.79 = (f32[2,384,128]{2,1,0:T(8,128)S(1)}, f32[2,256,128]{2,1,0:T(8,128)S(1)}, f32[2,128,128]{2,1,0:T(8,128)S(1)}, f32[2,384,128]{2,1,0:T(8,128)S(1)}, f32[2,6,128,128]{3,2,1,0:T(8,128)S(1)}) custom-call(s32[2,6]{1,0:T(2,128)S(1)} %bitcast.17, bf16[4,256,256]{2,1,0:T(8,128)(2,1)S(1)} %get-tuple-element.63.refs_1_, f32[6,128,128]{2,1,0:T(8,128)S(1)} %bitcast.9, ...), custom_call_target="tpu_custom_call" | custom-call | flops 1207959552 | bytes 5374000 | tf_op jit(solution)/shard_map/pallas_call | solution.py:326
  79.5 2.6 %shard_map.80 = (f32[2,384,128]{2,1,0:T(8,128)S(1)}, f32[2,256,128]{2,1,0:T(8,128)S(1)}, f32[2,128,128]{2,1,0:T(8,128)S(1)}, f32[2,384,128]{2,1,0:T(8,128)S(1)}, f32[2,6,128,128]{3,2,1,0:T(8,128)S(1)}) custom-call(s32[2,6]{1,0:T(2,128)S(1)} %bitcast.18, bf16[4,256,256]{2,1,0:T(8,128)(2,1)S(1)} %get-tuple-element.63.refs_1_, ...), custom_call_target="tpu_custom_call" | custom-call | flops 1207959552 | bytes 5636144 | tf_op jit(solution)/shard_map/pallas_call | solution.py:326
  82.2 4.1 %collective-permute-start.23 = (f32[2,384,128]{2,1,0:T(8,128)S(1)}, f32[2,384,128]{2,1,0:T(8,128)S(1)}, u32[]{:S(2)}, u32[]{:S(2)}) collective-permute-start(f32[2,384,128]{2,1,0:T(8,128)S(1)} %get-tuple-element.113), channel_id=1, source_target_pairs={{7,0},{0,1},{1,2},{2,3},{3,4},{4,5},{5,6},{6,7},{15,8},{8,9},{9,10... | collective-permute-start | bytes 1179656 | tf_op jit(solution)/shard_map/ppermute | solution.py:376
  86.3 4.8 %collective-permute-done.26.above.refs_5_ = f32[2,128,384]{2,1,0:T(8,128)S(1)} collective-permute-done((f32[2,128,384]{2,1,0:T(8,128)S(1)}, f32[2,128,384]{2,1,0:T(8,128)S(1)}, u32[]{:S(2)}, u32[]{:S(2)}) %collective-permute-start.26) | collective-permute-done | bytes 393248 | tf_op jit(solution)/shard_map/ppermute | solution.py:376
  91.1 5.6 %collective-permute-start.27 = (f32[2,256,128]{2,1,0:T(8,128)S(1)}, f32[2,256,128]{2,1,0:T(8,128)S(1)}, u32[]{:S(2)}, u32[]{:S(2)}) collective-permute-start(f32[2,256,128]{2,1,0:T(8,128)S(1)} %shard_map.85), channel_id=1, source_target_pairs={{7,0},{0,1},{1,2},{2,3},{3,4},{4,5},{5,6},{6,7},{15,8},{8,9},{9,10... | collective-permute-start | bytes 786440 | tf_op jit(solution)/shard_map/ppermute | solution.py:376
  96.7 2.6 %shard_map.81 = (f32[2,384,128]{2,1,0:T(8,128)S(1)}, f32[2,256,128]{2,1,0:T(8,128)S(1)}, f32[2,128,128]{2,1,0:T(8,128)S(1)}, f32[2,384,128]{2,1,0:T(8,128)S(1)}) custom-call(s32[2,6]{1,0:T(2,128)S(1)} %bitcast.19, bf16[4,256,256]{2,1,0:T(8,128)(2,1)S(1)} %get-tuple-element.63.refs_1_, f32[4,128,128]{2,1,0:T(8,128)S(1)} %get-tuple-element.64.refs_2_, ...), custom_call_target="tpu_custom_call" | custom-call | flops 1207959552 | bytes 3276848 | tf_op jit(solution)/shard_map/pallas_call | solution.py:326
  102.5 7.5 %collective-permute-done.25.refs_6_ = f32[2,128,128]{2,1,0:T(8,128)S(1)} collective-permute-done((f32[2,128,128]{2,1,0:T(8,128)S(1)}, f32[2,128,128]{2,1,0:T(8,128)S(1)}, u32[]{:S(2)}, u32[]{:S(2)}) %collective-permute-start.25) | collective-permute-done | bytes 131104 | tf_op jit(solution)/shard_map/ppermute | solution.py:376
  110.0 5.6 %collective-permute-done.24.refs_5_ = f32[2,128,128]{2,1,0:T(8,128)S(1)} collective-permute-done((f32[2,128,128]{2,1,0:T(8,128)S(1)}, f32[2,128,128]{2,1,0:T(8,128)S(1)}, u32[]{:S(2)}, u32[]{:S(2)}) %collective-permute-start.24) | collective-permute-done | bytes 131104 | tf_op jit(solution)/shard_map/ppermute | solution.py:376
  (76 shorter events, 26.1 us)
Async XLA Ops:
  1.6 13.9 %collective-permute-start.3 = (f32[2,2,128,128]{3,2,1,0:T(8,128)S(1)}, f32[2,2,128,128]{3,2,1,0:T(8,128)S(1)}, u32[]{:S(2)}, u32[]{:S(2)}) collective-permute-start(f32[2,2,128,128]{3,2,1,0:T(8,128)S(1)} %get-tuple-element.66), channel_id=1, source_target_pairs={{8,0},{16,8},{24,16},{32,24},{40,32},{48,40},{56,48},{64,56},{72,6... | collective-permute-start | bytes 786440 | tf_op jit(solution)/shard_map/ppermute | solution.py:376
  10.5 19.5 %collective-permute-start.5 = (f32[2,2,256,128]{3,2,1,0:T(8,128)S(1)}, f32[2,2,256,128]{3,2,1,0:T(8,128)S(1)}, u32[]{:S(2)}, u32[]{:S(2)}) collective-permute-start(f32[2,2,256,128]{3,2,1,0:T(8,128)S(1)} %get-tuple-element.68), channel_id=1, source_target_pairs={{1,0},{2,1},{3,2},{4,3},{5,4},{6,5},{7,6},{0,7},{9,8},{10,9},{11,1... | collective-permute-start | bytes 1572872 | tf_op jit(solution)/shard_map/ppermute | solution.py:376
  11.5 9.6 %collective-permute-start = (f32[2,128,256]{2,1,0:T(8,128)S(1)}, f32[2,128,256]{2,1,0:T(8,128)S(1)}, u32[]{:S(2)}, u32[]{:S(2)}) collective-permute-start(f32[2,128,256]{2,1,0:T(8,128)S(1)} %slice_bitcast_fusion), channel_id=1, source_target_pairs={{8,0},{16,8},{24,16},{32,24},{40,32},{48,40},{56,48},{64,56},{72,6... | collective-permute-start | bytes 786440 | tf_op jit(solution)/shard_map/ppermute | solution.py:376
  12.0 12.2 %collective-permute-start.1 = (f32[2,256,128]{2,1,0:T(8,128)S(1)}, f32[2,256,128]{2,1,0:T(8,128)S(1)}, u32[]{:S(2)}, u32[]{:S(2)}) collective-permute-start(f32[2,256,128]{2,1,0:T(8,128)S(1)} %get-tuple-element.62), channel_id=1, source_target_pairs={{1,0},{2,1},{3,2},{4,3},{5,4},{6,5},{7,6},{0,7},{9,8},{10,9},{11,1... | collective-permute-start | bytes 786440 | tf_op jit(solution)/shard_map/ppermute | solution.py:376
  14.2 15.8 %collective-permute-start.4 = (f32[2,2,128,128]{3,2,1,0:T(8,128)S(1)}, f32[2,2,128,128]{3,2,1,0:T(8,128)S(1)}, u32[]{:S(2)}, u32[]{:S(2)}) collective-permute-start(f32[2,2,128,128]{3,2,1,0:T(8,128)S(1)} %get-tuple-element.67), channel_id=1, source_target_pairs={{8,0},{16,8},{24,16},{32,24},{40,32},{48,40},{56,48},{64,56},{72,6... | collective-permute-start | bytes 786440 | tf_op jit(solution)/shard_map/ppermute | solution.py:376
  15.5 14.5 %collective-permute-start.6 = (f32[2,2,128,128]{3,2,1,0:T(8,128)S(1)}, f32[2,2,128,128]{3,2,1,0:T(8,128)S(1)}, u32[]{:S(2)}, u32[]{:S(2)}) collective-permute-start(f32[2,2,128,128]{3,2,1,0:T(8,128)S(1)} %collective-permute-done.3.refs_5_.low_left), channel_id=1, source_target_pairs={{1,0},{2,1},{3,2},{4,3},{5,4},{6,5},{7,6},{0,7},{9,8},{10,9},{11,1... | collective-permute-start | bytes 786440 | tf_op jit(solution)/shard_map/ppermute | solution.py:376
  38.2 11.2 %collective-permute-start.11 = (f32[2,128,384]{2,1,0:T(8,128)S(1)}, f32[2,128,384]{2,1,0:T(8,128)S(1)}, u32[]{:S(2)}, u32[]{:S(2)}) collective-permute-start(f32[2,128,384]{2,1,0:T(8,128)S(1)} %get-tuple-element.87), channel_id=1, source_target_pairs={{0,8},{8,0},{16,24},{24,16},{32,40},{40,32},{48,56},{56,48},{64,72... | collective-permute-start | bytes 1179656 | tf_op jit(solution)/shard_map/ppermute | solution.py:384
  38.3 14.4 %collective-permute-start.12 = (f32[2,128,384]{2,1,0:T(8,128)S(1)}, f32[2,128,384]{2,1,0:T(8,128)S(1)}, u32[]{:S(2)}, u32[]{:S(2)}) collective-permute-start(f32[2,128,384]{2,1,0:T(8,128)S(1)} %get-tuple-element.88), channel_id=1, source_target_pairs={{0,248},{8,16},{16,8},{24,32},{32,24},{40,48},{48,40},{56,64},{64,... | collective-permute-start | bytes 1179656 | tf_op jit(solution)/shard_map/ppermute | solution.py:384
  47.0 7.5 %collective-permute-start.8 = (f32[2,384,128]{2,1,0:T(8,128)S(1)}, f32[2,384,128]{2,1,0:T(8,128)S(1)}, u32[]{:S(2)}, u32[]{:S(2)}) collective-permute-start(f32[2,384,128]{2,1,0:T(8,128)S(1)} %get-tuple-element.73.left), channel_id=1, source_target_pairs={{1,0},{2,1},{3,2},{4,3},{5,4},{6,5},{7,6},{0,7},{9,8},{10,9},{11,1... | collective-permute-start | bytes 1179656 | tf_op jit(solution)/shard_map/ppermute | solution.py:376
  47.5 11.0 %collective-permute-start.15 = (f32[2,384,128]{2,1,0:T(8,128)S(1)}, f32[2,384,128]{2,1,0:T(8,128)S(1)}, u32[]{:S(2)}, u32[]{:S(2)}) collective-permute-start(f32[2,384,128]{2,1,0:T(8,128)S(1)} %get-tuple-element.98.right), channel_id=1, source_target_pairs={{7,0},{0,1},{1,2},{2,3},{3,4},{4,5},{5,6},{6,7},{15,8},{8,9},{9,10... | collective-permute-start | bytes 1179656 | tf_op jit(solution)/shard_map/ppermute | solution.py:376
  49.4 9.3 %collective-permute-start.16 = (f32[2,384,128]{2,1,0:T(8,128)S(1)}, f32[2,384,128]{2,1,0:T(8,128)S(1)}, u32[]{:S(2)}, u32[]{:S(2)}) collective-permute-start(f32[2,384,128]{2,1,0:T(8,128)S(1)} %get-tuple-element.95.left), channel_id=1, source_target_pairs={{1,0},{2,1},{3,2},{4,3},{5,4},{6,5},{7,6},{0,7},{9,8},{10,9},{11,1... | collective-permute-start | bytes 1179656 | tf_op jit(solution)/shard_map/ppermute | solution.py:376
  53.0 10.1 %collective-permute-start.14 = (f32[2,384,128]{2,1,0:T(8,128)S(1)}, f32[2,384,128]{2,1,0:T(8,128)S(1)}, u32[]{:S(2)}, u32[]{:S(2)}) collective-permute-start(f32[2,384,128]{2,1,0:T(8,128)S(1)} %get-tuple-element.89.left), channel_id=1, source_target_pairs={{1,0},{2,1},{3,2},{4,3},{5,4},{6,5},{7,6},{0,7},{9,8},{10,9},{11,1... | collective-permute-start | bytes 1179656 | tf_op jit(solution)/shard_map/ppermute | solution.py:376
  54.6 13.1 %collective-permute-start.10 = (f32[2,128,384]{2,1,0:T(8,128)S(1)}, f32[2,128,384]{2,1,0:T(8,128)S(1)}, u32[]{:S(2)}, u32[]{:S(2)}) collective-permute-start(f32[2,128,384]{2,1,0:T(8,128)S(1)} %get-tuple-element.78), channel_id=1, source_target_pairs={{0,248},{8,16},{16,8},{24,32},{32,24},{40,48},{48,40},{56,64},{64,... | collective-permute-start | bytes 1179656 | tf_op jit(solution)/shard_map/ppermute | solution.py:384
  58.5 9.1 %collective-permute-start.9 = (f32[2,128,384]{2,1,0:T(8,128)S(1)}, f32[2,128,384]{2,1,0:T(8,128)S(1)}, u32[]{:S(2)}, u32[]{:S(2)}) collective-permute-start(f32[2,128,384]{2,1,0:T(8,128)S(1)} %get-tuple-element.77), channel_id=1, source_target_pairs={{0,8},{8,0},{16,24},{24,16},{32,40},{40,32},{48,56},{56,48},{64,72... | collective-permute-start | bytes 1179656 | tf_op jit(solution)/shard_map/ppermute | solution.py:384
  58.8 16.3 %collective-permute-start.17 = (f32[2,128,384]{2,1,0:T(8,128)S(1)}, f32[2,128,384]{2,1,0:T(8,128)S(1)}, u32[]{:S(2)}, u32[]{:S(2)}) collective-permute-start(f32[2,128,384]{2,1,0:T(8,128)S(1)} %get-tuple-element.99), channel_id=1, source_target_pairs={{0,8},{8,0},{16,24},{24,16},{32,40},{40,32},{48,56},{56,48},{64,72... | collective-permute-start | bytes 1179656 | tf_op jit(solution)/shard_map/ppermute | solution.py:384
  60.1 15.9 %collective-permute-start.18 = (f32[2,128,384]{2,1,0:T(8,128)S(1)}, f32[2,128,384]{2,1,0:T(8,128)S(1)}, u32[]{:S(2)}, u32[]{:S(2)}) collective-permute-start(f32[2,128,384]{2,1,0:T(8,128)S(1)} %get-tuple-element.100), channel_id=1, source_target_pairs={{0,248},{8,16},{16,8},{24,32},{32,24},{40,48},{48,40},{56,64},{64,... | collective-permute-start | bytes 1179656 | tf_op jit(solution)/shard_map/ppermute | solution.py:384
  79.2 11.9 %collective-permute-start.26 = (f32[2,128,384]{2,1,0:T(8,128)S(1)}, f32[2,128,384]{2,1,0:T(8,128)S(1)}, u32[]{:S(2)}, u32[]{:S(2)}) collective-permute-start(f32[2,128,384]{2,1,0:T(8,128)S(1)} %shard_map.84), channel_id=1, source_target_pairs={{248,0},{0,8},{8,16},{16,24},{24,32},{32,40},{40,48},{48,56},{56,6... | collective-permute-start | bytes 1179656 | tf_op jit(solution)/shard_map/ppermute | solution.py:376
  82.2 19.0 %collective-permute-start.23 = (f32[2,384,128]{2,1,0:T(8,128)S(1)}, f32[2,384,128]{2,1,0:T(8,128)S(1)}, u32[]{:S(2)}, u32[]{:S(2)}) collective-permute-start(f32[2,384,128]{2,1,0:T(8,128)S(1)} %get-tuple-element.113), channel_id=1, source_target_pairs={{7,0},{0,1},{1,2},{2,3},{3,4},{4,5},{5,6},{6,7},{15,8},{8,9},{9,10... | collective-permute-start | bytes 1179656 | tf_op jit(solution)/shard_map/ppermute | solution.py:376
  91.1 10.3 %collective-permute-start.27 = (f32[2,256,128]{2,1,0:T(8,128)S(1)}, f32[2,256,128]{2,1,0:T(8,128)S(1)}, u32[]{:S(2)}, u32[]{:S(2)}) collective-permute-start(f32[2,256,128]{2,1,0:T(8,128)S(1)} %shard_map.85), channel_id=1, source_target_pairs={{7,0},{0,1},{1,2},{2,3},{3,4},{4,5},{5,6},{6,7},{15,8},{8,9},{9,10... | collective-permute-start | bytes 786440 | tf_op jit(solution)/shard_map/ppermute | solution.py:376
  99.4 18.0 %collective-permute-start.19 = (f32[2,256,128]{2,1,0:T(8,128)S(1)}, f32[2,256,128]{2,1,0:T(8,128)S(1)}, u32[]{:S(2)}, u32[]{:S(2)}) collective-permute-start(f32[2,256,128]{2,1,0:T(8,128)S(1)} %slice.14), channel_id=1, source_target_pairs={{7,0},{0,1},{1,2},{2,3},{3,4},{4,5},{5,6},{6,7},{15,8},{8,9},{9,10... | collective-permute-start | bytes 786440 | tf_op jit(solution)/shard_map/ppermute | solution.py:376
  101.1 8.8 %collective-permute-start.25 = (f32[2,128,128]{2,1,0:T(8,128)S(1)}, f32[2,128,128]{2,1,0:T(8,128)S(1)}, u32[]{:S(2)}, u32[]{:S(2)}) collective-permute-start(f32[2,128,128]{2,1,0:T(8,128)S(1)} %get-tuple-element.114), channel_id=1, source_target_pairs={{248,0},{0,8},{8,16},{16,24},{24,32},{32,40},{40,48},{48,56},{56,6... | collective-permute-start | bytes 393224 | tf_op jit(solution)/shard_map/ppermute | solution.py:376
  101.2 15.3 %collective-permute-start.22 = (f32[2,128,128]{2,1,0:T(8,128)S(1)}, f32[2,128,128]{2,1,0:T(8,128)S(1)}, u32[]{:S(2)}, u32[]{:S(2)}) collective-permute-start(f32[2,128,128]{2,1,0:T(8,128)S(1)} %get-tuple-element.110), channel_id=1, source_target_pairs={{248,0},{0,8},{8,16},{16,24},{24,32},{32,40},{40,48},{48,56},{56,6... | collective-permute-start | bytes 393224 | tf_op jit(solution)/shard_map/ppermute | solution.py:376
  101.5 14.1 %collective-permute-start.24 = (f32[2,128,128]{2,1,0:T(8,128)S(1)}, f32[2,128,128]{2,1,0:T(8,128)S(1)}, u32[]{:S(2)}, u32[]{:S(2)}) collective-permute-start(f32[2,128,128]{2,1,0:T(8,128)S(1)} %shard_map.83), channel_id=1, source_target_pairs={{248,0},{0,8},{8,16},{16,24},{24,32},{32,40},{40,48},{48,56},{56,6... | collective-permute-start | bytes 393224 | tf_op jit(solution)/shard_map/ppermute | solution.py:376
  101.5 15.9 %collective-permute-start.21 = (f32[2,128,128]{2,1,0:T(8,128)S(1)}, f32[2,128,128]{2,1,0:T(8,128)S(1)}, u32[]{:S(2)}, u32[]{:S(2)}) collective-permute-start(f32[2,128,128]{2,1,0:T(8,128)S(1)} %shard_map.82), channel_id=1, source_target_pairs={{248,0},{0,8},{8,16},{16,24},{24,32},{32,40},{40,48},{48,56},{56,6... | collective-permute-start | bytes 393224 | tf_op jit(solution)/shard_map/ppermute | solution.py:376
  (11 other events, 129.1 us)

commit v7 on v6

--- a/solution.py
+++ b/solution.py
@@ -448,7 +448,7 @@
 def sums_kernel(count, left, middle, low, right, *refs):
     h, t = PROBE, TILE
     even_out, odd_out = refs[-2:]
-    from_left, from_right = refs[:count] if count else (None, None)
+    from_left, from_right = (*refs[:count], None, None)[:2]
 
     def total(own, other, rows):
         return own[:, rows] if other is None else own[:, rows] + other[:, rows]
@@ -458,8 +458,9 @@
         up[:, :, :h] = total(left, from_left, slice(0, h))
         down[:, :, h:t] = low[...]
         up[:, :, h:t] = middle[:, :h]
-        down[:, :, t:] = total(right, from_right, slice(t, t + h))
-        up[:, :, t:] = total(right, from_right, slice(0, h))
+        if count != 1:
+            down[:, :, t:] = total(right, from_right, slice(t, t + h))
+            up[:, :, t:] = total(right, from_right, slice(0, h))
 
     parity = lax.axis_index("row") & 1
 
@@ -473,8 +474,9 @@
 
 
 def sums(grad, columns):
+    width = TILE if len(columns) == 1 else EXT
     body = functools.partial(sums_kernel, len(columns))
-    return plain(body, [shape(2, PROBE, EXT)] * 2, [*grad, *columns])
+    return plain(body, [shape(2, PROBE, width)] * 2, [*grad, *columns])
 
 
 class Chosen:
@@ -495,8 +497,11 @@
         out[:, t:] = own[:, t:] + below[:, :, cols]
 
 
-def update_kernel(rows_first, tile, low_left, low_right, side, corner, left, middle, bottom, right, *refs):
-    from_left, from_right, even, odd, new_l, new_m, new_r = refs
+def update_kernel(rows_first, narrow, tile, low_left, low_right, side, corner, left, middle, bottom, right, *refs):
+    if narrow:
+        from_left, even, odd, new_l, new_m = refs
+    else:
+        from_left, from_right, even, odd, new_l, new_m, new_r = refs
     h, t = PROBE, TILE
     above, below = Chosen(odd, even), Chosen(even, odd)
     first, second, third = slice(0, h), slice(h, t), slice(t, t + h)
@@ -514,6 +519,8 @@
     new_m[:, top] = tile[:, 0, top, second] - STEP * (middle[:, top] + above[:, :, second])
     new_m[:, mid] = tile[:, 0, mid, second] - STEP * middle[:, mid]
     new_m[:, end] = low_right[...] - STEP * (bottom[...] + below[:, :, second])
+    if narrow:
+        return
     new_r[:, top] = side[:, top] - STEP * side_sum(right, from_right, top, third)
     new_r[:, mid] = side[:, mid] - STEP * side_sum(right, from_right, mid, third)
     new_r[:, end] = corner[...] - STEP * side_sum(right, from_right, end, third)
@@ -522,8 +529,9 @@
 def update(layer, field, grad, columns, even, odd, rows_first):
     operands = [*field, *grad, *columns, even, odd]
     specs = field_specs(0, layer, fill_first)
-    body = functools.partial(update_kernel, rows_first)
-    return plain(body, [SIDE] * 3, operands, specs)
+    narrow = len(columns) == 1
+    body = functools.partial(update_kernel, rows_first, narrow)
+    return plain(body, [SIDE] * (2 if narrow else 3), operands, specs)
 
 
 def spill_kernel(left, from_left, down):
@@ -536,6 +544,11 @@
     down[:, :, :h] = left[:, t:]
     down[:, :, h:t] = low[...]
     down[:, :, t:] = right[:, t:]
+
+
+def both_kernel(first, second, down):
+    down[0] = first[...]
+    down[1] = second[...]
 
 
 def east_kernel(right, above, east):
@@ -560,8 +573,10 @@
 def last(layer, piece, above, result):
     operands = [*piece, *above]
     specs, aliases = {}, {}
+    if len(above) == 2:
+        specs[6] = pl.BlockSpec((None, 2, PROBE, PROBE), lambda i: (layer, 0, 0, 0))
     if result is not None:
-        specs, aliases = {len(operands): pl.BlockSpec(memory_space=pl.ANY)}, {len(operands): 0}
+        specs[len(operands)], aliases = pl.BlockSpec(memory_space=pl.ANY), {len(operands): 0}
         operands.append(result)
     return plain(
         functools.partial(last_kernel, len(above) == 1),
@@ -610,24 +625,29 @@
     grads = gradients(fields, fill_first)
     renewed = [None] * SLICES
 
-    def columns(west, east):
+    def columns(west, east, layer):
         from_left = shifted(east, "col", 1)
+        if layer == 1:
+            return [from_left]
         from_right = shifted(west, "col", -1)
         return [from_left, from_right]
 
-    for layer in (1, 0, 2):
-        grad, rows_first = grads[layer], layer == 1
-        moved = [] if rows_first else columns(grad[0], grad[3])
+    for layer in (2, 1, 0):
+        grad, rows_first = grads[layer], layer == 2
+        moved = [] if rows_first else columns(grad[0], grad[3], layer)
         for_even, for_odd = sums(grad, moved)
         even = swapped(for_even, 0)
         odd = swapped(for_odd, 1)
         if rows_first:
             west, east = plain(edges_kernel, [SIDE] * 2, [grad[0], grad[3], even, odd])
-            moved = columns(west, east)
+            moved = columns(west, east, layer)
             grad = [west, grad[1], grad[2], east]
-        renewed[layer] = list(update(layer, fields[layer], grad, moved, even, odd, rows_first))
+        new = list(update(layer, fields[layer], grad, moved, even, odd, rows_first))
+        if layer == 1:
+            new.append(shifted(new[0], "col", -1))
+        renewed[layer] = new
     grads = gradients(renewed, fill_next)
-    from_left, above_m, above_l = {}, {}, {}
+    from_left, above_l = {}, {}
     down = plain(join_kernel, [shape(2, h, EXT)], [grads[2][0], grads[2][2], grads[2][3]])[0]
     above2 = shifted(down, "row", 1)
     east = plain(east_kernel, [shape(2, t, h)], [grads[2][3], above2])[0]
@@ -635,14 +655,15 @@
     for layer in (1, 0):
         right = grads[layer][3]
         from_left[layer] = shifted(right if layer else right[:, t:], "col", 1)
-        above_m[layer] = shifted(grads[layer][2], "row", 1)
         down = plain(spill_kernel, [shape(2, h, h)], [grads[layer][0], from_left[layer]])[0]
         above_l[layer] = shifted(down, "row", 1)
+    down = plain(both_kernel, [shape(2, 2, h, h)], [grads[0][2], grads[1][2]])[0]
+    above_m = shifted(down, "row", 1)
     from_left[0] = shifted(grads[0][3][:, :t], "col", 1)
     pieces = [(renewed[n][0], renewed[n][1], grads[n][0], grads[n][1], from_left[n]) for n in range(SLICES)]
     result = last(2, pieces[2], [above2], None)
-    result = last(1, pieces[1], [above_l[1], above_m[1]], result)
-    return last(0, pieces[0], [above_l[0], above_m[0]], result)
+    result = last(1, pieces[1], [above_l[1], above_m], result)
+    return last(0, pieces[0], [above_l[0], above_m], result)
 
 
 def solution(mesh):

time: 118 us -> 114 us (0.966)
  the two profiles are of different devices: /device:TPU:1 before, /device:TPU:7 now
where the time goes in v7:
time: 114 us; the launch traced here: 112 us
  starting transfers between devices  42.9 us (38%)
  waiting for transfers between devices  37.2 us (33%)
  Pallas kernels  30.3 us (27%)
  local copies, waits for them, and re-layouts  1.49 us (1%)
    ppermute x21, waiting for transfers between devices, shifted(): lax.ppermute(block, axis, [((i - distance) % size, i) for i in range(size)])  29 us
    ppermute x21, starting transfers between devices, shifted(): lax.ppermute(block, axis, [((i - distance) % size, i) for i in range(size)])  26.9 us
    pallas_call x10, Pallas kernels, run(): pl.pallas_call(body, grid=(1,), in_specs=in_specs, out_specs=[whole(o) fo...  26 us
    ppermute x6, starting transfers between devices, swapped(): return lax.ppermute(block, 'row', sorted(route))  16.1 us
    ppermute x6, waiting for transfers between devices, swapped(): return lax.ppermute(block, 'row', sorted(route))  8.16 us
    pallas_call x16, Pallas kernels, plain(): pl.pallas_call(body, grid=(1,), in_specs=[specs.get(n, None) or whole(o)...  4.16 us
  transfers between devices with their start and end apart: 27, of which 14 were waited for; matrix products, arithmetic and copies ran while one was open for 0% of the time, Pallas kernels for 14%

profile of v7, /device:TPU:7, one launch (start us, length us, event | category | flops | bytes accessed | tf_op | source)
XLA Modules:
  0.0 112.3 jit_solution(1585416693693181)
XLA Ops:
  1.6 8.1 %collective-permute-start.3 = (f32[2,2,128,128]{3,2,1,0:T(8,128)S(1)}, f32[2,2,128,128]{3,2,1,0:T(8,128)S(1)}, u32[]{:S(2)}, u32[]{:S(2)}) collective-permute-start(f32[2,2,128,128]{3,2,1,0:T(8,128)S(1)} %get-tuple-element.65), channel_id=1, source_target_pairs={{8,0},{16,8},{24,16},{32,24},{40,32},{48,40},{56,48},{64,56},{72,6... | collective-permute-start | bytes 786440 | tf_op jit(solution)/shard_map/ppermute | solution.py:376
  14.7 2.7 %collective-permute-start.6 = (f32[2,2,128,128]{3,2,1,0:T(8,128)S(1)}, f32[2,2,128,128]{3,2,1,0:T(8,128)S(1)}, u32[]{:S(2)}, u32[]{:S(2)}) collective-permute-start(f32[2,2,128,128]{3,2,1,0:T(8,128)S(1)} %collective-permute-done.3.refs_5_.low_left), channel_id=1, source_target_pairs={{1,0},{2,1},{3,2},{4,3},{5,4},{6,5},{7,6},{0,7},{9,8},{10,9},{11,1... | collective-permute-start | bytes 786440 | tf_op jit(solution)/shard_map/ppermute | solution.py:376
  17.3 3.0 %collective-permute-done.refs_4_.refs_5_.low_left.low_right = f32[2,128,256]{2,1,0:T(8,128)S(1)} collective-permute-done((f32[2,128,256]{2,1,0:T(8,128)S(1)}, f32[2,128,256]{2,1,0:T(8,128)S(1)}, u32[]{:S(2)}, u32[]{:S(2)}) %collective-permute-start) | collective-permute-done | bytes 262176 | tf_op jit(solution)/shard_map/ppermute | solution.py:376
  20.3 2.7 %collective-permute-start.2 = (f32[2,128,128]{2,1,0:T(8,128)S(1)}, f32[2,128,128]{2,1,0:T(8,128)S(1)}, u32[]{:S(2)}, u32[]{:S(2)}) collective-permute-start(f32[2,128,128]{2,1,0:T(8,128)S(1)} %slice.16), channel_id=1, source_target_pairs={{1,0},{2,1},{3,2},{4,3},{5,4},{6,5},{7,6},{0,7},{9,8},{10,9},{11,1... | collective-permute-start | bytes 393224 | tf_op jit(solution)/shard_map/ppermute | solution.py:376
  23.4 3.1 %collective-permute-done.2.refs_7_.corner = f32[2,128,128]{2,1,0:T(8,128)S(1)} collective-permute-done((f32[2,128,128]{2,1,0:T(8,128)S(1)}, f32[2,128,128]{2,1,0:T(8,128)S(1)}, u32[]{:S(2)}, u32[]{:S(2)}) %collective-permute-start.2) | collective-permute-done | bytes 131104 | tf_op jit(solution)/shard_map/ppermute | solution.py:376
  26.5 2.4 %shard_map.65 = (f32[2,6,128,128]{3,2,1,0:T(8,128)}, f32[2,6,128,128]{3,2,1,0:T(8,128)S(1)}) custom-call(s32[2,6]{1,0:T(2,128)S(1)} %bitcast.10, bf16[4,256,256]{2,1,0:T(8,128)(2,1)S(1)} %get-tuple-element.62.refs_1_, f32[4,128,128]{2,1,0:T(8,128)S(1)} %get-tuple-element.63.refs_2_, f32[2,3,256,256]{3,2,1,0:T(8,128)S(1)} %copy-done.1, ...), custom_call_target="tpu_custom_call" | custom-call | flops 1207959552 | bytes 5374000 | tf_op jit(solution)/shard_map/pallas_call | solution.py:326
  29.0 2.4 %shard_map.66 = (f32[2,6,128,128]{3,2,1,0:T(8,128)S(1)}, f32[2,6,128,128]{3,2,1,0:T(8,128)S(1)}) custom-call(s32[2,6]{1,0:T(2,128)S(1)} %bitcast.11, bf16[4,256,256]{2,1,0:T(8,128)(2,1)S(1)} %get-tuple-element.62.refs_1_, f32[4,128,128]{2,1,0:T(8,128)S(1)} %get-tuple-element.63.refs_2_, f32[2,6,128,128]{3,2,1,0:T(8,128)S(1)} %get-tuple-element.64.refs_3_.refs_4_, ...), custom_call_target="tpu_custom_call" | custom-call | flops 1207959552 | bytes 6553648 | tf_op jit(solution)/shard_map/pallas_call | solution.py:326
  31.4 2.9 %shard_map.67 = (f32[2,384,128]{2,1,0:T(8,128)S(1)}, f32[2,256,128]{2,1,0:T(8,128)S(1)}, f32[2,128,128]{2,1,0:T(8,128)S(1)}, f32[2,384,128]{2,1,0:T(8,128)S(1)}, f32[2,6,128,128]{3,2,1,0:T(8,128)S(1)}) custom-call(s32[2,6]{1,0:T(2,128)S(1)} %bitcast.12, bf16[4,256,256]{2,1,0:T(8,128)(2,1)S(1)} %get-tuple-element.62.refs_1_, f32[6,128,128]{2,1,0:T(8,128)S(1)} %bitcast.8, ...), custom_call_target="tpu_custom_call" | custom-call | flops 1207959552 | bytes 7077936 | tf_op jit(solution)/shard_map/pallas_call | solution.py:326
  34.4 2.7 %shard_map.68 = (f32[2,384,128]{2,1,0:T(8,128)S(1)}, f32[2,256,128]{2,1,0:T(8,128)S(1)}, f32[2,128,128]{2,1,0:T(8,128)S(1)}, f32[2,384,128]{2,1,0:T(8,128)S(1)}, f32[2,6,128,128]{3,2,1,0:T(8,128)S(1)}) custom-call(s32[2,6]{1,0:T(2,128)S(1)} %bitcast.13, bf16[4,256,256]{2,1,0:T(8,128)(2,1)S(1)} %get-tuple-element.62.refs_1_, ...), custom_call_target="tpu_custom_call" | custom-call | flops 1207959552 | bytes 5636144 | tf_op jit(solution)/shard_map/pallas_call | solution.py:326
  37.1 2.6 %shard_map.69 = (f32[2,384,128]{2,1,0:T(8,128)S(1)}, f32[2,256,128]{2,1,0:T(8,128)S(1)}, f32[2,128,128]{2,1,0:T(8,128)S(1)}, f32[2,384,128]{2,1,0:T(8,128)S(1)}) custom-call(s32[2,6]{1,0:T(2,128)S(1)} %bitcast.14, bf16[4,256,256]{2,1,0:T(8,128)(2,1)S(1)} %get-tuple-element.62.refs_1_, f32[4,128,128]{2,1,0:T(8,128)S(1)} %get-tuple-element.63.refs_2_, ...), custom_call_target="tpu_custom_call" | custom-call | flops 1207959552 | bytes 3276848 | tf_op jit(solution)/shard_map/pallas_call | solution.py:326
  40.2 2.5 %collective-permute-start.7 = (f32[2,384,128]{2,1,0:T(8,128)S(1)}, f32[2,384,128]{2,1,0:T(8,128)S(1)}, u32[]{:S(2)}, u32[]{:S(2)}) collective-permute-start(f32[2,384,128]{2,1,0:T(8,128)S(1)} %get-tuple-element.75.right), channel_id=1, source_target_pairs={{7,0},{0,1},{1,2},{2,3},{3,4},{4,5},{5,6},{6,7},{15,8},{8,9},{9,10... | collective-permute-start | bytes 1179656 | tf_op jit(solution)/shard_map/ppermute | solution.py:376
  42.8 5.3 %collective-permute-start.16 = (f32[2,128,384]{2,1,0:T(8,128)S(1)}, f32[2,128,384]{2,1,0:T(8,128)S(1)}, u32[]{:S(2)}, u32[]{:S(2)}) collective-permute-start(f32[2,128,384]{2,1,0:T(8,128)S(1)} %get-tuple-element.96), channel_id=1, source_target_pairs={{0,248},{8,16},{16,8},{24,32},{32,24},{40,48},{48,40},{56,64},{64,... | collective-permute-start | bytes 1179656 | tf_op jit(solution)/shard_map/ppermute | solution.py:384
  48.4 5.2 %collective-permute-start.13 = (f32[2,128,256]{2,1,0:T(8,128)S(1)}, f32[2,128,256]{2,1,0:T(8,128)S(1)}, u32[]{:S(2)}, u32[]{:S(2)}) collective-permute-start(f32[2,128,256]{2,1,0:T(8,128)S(1)} %get-tuple-element.87), channel_id=1, source_target_pairs={{0,248},{8,16},{16,8},{24,32},{32,24},{40,48},{48,40},{56,64},{64,... | collective-permute-start | bytes 786440 | tf_op jit(solution)/shard_map/ppermute | solution.py:384
  53.9 5.2 %collective-permute-start.10 = (f32[2,128,384]{2,1,0:T(8,128)S(1)}, f32[2,128,384]{2,1,0:T(8,128)S(1)}, u32[]{:S(2)}, u32[]{:S(2)}) collective-permute-start(f32[2,128,384]{2,1,0:T(8,128)S(1)} %get-tuple-element.77), channel_id=1, source_target_pairs={{0,248},{8,16},{16,8},{24,32},{32,24},{40,48},{48,40},{56,64},{64,... | collective-permute-start | bytes 1179656 | tf_op jit(solution)/shard_map/ppermute | solution.py:384
  59.5 2.7 %collective-permute-start.17 = (f32[2,384,128]{2,1,0:T(8,128)S(1)}, f32[2,384,128]{2,1,0:T(8,128)S(1)}, u32[]{:S(2)}, u32[]{:S(2)}) collective-permute-start(f32[2,384,128]{2,1,0:T(8,128)S(1)} %get-tuple-element.98.right), channel_id=1, source_target_pairs={{7,0},{0,1},{1,2},{2,3},{3,4},{4,5},{5,6},{6,7},{15,8},{8,9},{9,10... | collective-permute-start | bytes 1179656 | tf_op jit(solution)/shard_map/ppermute | solution.py:376
  63.6 2.9 %collective-permute-done.9.refs_2_ = f32[2,128,384]{2,1,0:T(8,128)S(1)} collective-permute-done((f32[2,128,384]{2,1,0:T(8,128)S(1)}, f32[2,128,384]{2,1,0:T(8,128)S(1)}, u32[]{:S(2)}, u32[]{:S(2)}) %collective-permute-start.9) | collective-permute-done | bytes 393248 | tf_op jit(solution)/shard_map/ppermute | solution.py:384
  66.5 3.7 %collective-permute-done.10.refs_3_ = f32[2,128,384]{2,1,0:T(8,128)S(1)} collective-permute-done((f32[2,128,384]{2,1,0:T(8,128)S(1)}, f32[2,128,384]{2,1,0:T(8,128)S(1)}, u32[]{:S(2)}, u32[]{:S(2)}) %collective-permute-start.10) | collective-permute-done | bytes 393248 | tf_op jit(solution)/shard_map/ppermute | solution.py:384
  75.6 2.9 %shard_map.79 = (f32[2,384,128]{2,1,0:T(8,128)S(1)}, f32[2,256,128]{2,1,0:T(8,128)S(1)}, f32[2,128,128]{2,1,0:T(8,128)S(1)}, f32[2,384,128]{2,1,0:T(8,128)S(1)}, f32[2,6,128,128]{3,2,1,0:T(8,128)S(1)}) custom-call(s32[2,6]{1,0:T(2,128)S(1)} %bitcast.17, bf16[4,256,256]{2,1,0:T(8,128)(2,1)S(1)} %get-tuple-element.62.refs_1_, f32[6,128,128]{2,1,0:T(8,128)S(1)} %bitcast.9, ...), custom_call_target="tpu_custom_call" | custom-call | flops 1207959552 | bytes 5374000 | tf_op jit(solution)/shard_map/pallas_call | solution.py:326
  78.9 2.7 %shard_map.80 = (f32[2,384,128]{2,1,0:T(8,128)S(1)}, f32[2,256,128]{2,1,0:T(8,128)S(1)}, f32[2,128,128]{2,1,0:T(8,128)S(1)}, f32[2,384,128]{2,1,0:T(8,128)S(1)}, f32[2,6,128,128]{3,2,1,0:T(8,128)S(1)}) custom-call(s32[2,6]{1,0:T(2,128)S(1)} %bitcast.18, bf16[4,256,256]{2,1,0:T(8,128)(2,1)S(1)} %get-tuple-element.62.refs_1_, ...), custom_call_target="tpu_custom_call" | custom-call | flops 1207959552 | bytes 5636144 | tf_op jit(solution)/shard_map/pallas_call | solution.py:326
  83.3 2.6 %shard_map.81 = (f32[2,384,128]{2,1,0:T(8,128)S(1)}, f32[2,256,128]{2,1,0:T(8,128)S(1)}, f32[2,128,128]{2,1,0:T(8,128)S(1)}, f32[2,384,128]{2,1,0:T(8,128)S(1)}) custom-call(s32[2,6]{1,0:T(2,128)S(1)} %bitcast.19, bf16[4,256,256]{2,1,0:T(8,128)(2,1)S(1)} %get-tuple-element.62.refs_1_, f32[4,128,128]{2,1,0:T(8,128)S(1)} %get-tuple-element.63.refs_2_, ...), custom_call_target="tpu_custom_call" | custom-call | flops 1207959552 | bytes 3276848 | tf_op jit(solution)/shard_map/pallas_call | solution.py:326
  85.8 7.4 %collective-permute-done.25.above.refs_5_ = f32[2,128,384]{2,1,0:T(8,128)S(1)} collective-permute-done((f32[2,128,384]{2,1,0:T(8,128)S(1)}, f32[2,128,384]{2,1,0:T(8,128)S(1)}, u32[]{:S(2)}, u32[]{:S(2)}) %collective-permute-start.25) | collective-permute-done | bytes 393248 | tf_op jit(solution)/shard_map/ppermute | solution.py:376
  96.3 2.9 %collective-permute-done.20.from_left = f32[2,128,128]{2,1,0:T(8,128)S(1)} collective-permute-done((f32[2,128,128]{2,1,0:T(8,128)S(1)}, f32[2,128,128]{2,1,0:T(8,128)S(1)}, u32[]{:S(2)}, u32[]{:S(2)}) %collective-permute-start.20) | collective-permute-done | bytes 131104 | tf_op jit(solution)/shard_map/ppermute | solution.py:376
  100.3 6.0 %collective-permute-done.22.refs_6_ = f32[2,2,128,128]{3,2,1,0:T(8,128)S(1)} collective-permute-done((f32[2,2,128,128]{3,2,1,0:T(8,128)S(1)}, f32[2,2,128,128]{3,2,1,0:T(8,128)S(1)}, u32[]{:S(2)}, u32[]{:S(2)}) %collective-permute-start.22) | collective-permute-done | bytes 262176 | tf_op jit(solution)/shard_map/ppermute | solution.py:376
  106.3 2.8 %collective-permute-done.24.refs_5_ = f32[2,128,128]{2,1,0:T(8,128)S(1)} collective-permute-done((f32[2,128,128]{2,1,0:T(8,128)S(1)}, f32[2,128,128]{2,1,0:T(8,128)S(1)}, u32[]{:S(2)}, u32[]{:S(2)}) %collective-permute-start.24) | collective-permute-done | bytes 131104 | tf_op jit(solution)/shard_map/ppermute | solution.py:376
  (75 shorter events, 24.6 us)
Async XLA Ops:
  1.6 13.1 %collective-permute-start.3 = (f32[2,2,128,128]{3,2,1,0:T(8,128)S(1)}, f32[2,2,128,128]{3,2,1,0:T(8,128)S(1)}, u32[]{:S(2)}, u32[]{:S(2)}) collective-permute-start(f32[2,2,128,128]{3,2,1,0:T(8,128)S(1)} %get-tuple-element.65), channel_id=1, source_target_pairs={{8,0},{16,8},{24,16},{32,24},{40,32},{48,40},{56,48},{64,56},{72,6... | collective-permute-start | bytes 786440 | tf_op jit(solution)/shard_map/ppermute | solution.py:376
  9.7 19.3 %collective-permute-start.5 = (f32[2,2,256,128]{3,2,1,0:T(8,128)S(1)}, f32[2,2,256,128]{3,2,1,0:T(8,128)S(1)}, u32[]{:S(2)}, u32[]{:S(2)}) collective-permute-start(f32[2,2,256,128]{3,2,1,0:T(8,128)S(1)} %get-tuple-element.67), channel_id=1, source_target_pairs={{1,0},{2,1},{3,2},{4,3},{5,4},{6,5},{7,6},{0,7},{9,8},{10,9},{11,1... | collective-permute-start | bytes 1572872 | tf_op jit(solution)/shard_map/ppermute | solution.py:376
  10.7 9.6 %collective-permute-start = (f32[2,128,256]{2,1,0:T(8,128)S(1)}, f32[2,128,256]{2,1,0:T(8,128)S(1)}, u32[]{:S(2)}, u32[]{:S(2)}) collective-permute-start(f32[2,128,256]{2,1,0:T(8,128)S(1)} %slice_bitcast_fusion), channel_id=1, source_target_pairs={{8,0},{16,8},{24,16},{32,24},{40,32},{48,40},{56,48},{64,56},{72,6... | collective-permute-start | bytes 786440 | tf_op jit(solution)/shard_map/ppermute | solution.py:376
  11.2 12.2 %collective-permute-start.1 = (f32[2,256,128]{2,1,0:T(8,128)S(1)}, f32[2,256,128]{2,1,0:T(8,128)S(1)}, u32[]{:S(2)}, u32[]{:S(2)}) collective-permute-start(f32[2,256,128]{2,1,0:T(8,128)S(1)} %get-tuple-element.61), channel_id=1, source_target_pairs={{1,0},{2,1},{3,2},{4,3},{5,4},{6,5},{7,6},{0,7},{9,8},{10,9},{11,1... | collective-permute-start | bytes 786440 | tf_op jit(solution)/shard_map/ppermute | solution.py:376
  11.9 17.1 %collective-permute-start.4 = (f32[2,2,128,128]{3,2,1,0:T(8,128)S(1)}, f32[2,2,128,128]{3,2,1,0:T(8,128)S(1)}, u32[]{:S(2)}, u32[]{:S(2)}) collective-permute-start(f32[2,2,128,128]{3,2,1,0:T(8,128)S(1)} %get-tuple-element.66), channel_id=1, source_target_pairs={{8,0},{16,8},{24,16},{32,24},{40,32},{48,40},{56,48},{64,56},{72,6... | collective-permute-start | bytes 786440 | tf_op jit(solution)/shard_map/ppermute | solution.py:376
  14.7 14.3 %collective-permute-start.6 = (f32[2,2,128,128]{3,2,1,0:T(8,128)S(1)}, f32[2,2,128,128]{3,2,1,0:T(8,128)S(1)}, u32[]{:S(2)}, u32[]{:S(2)}) collective-permute-start(f32[2,2,128,128]{3,2,1,0:T(8,128)S(1)} %collective-permute-done.3.refs_5_.low_left), channel_id=1, source_target_pairs={{1,0},{2,1},{3,2},{4,3},{5,4},{6,5},{7,6},{0,7},{9,8},{10,9},{11,1... | collective-permute-start | bytes 786440 | tf_op jit(solution)/shard_map/ppermute | solution.py:376
  37.0 11.0 %collective-permute-start.11 = (f32[2,384,128]{2,1,0:T(8,128)S(1)}, f32[2,384,128]{2,1,0:T(8,128)S(1)}, u32[]{:S(2)}, u32[]{:S(2)}) collective-permute-start(f32[2,384,128]{2,1,0:T(8,128)S(1)} %get-tuple-element.85.right), channel_id=1, source_target_pairs={{7,0},{0,1},{1,2},{2,3},{3,4},{4,5},{5,6},{6,7},{15,8},{8,9},{9,10... | collective-permute-start | bytes 1179656 | tf_op jit(solution)/shard_map/ppermute | solution.py:376
  39.6 8.7 %collective-permute-start.8 = (f32[2,384,128]{2,1,0:T(8,128)S(1)}, f32[2,384,128]{2,1,0:T(8,128)S(1)}, u32[]{:S(2)}, u32[]{:S(2)}) collective-permute-start(f32[2,384,128]{2,1,0:T(8,128)S(1)} %get-tuple-element.72.left), channel_id=1, source_target_pairs={{1,0},{2,1},{3,2},{4,3},{5,4},{6,5},{7,6},{0,7},{9,8},{10,9},{11,1... | collective-permute-start | bytes 1179656 | tf_op jit(solution)/shard_map/ppermute | solution.py:376
  40.2 13.4 %collective-permute-start.7 = (f32[2,384,128]{2,1,0:T(8,128)S(1)}, f32[2,384,128]{2,1,0:T(8,128)S(1)}, u32[]{:S(2)}, u32[]{:S(2)}) collective-permute-start(f32[2,384,128]{2,1,0:T(8,128)S(1)} %get-tuple-element.75.right), channel_id=1, source_target_pairs={{7,0},{0,1},{1,2},{2,3},{3,4},{4,5},{5,6},{6,7},{15,8},{8,9},{9,10... | collective-permute-start | bytes 1179656 | tf_op jit(solution)/shard_map/ppermute | solution.py:376
  42.7 11.2 %collective-permute-start.15 = (f32[2,128,384]{2,1,0:T(8,128)S(1)}, f32[2,128,384]{2,1,0:T(8,128)S(1)}, u32[]{:S(2)}, u32[]{:S(2)}) collective-permute-start(f32[2,128,384]{2,1,0:T(8,128)S(1)} %get-tuple-element.95), channel_id=1, source_target_pairs={{0,8},{8,0},{16,24},{24,16},{32,40},{40,32},{48,56},{56,48},{64,72... | collective-permute-start | bytes 1179656 | tf_op jit(solution)/shard_map/ppermute | solution.py:384
  42.8 16.4 %collective-permute-start.16 = (f32[2,128,384]{2,1,0:T(8,128)S(1)}, f32[2,128,384]{2,1,0:T(8,128)S(1)}, u32[]{:S(2)}, u32[]{:S(2)}) collective-permute-start(f32[2,128,384]{2,1,0:T(8,128)S(1)} %get-tuple-element.96), channel_id=1, source_target_pairs={{0,248},{8,16},{16,8},{24,32},{32,24},{40,48},{48,40},{56,64},{64,... | collective-permute-start | bytes 1179656 | tf_op jit(solution)/shard_map/ppermute | solution.py:384
  48.2 11.4 %collective-permute-start.12 = (f32[2,128,256]{2,1,0:T(8,128)S(1)}, f32[2,128,256]{2,1,0:T(8,128)S(1)}, u32[]{:S(2)}, u32[]{:S(2)}) collective-permute-start(f32[2,128,256]{2,1,0:T(8,128)S(1)} %get-tuple-element.86), channel_id=1, source_target_pairs={{0,8},{8,0},{16,24},{24,16},{32,40},{40,32},{48,56},{56,48},{64,72... | collective-permute-start | bytes 786440 | tf_op jit(solution)/shard_map/ppermute | solution.py:384
  48.4 15.0 %collective-permute-start.13 = (f32[2,128,256]{2,1,0:T(8,128)S(1)}, f32[2,128,256]{2,1,0:T(8,128)S(1)}, u32[]{:S(2)}, u32[]{:S(2)}) collective-permute-start(f32[2,128,256]{2,1,0:T(8,128)S(1)} %get-tuple-element.87), channel_id=1, source_target_pairs={{0,248},{8,16},{16,8},{24,32},{32,24},{40,48},{48,40},{56,64},{64,... | collective-permute-start | bytes 786440 | tf_op jit(solution)/shard_map/ppermute | solution.py:384
  53.7 12.8 %collective-permute-start.9 = (f32[2,128,384]{2,1,0:T(8,128)S(1)}, f32[2,128,384]{2,1,0:T(8,128)S(1)}, u32[]{:S(2)}, u32[]{:S(2)}) collective-permute-start(f32[2,128,384]{2,1,0:T(8,128)S(1)} %get-tuple-element.76), channel_id=1, source_target_pairs={{0,8},{8,0},{16,24},{24,16},{32,40},{40,32},{48,56},{56,48},{64,72... | collective-permute-start | bytes 1179656 | tf_op jit(solution)/shard_map/ppermute | solution.py:384
  53.9 16.3 %collective-permute-start.10 = (f32[2,128,384]{2,1,0:T(8,128)S(1)}, f32[2,128,384]{2,1,0:T(8,128)S(1)}, u32[]{:S(2)}, u32[]{:S(2)}) collective-permute-start(f32[2,128,384]{2,1,0:T(8,128)S(1)} %get-tuple-element.77), channel_id=1, source_target_pairs={{0,248},{8,16},{16,8},{24,32},{32,24},{40,48},{48,40},{56,64},{64,... | collective-permute-start | bytes 1179656 | tf_op jit(solution)/shard_map/ppermute | solution.py:384
  59.2 11.2 %collective-permute-start.18 = (f32[2,384,128]{2,1,0:T(8,128)S(1)}, f32[2,384,128]{2,1,0:T(8,128)S(1)}, u32[]{:S(2)}, u32[]{:S(2)}) collective-permute-start(f32[2,384,128]{2,1,0:T(8,128)S(1)} %get-tuple-element.97.left), channel_id=1, source_target_pairs={{1,0},{2,1},{3,2},{4,3},{5,4},{6,5},{7,6},{0,7},{9,8},{10,9},{11,1... | collective-permute-start | bytes 1179656 | tf_op jit(solution)/shard_map/ppermute | solution.py:376
  59.5 11.0 %collective-permute-start.17 = (f32[2,384,128]{2,1,0:T(8,128)S(1)}, f32[2,384,128]{2,1,0:T(8,128)S(1)}, u32[]{:S(2)}, u32[]{:S(2)}) collective-permute-start(f32[2,384,128]{2,1,0:T(8,128)S(1)} %get-tuple-element.98.right), channel_id=1, source_target_pairs={{7,0},{0,1},{1,2},{2,3},{3,4},{4,5},{5,6},{6,7},{15,8},{8,9},{9,10... | collective-permute-start | bytes 1179656 | tf_op jit(solution)/shard_map/ppermute | solution.py:376
  63.6 9.6 %collective-permute-start.14 = (f32[2,384,128]{2,1,0:T(8,128)S(1)}, f32[2,384,128]{2,1,0:T(8,128)S(1)}, u32[]{:S(2)}, u32[]{:S(2)}) collective-permute-start(f32[2,384,128]{2,1,0:T(8,128)S(1)} %get-tuple-element.88.refs_4_.refs_0_), channel_id=1, source_target_pairs={{1,0},{2,1},{3,2},{4,3},{5,4},{6,5},{7,6},{0,7},{9,8},{10,9},{11,1... | collective-permute-start | bytes 1179656 | tf_op jit(solution)/shard_map/ppermute | solution.py:376
  78.5 14.7 %collective-permute-start.25 = (f32[2,128,384]{2,1,0:T(8,128)S(1)}, f32[2,128,384]{2,1,0:T(8,128)S(1)}, u32[]{:S(2)}, u32[]{:S(2)}) collective-permute-start(f32[2,128,384]{2,1,0:T(8,128)S(1)} %shard_map.85), channel_id=1, source_target_pairs={{248,0},{0,8},{8,16},{16,24},{24,32},{32,40},{40,48},{48,56},{56,6... | collective-permute-start | bytes 1179656 | tf_op jit(solution)/shard_map/ppermute | solution.py:376
  81.6 14.7 %collective-permute-start.23 = (f32[2,384,128]{2,1,0:T(8,128)S(1)}, f32[2,384,128]{2,1,0:T(8,128)S(1)}, u32[]{:S(2)}, u32[]{:S(2)}) collective-permute-start(f32[2,384,128]{2,1,0:T(8,128)S(1)} %get-tuple-element.112), channel_id=1, source_target_pairs={{7,0},{0,1},{1,2},{2,3},{3,4},{4,5},{5,6},{6,7},{15,8},{8,9},{9,10... | collective-permute-start | bytes 1179656 | tf_op jit(solution)/shard_map/ppermute | solution.py:376
  94.6 11.7 %collective-permute-start.22 = (f32[2,2,128,128]{3,2,1,0:T(8,128)S(1)}, f32[2,2,128,128]{3,2,1,0:T(8,128)S(1)}, u32[]{:S(2)}, u32[]{:S(2)}) collective-permute-start(f32[2,2,128,128]{3,2,1,0:T(8,128)S(1)} %shard_map.83), channel_id=1, source_target_pairs={{248,0},{0,8},{8,16},{16,24},{24,32},{32,40},{40,48},{48,56},{56,6... | collective-permute-start | bytes 786440 | tf_op jit(solution)/shard_map/ppermute | solution.py:376
  94.7 16.6 %collective-permute-start.19 = (f32[2,256,128]{2,1,0:T(8,128)S(1)}, f32[2,256,128]{2,1,0:T(8,128)S(1)}, u32[]{:S(2)}, u32[]{:S(2)}) collective-permute-start(f32[2,256,128]{2,1,0:T(8,128)S(1)} %slice.14), channel_id=1, source_target_pairs={{7,0},{0,1},{1,2},{2,3},{3,4},{4,5},{5,6},{6,7},{15,8},{8,9},{9,10... | collective-permute-start | bytes 786440 | tf_op jit(solution)/shard_map/ppermute | solution.py:376
  96.2 12.9 %collective-permute-start.24 = (f32[2,128,128]{2,1,0:T(8,128)S(1)}, f32[2,128,128]{2,1,0:T(8,128)S(1)}, u32[]{:S(2)}, u32[]{:S(2)}) collective-permute-start(f32[2,128,128]{2,1,0:T(8,128)S(1)} %shard_map.84), channel_id=1, source_target_pairs={{248,0},{0,8},{8,16},{16,24},{24,32},{32,40},{40,48},{48,56},{56,6... | collective-permute-start | bytes 393224 | tf_op jit(solution)/shard_map/ppermute | solution.py:376
  99.3 12.1 %collective-permute-start.21 = (f32[2,128,128]{2,1,0:T(8,128)S(1)}, f32[2,128,128]{2,1,0:T(8,128)S(1)}, u32[]{:S(2)}, u32[]{:S(2)}) collective-permute-start(f32[2,128,128]{2,1,0:T(8,128)S(1)} %shard_map.82), channel_id=1, source_target_pairs={{248,0},{0,8},{8,16},{16,24},{24,32},{32,40},{40,48},{48,56},{56,6... | collective-permute-start | bytes 393224 | tf_op jit(solution)/shard_map/ppermute | solution.py:376
  (10 other events, 119.8 us)

commit v8 on v7

--- a/solution.py
+++ b/solution.py
@@ -546,11 +546,6 @@
     down[:, :, t:] = right[:, t:]
 
 
-def both_kernel(first, second, down):
-    down[0] = first[...]
-    down[1] = second[...]
-
-
 def east_kernel(right, above, east):
     h, t = PROBE, TILE
     east[:, :h] = right[:, :h] + above[:, :, t:]
@@ -573,10 +568,8 @@
 def last(layer, piece, above, result):
     operands = [*piece, *above]
     specs, aliases = {}, {}
-    if len(above) == 2:
-        specs[6] = pl.BlockSpec((None, 2, PROBE, PROBE), lambda i: (layer, 0, 0, 0))
     if result is not None:
-        specs[len(operands)], aliases = pl.BlockSpec(memory_space=pl.ANY), {len(operands): 0}
+        specs, aliases = {len(operands): pl.BlockSpec(memory_space=pl.ANY)}, {len(operands): 0}
         operands.append(result)
     return plain(
         functools.partial(last_kernel, len(above) == 1),
@@ -647,7 +640,7 @@
             new.append(shifted(new[0], "col", -1))
         renewed[layer] = new
     grads = gradients(renewed, fill_next)
-    from_left, above_l = {}, {}
+    from_left, above_m, above_l = {}, {}, {}
     down = plain(join_kernel, [shape(2, h, EXT)], [grads[2][0], grads[2][2], grads[2][3]])[0]
     above2 = shifted(down, "row", 1)
     east = plain(east_kernel, [shape(2, t, h)], [grads[2][3], above2])[0]
@@ -655,15 +648,14 @@
     for layer in (1, 0):
         right = grads[layer][3]
         from_left[layer] = shifted(right if layer else right[:, t:], "col", 1)
+        above_m[layer] = shifted(grads[layer][2], "row", 1)
         down = plain(spill_kernel, [shape(2, h, h)], [grads[layer][0], from_left[layer]])[0]
         above_l[layer] = shifted(down, "row", 1)
-    down = plain(both_kernel, [shape(2, 2, h, h)], [grads[0][2], grads[1][2]])[0]
-    above_m = shifted(down, "row", 1)
     from_left[0] = shifted(grads[0][3][:, :t], "col", 1)
     pieces = [(renewed[n][0], renewed[n][1], grads[n][0], grads[n][1], from_left[n]) for n in range(SLICES)]
     result = last(2, pieces[2], [above2], None)
-    result = last(1, pieces[1], [above_l[1], above_m], result)
-    return last(0, pieces[0], [above_l[0], above_m], result)
+    result = last(1, pieces[1], [above_l[1], above_m[1]], result)
+    return last(0, pieces[0], [above_l[0], above_m[0]], result)
 
 
 def solution(mesh):

time: 114 us -> 118 us (1.035)
  waiting for transfers between devices: 37.2 us -> 41.2 us
    ppermute x21 -> x22, waiting for transfers between devices: 29 us -> 33.1 us  [shifted(): lax.ppermute(block, axis, [((i - distance) % size, i) for i in range(size)])]
    ppermute x21 -> x22, starting transfers between devices: 26.9 us -> 26.7 us  [shifted(): lax.ppermute(block, axis, [((i - distance) % size, i) for i in range(size)])]
    pallas_call x16 -> x15, Pallas kernels: 4.16 us -> 4.16 us  [plain(): pl.pallas_call(body, grid=(1,), in_specs=[specs.get(n, None) or whole(o)...]
  transfers between devices with their start and end apart: 27 -> 28, of which waited for: 14 -> 14; matrix products, arithmetic and copies ran while one was open for 0% -> 0% of each run, Pallas kernels for 14% -> 14%
where the time goes in v8:
time: 118 us; the launch traced here: 116 us
  starting transfers between devices  42.8 us (36%)
  waiting for transfers between devices  41.2 us (35%)
  Pallas kernels  30.3 us (26%)
  local copies, waits for them, and re-layouts  1.49 us (1%)
    ppermute x22, waiting for transfers between devices, shifted(): lax.ppermute(block, axis, [((i - distance) % size, i) for i in range(size)])  33.1 us
    ppermute x22, starting transfers between devices, shifted(): lax.ppermute(block, axis, [((i - distance) % size, i) for i in range(size)])  26.7 us
    pallas_call x10, Pallas kernels, run(): pl.pallas_call(body, grid=(1,), in_specs=in_specs, out_specs=[whole(o) fo...  26 us
    ppermute x6, starting transfers between devices, swapped(): return lax.ppermute(block, 'row', sorted(route))  16.1 us
    ppermute x6, waiting for transfers between devices, swapped(): return lax.ppermute(block, 'row', sorted(route))  8.16 us
    pallas_call x15, Pallas kernels, plain(): pl.pallas_call(body, grid=(1,), in_specs=[specs.get(n, None) or whole(o)...  4.16 us
  transfers between devices with their start and end apart: 28, of which 14 were waited for; matrix products, arithmetic and copies ran while one was open for 0% of the time, Pallas kernels for 14%

profile of v8, /device:TPU:7, one launch (start us, length us, event | category | flops | bytes accessed | tf_op | source)
XLA Modules:
  0.0 116.1 jit_solution(167242961449398979)
XLA Ops:
  1.6 8.1 %collective-permute-start.3 = (f32[2,2,128,128]{3,2,1,0:T(8,128)S(1)}, f32[2,2,128,128]{3,2,1,0:T(8,128)S(1)}, u32[]{:S(2)}, u32[]{:S(2)}) collective-permute-start(f32[2,2,128,128]{3,2,1,0:T(8,128)S(1)} %get-tuple-element.65), channel_id=1, source_target_pairs={{8,0},{16,8},{24,16},{32,24},{40,32},{48,40},{56,48},{64,56},{72,6... | collective-permute-start | bytes 786440 | tf_op jit(solution)/shard_map/ppermute | solution.py:376
  14.7 2.7 %collective-permute-start.6 = (f32[2,2,128,128]{3,2,1,0:T(8,128)S(1)}, f32[2,2,128,128]{3,2,1,0:T(8,128)S(1)}, u32[]{:S(2)}, u32[]{:S(2)}) collective-permute-start(f32[2,2,128,128]{3,2,1,0:T(8,128)S(1)} %collective-permute-done.3.refs_5_.low_left), channel_id=1, source_target_pairs={{1,0},{2,1},{3,2},{4,3},{5,4},{6,5},{7,6},{0,7},{9,8},{10,9},{11,1... | collective-permute-start | bytes 786440 | tf_op jit(solution)/shard_map/ppermute | solution.py:376
  17.3 3.0 %collective-permute-done.refs_4_.refs_5_.low_left.low_right = f32[2,128,256]{2,1,0:T(8,128)S(1)} collective-permute-done((f32[2,128,256]{2,1,0:T(8,128)S(1)}, f32[2,128,256]{2,1,0:T(8,128)S(1)}, u32[]{:S(2)}, u32[]{:S(2)}) %collective-permute-start) | collective-permute-done | bytes 262176 | tf_op jit(solution)/shard_map/ppermute | solution.py:376
  20.3 2.7 %collective-permute-start.2 = (f32[2,128,128]{2,1,0:T(8,128)S(1)}, f32[2,128,128]{2,1,0:T(8,128)S(1)}, u32[]{:S(2)}, u32[]{:S(2)}) collective-permute-start(f32[2,128,128]{2,1,0:T(8,128)S(1)} %slice.16), channel_id=1, source_target_pairs={{1,0},{2,1},{3,2},{4,3},{5,4},{6,5},{7,6},{0,7},{9,8},{10,9},{11,1... | collective-permute-start | bytes 393224 | tf_op jit(solution)/shard_map/ppermute | solution.py:376
  23.4 3.1 %collective-permute-done.2.refs_7_.corner = f32[2,128,128]{2,1,0:T(8,128)S(1)} collective-permute-done((f32[2,128,128]{2,1,0:T(8,128)S(1)}, f32[2,128,128]{2,1,0:T(8,128)S(1)}, u32[]{:S(2)}, u32[]{:S(2)}) %collective-permute-start.2) | collective-permute-done | bytes 131104 | tf_op jit(solution)/shard_map/ppermute | solution.py:376
  26.5 2.4 %shard_map.65 = (f32[2,6,128,128]{3,2,1,0:T(8,128)}, f32[2,6,128,128]{3,2,1,0:T(8,128)S(1)}) custom-call(s32[2,6]{1,0:T(2,128)S(1)} %bitcast.10, bf16[4,256,256]{2,1,0:T(8,128)(2,1)S(1)} %get-tuple-element.62.refs_1_, f32[4,128,128]{2,1,0:T(8,128)S(1)} %get-tuple-element.63.refs_2_, f32[2,3,256,256]{3,2,1,0:T(8,128)S(1)} %copy-done.1, ...), custom_call_target="tpu_custom_call" | custom-call | flops 1207959552 | bytes 5374000 | tf_op jit(solution)/shard_map/pallas_call | solution.py:326
  29.0 2.4 %shard_map.66 = (f32[2,6,128,128]{3,2,1,0:T(8,128)S(1)}, f32[2,6,128,128]{3,2,1,0:T(8,128)S(1)}) custom-call(s32[2,6]{1,0:T(2,128)S(1)} %bitcast.11, bf16[4,256,256]{2,1,0:T(8,128)(2,1)S(1)} %get-tuple-element.62.refs_1_, f32[4,128,128]{2,1,0:T(8,128)S(1)} %get-tuple-element.63.refs_2_, f32[2,6,128,128]{3,2,1,0:T(8,128)S(1)} %get-tuple-element.64.refs_3_.refs_4_, ...), custom_call_target="tpu_custom_call" | custom-call | flops 1207959552 | bytes 6553648 | tf_op jit(solution)/shard_map/pallas_call | solution.py:326
  31.4 2.9 %shard_map.67 = (f32[2,384,128]{2,1,0:T(8,128)S(1)}, f32[2,256,128]{2,1,0:T(8,128)S(1)}, f32[2,128,128]{2,1,0:T(8,128)S(1)}, f32[2,384,128]{2,1,0:T(8,128)S(1)}, f32[2,6,128,128]{3,2,1,0:T(8,128)S(1)}) custom-call(s32[2,6]{1,0:T(2,128)S(1)} %bitcast.12, bf16[4,256,256]{2,1,0:T(8,128)(2,1)S(1)} %get-tuple-element.62.refs_1_, f32[6,128,128]{2,1,0:T(8,128)S(1)} %bitcast.8, ...), custom_call_target="tpu_custom_call" | custom-call | flops 1207959552 | bytes 7077936 | tf_op jit(solution)/shard_map/pallas_call | solution.py:326
  34.4 2.7 %shard_map.68 = (f32[2,384,128]{2,1,0:T(8,128)S(1)}, f32[2,256,128]{2,1,0:T(8,128)S(1)}, f32[2,128,128]{2,1,0:T(8,128)S(1)}, f32[2,384,128]{2,1,0:T(8,128)S(1)}, f32[2,6,128,128]{3,2,1,0:T(8,128)S(1)}) custom-call(s32[2,6]{1,0:T(2,128)S(1)} %bitcast.13, bf16[4,256,256]{2,1,0:T(8,128)(2,1)S(1)} %get-tuple-element.62.refs_1_, ...), custom_call_target="tpu_custom_call" | custom-call | flops 1207959552 | bytes 5636144 | tf_op jit(solution)/shard_map/pallas_call | solution.py:326
  37.1 2.6 %shard_map.69 = (f32[2,384,128]{2,1,0:T(8,128)S(1)}, f32[2,256,128]{2,1,0:T(8,128)S(1)}, f32[2,128,128]{2,1,0:T(8,128)S(1)}, f32[2,384,128]{2,1,0:T(8,128)S(1)}) custom-call(s32[2,6]{1,0:T(2,128)S(1)} %bitcast.14, bf16[4,256,256]{2,1,0:T(8,128)(2,1)S(1)} %get-tuple-element.62.refs_1_, f32[4,128,128]{2,1,0:T(8,128)S(1)} %get-tuple-element.63.refs_2_, ...), custom_call_target="tpu_custom_call" | custom-call | flops 1207959552 | bytes 3276848 | tf_op jit(solution)/shard_map/pallas_call | solution.py:326
  40.2 2.5 %collective-permute-start.7 = (f32[2,384,128]{2,1,0:T(8,128)S(1)}, f32[2,384,128]{2,1,0:T(8,128)S(1)}, u32[]{:S(2)}, u32[]{:S(2)}) collective-permute-start(f32[2,384,128]{2,1,0:T(8,128)S(1)} %get-tuple-element.75.right), channel_id=1, source_target_pairs={{7,0},{0,1},{1,2},{2,3},{3,4},{4,5},{5,6},{6,7},{15,8},{8,9},{9,10... | collective-permute-start | bytes 1179656 | tf_op jit(solution)/shard_map/ppermute | solution.py:376
  42.8 5.3 %collective-permute-start.16 = (f32[2,128,384]{2,1,0:T(8,128)S(1)}, f32[2,128,384]{2,1,0:T(8,128)S(1)}, u32[]{:S(2)}, u32[]{:S(2)}) collective-permute-start(f32[2,128,384]{2,1,0:T(8,128)S(1)} %get-tuple-element.96), channel_id=1, source_target_pairs={{0,248},{8,16},{16,8},{24,32},{32,24},{40,48},{48,40},{56,64},{64,... | collective-permute-start | bytes 1179656 | tf_op jit(solution)/shard_map/ppermute | solution.py:384
  48.4 5.2 %collective-permute-start.13 = (f32[2,128,256]{2,1,0:T(8,128)S(1)}, f32[2,128,256]{2,1,0:T(8,128)S(1)}, u32[]{:S(2)}, u32[]{:S(2)}) collective-permute-start(f32[2,128,256]{2,1,0:T(8,128)S(1)} %get-tuple-element.87), channel_id=1, source_target_pairs={{0,248},{8,16},{16,8},{24,32},{32,24},{40,48},{48,40},{56,64},{64,... | collective-permute-start | bytes 786440 | tf_op jit(solution)/shard_map/ppermute | solution.py:384
  53.9 5.2 %collective-permute-start.10 = (f32[2,128,384]{2,1,0:T(8,128)S(1)}, f32[2,128,384]{2,1,0:T(8,128)S(1)}, u32[]{:S(2)}, u32[]{:S(2)}) collective-permute-start(f32[2,128,384]{2,1,0:T(8,128)S(1)} %get-tuple-element.77), channel_id=1, source_target_pairs={{0,248},{8,16},{16,8},{24,32},{32,24},{40,48},{48,40},{56,64},{64,... | collective-permute-start | bytes 1179656 | tf_op jit(solution)/shard_map/ppermute | solution.py:384
  59.5 2.7 %collective-permute-start.17 = (f32[2,384,128]{2,1,0:T(8,128)S(1)}, f32[2,384,128]{2,1,0:T(8,128)S(1)}, u32[]{:S(2)}, u32[]{:S(2)}) collective-permute-start(f32[2,384,128]{2,1,0:T(8,128)S(1)} %get-tuple-element.98.right), channel_id=1, source_target_pairs={{7,0},{0,1},{1,2},{2,3},{3,4},{4,5},{5,6},{6,7},{15,8},{8,9},{9,10... | collective-permute-start | bytes 1179656 | tf_op jit(solution)/shard_map/ppermute | solution.py:376
  63.6 2.9 %collective-permute-done.9.refs_2_ = f32[2,128,384]{2,1,0:T(8,128)S(1)} collective-permute-done((f32[2,128,384]{2,1,0:T(8,128)S(1)}, f32[2,128,384]{2,1,0:T(8,128)S(1)}, u32[]{:S(2)}, u32[]{:S(2)}) %collective-permute-start.9) | collective-permute-done | bytes 393248 | tf_op jit(solution)/shard_map/ppermute | solution.py:384
  66.5 3.7 %collective-permute-done.10.refs_3_ = f32[2,128,384]{2,1,0:T(8,128)S(1)} collective-permute-done((f32[2,128,384]{2,1,0:T(8,128)S(1)}, f32[2,128,384]{2,1,0:T(8,128)S(1)}, u32[]{:S(2)}, u32[]{:S(2)}) %collective-permute-start.10) | collective-permute-done | bytes 393248 | tf_op jit(solution)/shard_map/ppermute | solution.py:384
  73.2 2.4 %shard_map.75 = (f32[2,6,128,128]{3,2,1,0:T(8,128)S(1)}, f32[2,6,128,128]{3,2,1,0:T(8,128)S(1)}) custom-call(s32[2,6]{1,0:T(2,128)S(1)} %bitcast.16, bf16[4,256,256]{2,1,0:T(8,128)(2,1)S(1)} %get-tuple-element.62.refs_1_, f32[4,128,128]{2,1,0:T(8,128)S(1)} %get-tuple-element.63.refs_2_, f32[2,6,128,128]{3,2,1,0:T(8,128)S(1)} %get-tuple-element.81.refs_3_.refs_4_, ...), custom_call_target="tpu_custom_call" | custom-call | flops 1207959552 | bytes 4849712 | tf_op jit(solution)/shard_map/pallas_call | solution.py:326
  75.6 2.9 %shard_map.79 = (f32[2,384,128]{2,1,0:T(8,128)S(1)}, f32[2,256,128]{2,1,0:T(8,128)S(1)}, f32[2,128,128]{2,1,0:T(8,128)S(1)}, f32[2,384,128]{2,1,0:T(8,128)S(1)}, f32[2,6,128,128]{3,2,1,0:T(8,128)S(1)}) custom-call(s32[2,6]{1,0:T(2,128)S(1)} %bitcast.17, bf16[4,256,256]{2,1,0:T(8,128)(2,1)S(1)} %get-tuple-element.62.refs_1_, f32[6,128,128]{2,1,0:T(8,128)S(1)} %bitcast.9, ...), custom_call_target="tpu_custom_call" | custom-call | flops 1207959552 | bytes 5374000 | tf_op jit(solution)/shard_map/pallas_call | solution.py:326
  78.9 2.7 %shard_map.80 = (f32[2,384,128]{2,1,0:T(8,128)S(1)}, f32[2,256,128]{2,1,0:T(8,128)S(1)}, f32[2,128,128]{2,1,0:T(8,128)S(1)}, f32[2,384,128]{2,1,0:T(8,128)S(1)}, f32[2,6,128,128]{3,2,1,0:T(8,128)S(1)}) custom-call(s32[2,6]{1,0:T(2,128)S(1)} %bitcast.18, bf16[4,256,256]{2,1,0:T(8,128)(2,1)S(1)} %get-tuple-element.62.refs_1_, ...), custom_call_target="tpu_custom_call" | custom-call | flops 1207959552 | bytes 5636144 | tf_op jit(solution)/shard_map/pallas_call | solution.py:326
  83.3 10.0 %collective-permute-done.26.above.refs_5_ = f32[2,128,384]{2,1,0:T(8,128)S(1)} collective-permute-done((f32[2,128,384]{2,1,0:T(8,128)S(1)}, f32[2,128,384]{2,1,0:T(8,128)S(1)}, u32[]{:S(2)}, u32[]{:S(2)}) %collective-permute-start.26) | collective-permute-done | bytes 393248 | tf_op jit(solution)/shard_map/ppermute | solution.py:376
  94.6 2.6 %shard_map.81 = (f32[2,384,128]{2,1,0:T(8,128)S(1)}, f32[2,256,128]{2,1,0:T(8,128)S(1)}, f32[2,128,128]{2,1,0:T(8,128)S(1)}, f32[2,384,128]{2,1,0:T(8,128)S(1)}) custom-call(s32[2,6]{1,0:T(2,128)S(1)} %bitcast.19, bf16[4,256,256]{2,1,0:T(8,128)(2,1)S(1)} %get-tuple-element.62.refs_1_, f32[4,128,128]{2,1,0:T(8,128)S(1)} %get-tuple-element.63.refs_2_, ...), custom_call_target="tpu_custom_call" | custom-call | flops 1207959552 | bytes 3276848 | tf_op jit(solution)/shard_map/pallas_call | solution.py:326
  100.3 10.0 %collective-permute-done.25.refs_6_ = f32[2,128,128]{2,1,0:T(8,128)S(1)} collective-permute-done((f32[2,128,128]{2,1,0:T(8,128)S(1)}, f32[2,128,128]{2,1,0:T(8,128)S(1)}, u32[]{:S(2)}, u32[]{:S(2)}) %collective-permute-start.25) | collective-permute-done | bytes 131104 | tf_op jit(solution)/shard_map/ppermute | solution.py:376
  110.3 2.8 %collective-permute-done.24.refs_5_ = f32[2,128,128]{2,1,0:T(8,128)S(1)} collective-permute-done((f32[2,128,128]{2,1,0:T(8,128)S(1)}, f32[2,128,128]{2,1,0:T(8,128)S(1)}, u32[]{:S(2)}, u32[]{:S(2)}) %collective-permute-start.24) | collective-permute-done | bytes 131104 | tf_op jit(solution)/shard_map/ppermute | solution.py:376
  (76 shorter events, 22.4 us)
Async XLA Ops:
  1.6 13.1 %collective-permute-start.3 = (f32[2,2,128,128]{3,2,1,0:T(8,128)S(1)}, f32[2,2,128,128]{3,2,1,0:T(8,128)S(1)}, u32[]{:S(2)}, u32[]{:S(2)}) collective-permute-start(f32[2,2,128,128]{3,2,1,0:T(8,128)S(1)} %get-tuple-element.65), channel_id=1, source_target_pairs={{8,0},{16,8},{24,16},{32,24},{40,32},{48,40},{56,48},{64,56},{72,6... | collective-permute-start | bytes 786440 | tf_op jit(solution)/shard_map/ppermute | solution.py:376
  9.7 19.3 %collective-permute-start.5 = (f32[2,2,256,128]{3,2,1,0:T(8,128)S(1)}, f32[2,2,256,128]{3,2,1,0:T(8,128)S(1)}, u32[]{:S(2)}, u32[]{:S(2)}) collective-permute-start(f32[2,2,256,128]{3,2,1,0:T(8,128)S(1)} %get-tuple-element.67), channel_id=1, source_target_pairs={{1,0},{2,1},{3,2},{4,3},{5,4},{6,5},{7,6},{0,7},{9,8},{10,9},{11,1... | collective-permute-start | bytes 1572872 | tf_op jit(solution)/shard_map/ppermute | solution.py:376
  10.7 9.6 %collective-permute-start = (f32[2,128,256]{2,1,0:T(8,128)S(1)}, f32[2,128,256]{2,1,0:T(8,128)S(1)}, u32[]{:S(2)}, u32[]{:S(2)}) collective-permute-start(f32[2,128,256]{2,1,0:T(8,128)S(1)} %slice_bitcast_fusion), channel_id=1, source_target_pairs={{8,0},{16,8},{24,16},{32,24},{40,32},{48,40},{56,48},{64,56},{72,6... | collective-permute-start | bytes 786440 | tf_op jit(solution)/shard_map/ppermute | solution.py:376
  11.2 12.2 %collective-permute-start.1 = (f32[2,256,128]{2,1,0:T(8,128)S(1)}, f32[2,256,128]{2,1,0:T(8,128)S(1)}, u32[]{:S(2)}, u32[]{:S(2)}) collective-permute-start(f32[2,256,128]{2,1,0:T(8,128)S(1)} %get-tuple-element.61), channel_id=1, source_target_pairs={{1,0},{2,1},{3,2},{4,3},{5,4},{6,5},{7,6},{0,7},{9,8},{10,9},{11,1... | collective-permute-start | bytes 786440 | tf_op jit(solution)/shard_map/ppermute | solution.py:376
  11.9 17.1 %collective-permute-start.4 = (f32[2,2,128,128]{3,2,1,0:T(8,128)S(1)}, f32[2,2,128,128]{3,2,1,0:T(8,128)S(1)}, u32[]{:S(2)}, u32[]{:S(2)}) collective-permute-start(f32[2,2,128,128]{3,2,1,0:T(8,128)S(1)} %get-tuple-element.66), channel_id=1, source_target_pairs={{8,0},{16,8},{24,16},{32,24},{40,32},{48,40},{56,48},{64,56},{72,6... | collective-permute-start | bytes 786440 | tf_op jit(solution)/shard_map/ppermute | solution.py:376
  14.7 14.3 %collective-permute-start.6 = (f32[2,2,128,128]{3,2,1,0:T(8,128)S(1)}, f32[2,2,128,128]{3,2,1,0:T(8,128)S(1)}, u32[]{:S(2)}, u32[]{:S(2)}) collective-permute-start(f32[2,2,128,128]{3,2,1,0:T(8,128)S(1)} %collective-permute-done.3.refs_5_.low_left), channel_id=1, source_target_pairs={{1,0},{2,1},{3,2},{4,3},{5,4},{6,5},{7,6},{0,7},{9,8},{10,9},{11,1... | collective-permute-start | bytes 786440 | tf_op jit(solution)/shard_map/ppermute | solution.py:376
  37.0 11.0 %collective-permute-start.11 = (f32[2,384,128]{2,1,0:T(8,128)S(1)}, f32[2,384,128]{2,1,0:T(8,128)S(1)}, u32[]{:S(2)}, u32[]{:S(2)}) collective-permute-start(f32[2,384,128]{2,1,0:T(8,128)S(1)} %get-tuple-element.85.right), channel_id=1, source_target_pairs={{7,0},{0,1},{1,2},{2,3},{3,4},{4,5},{5,6},{6,7},{15,8},{8,9},{9,10... | collective-permute-start | bytes 1179656 | tf_op jit(solution)/shard_map/ppermute | solution.py:376
  40.2 13.4 %collective-permute-start.7 = (f32[2,384,128]{2,1,0:T(8,128)S(1)}, f32[2,384,128]{2,1,0:T(8,128)S(1)}, u32[]{:S(2)}, u32[]{:S(2)}) collective-permute-start(f32[2,384,128]{2,1,0:T(8,128)S(1)} %get-tuple-element.75.right), channel_id=1, source_target_pairs={{7,0},{0,1},{1,2},{2,3},{3,4},{4,5},{5,6},{6,7},{15,8},{8,9},{9,10... | collective-permute-start | bytes 1179656 | tf_op jit(solution)/shard_map/ppermute | solution.py:376
  42.7 11.2 %collective-permute-start.15 = (f32[2,128,384]{2,1,0:T(8,128)S(1)}, f32[2,128,384]{2,1,0:T(8,128)S(1)}, u32[]{:S(2)}, u32[]{:S(2)}) collective-permute-start(f32[2,128,384]{2,1,0:T(8,128)S(1)} %get-tuple-element.95), channel_id=1, source_target_pairs={{0,8},{8,0},{16,24},{24,16},{32,40},{40,32},{48,56},{56,48},{64,72... | collective-permute-start | bytes 1179656 | tf_op jit(solution)/shard_map/ppermute | solution.py:384
  42.8 16.4 %collective-permute-start.16 = (f32[2,128,384]{2,1,0:T(8,128)S(1)}, f32[2,128,384]{2,1,0:T(8,128)S(1)}, u32[]{:S(2)}, u32[]{:S(2)}) collective-permute-start(f32[2,128,384]{2,1,0:T(8,128)S(1)} %get-tuple-element.96), channel_id=1, source_target_pairs={{0,248},{8,16},{16,8},{24,32},{32,24},{40,48},{48,40},{56,64},{64,... | collective-permute-start | bytes 1179656 | tf_op jit(solution)/shard_map/ppermute | solution.py:384
  48.2 11.4 %collective-permute-start.12 = (f32[2,128,256]{2,1,0:T(8,128)S(1)}, f32[2,128,256]{2,1,0:T(8,128)S(1)}, u32[]{:S(2)}, u32[]{:S(2)}) collective-permute-start(f32[2,128,256]{2,1,0:T(8,128)S(1)} %get-tuple-element.86), channel_id=1, source_target_pairs={{0,8},{8,0},{16,24},{24,16},{32,40},{40,32},{48,56},{56,48},{64,72... | collective-permute-start | bytes 786440 | tf_op jit(solution)/shard_map/ppermute | solution.py:384
  48.4 15.0 %collective-permute-start.13 = (f32[2,128,256]{2,1,0:T(8,128)S(1)}, f32[2,128,256]{2,1,0:T(8,128)S(1)}, u32[]{:S(2)}, u32[]{:S(2)}) collective-permute-start(f32[2,128,256]{2,1,0:T(8,128)S(1)} %get-tuple-element.87), channel_id=1, source_target_pairs={{0,248},{8,16},{16,8},{24,32},{32,24},{40,48},{48,40},{56,64},{64,... | collective-permute-start | bytes 786440 | tf_op jit(solution)/shard_map/ppermute | solution.py:384
  53.7 12.8 %collective-permute-start.9 = (f32[2,128,384]{2,1,0:T(8,128)S(1)}, f32[2,128,384]{2,1,0:T(8,128)S(1)}, u32[]{:S(2)}, u32[]{:S(2)}) collective-permute-start(f32[2,128,384]{2,1,0:T(8,128)S(1)} %get-tuple-element.76), channel_id=1, source_target_pairs={{0,8},{8,0},{16,24},{24,16},{32,40},{40,32},{48,56},{56,48},{64,72... | collective-permute-start | bytes 1179656 | tf_op jit(solution)/shard_map/ppermute | solution.py:384
  53.9 16.3 %collective-permute-start.10 = (f32[2,128,384]{2,1,0:T(8,128)S(1)}, f32[2,128,384]{2,1,0:T(8,128)S(1)}, u32[]{:S(2)}, u32[]{:S(2)}) collective-permute-start(f32[2,128,384]{2,1,0:T(8,128)S(1)} %get-tuple-element.77), channel_id=1, source_target_pairs={{0,248},{8,16},{16,8},{24,32},{32,24},{40,48},{48,40},{56,64},{64,... | collective-permute-start | bytes 1179656 | tf_op jit(solution)/shard_map/ppermute | solution.py:384
  59.2 11.2 %collective-permute-start.18 = (f32[2,384,128]{2,1,0:T(8,128)S(1)}, f32[2,384,128]{2,1,0:T(8,128)S(1)}, u32[]{:S(2)}, u32[]{:S(2)}) collective-permute-start(f32[2,384,128]{2,1,0:T(8,128)S(1)} %get-tuple-element.97.left), channel_id=1, source_target_pairs={{1,0},{2,1},{3,2},{4,3},{5,4},{6,5},{7,6},{0,7},{9,8},{10,9},{11,1... | collective-permute-start | bytes 1179656 | tf_op jit(solution)/shard_map/ppermute | solution.py:376
  59.5 11.0 %collective-permute-start.17 = (f32[2,384,128]{2,1,0:T(8,128)S(1)}, f32[2,384,128]{2,1,0:T(8,128)S(1)}, u32[]{:S(2)}, u32[]{:S(2)}) collective-permute-start(f32[2,384,128]{2,1,0:T(8,128)S(1)} %get-tuple-element.98.right), channel_id=1, source_target_pairs={{7,0},{0,1},{1,2},{2,3},{3,4},{4,5},{5,6},{6,7},{15,8},{8,9},{9,10... | collective-permute-start | bytes 1179656 | tf_op jit(solution)/shard_map/ppermute | solution.py:376
  63.6 9.6 %collective-permute-start.14 = (f32[2,384,128]{2,1,0:T(8,128)S(1)}, f32[2,384,128]{2,1,0:T(8,128)S(1)}, u32[]{:S(2)}, u32[]{:S(2)}) collective-permute-start(f32[2,384,128]{2,1,0:T(8,128)S(1)} %get-tuple-element.88.refs_4_.refs_0_), channel_id=1, source_target_pairs={{1,0},{2,1},{3,2},{4,3},{5,4},{6,5},{7,6},{0,7},{9,8},{10,9},{11,1... | collective-permute-start | bytes 1179656 | tf_op jit(solution)/shard_map/ppermute | solution.py:376
  78.5 14.7 %collective-permute-start.26 = (f32[2,128,384]{2,1,0:T(8,128)S(1)}, f32[2,128,384]{2,1,0:T(8,128)S(1)}, u32[]{:S(2)}, u32[]{:S(2)}) collective-permute-start(f32[2,128,384]{2,1,0:T(8,128)S(1)} %shard_map.84), channel_id=1, source_target_pairs={{248,0},{0,8},{8,16},{16,24},{24,32},{32,40},{40,48},{48,56},{56,6... | collective-permute-start | bytes 1179656 | tf_op jit(solution)/shard_map/ppermute | solution.py:376
  81.6 17.2 %collective-permute-start.23 = (f32[2,384,128]{2,1,0:T(8,128)S(1)}, f32[2,384,128]{2,1,0:T(8,128)S(1)}, u32[]{:S(2)}, u32[]{:S(2)}) collective-permute-start(f32[2,384,128]{2,1,0:T(8,128)S(1)} %get-tuple-element.111), channel_id=1, source_target_pairs={{7,0},{0,1},{1,2},{2,3},{3,4},{4,5},{5,6},{6,7},{15,8},{8,9},{9,10... | collective-permute-start | bytes 1179656 | tf_op jit(solution)/shard_map/ppermute | solution.py:376
  97.2 18.0 %collective-permute-start.19 = (f32[2,256,128]{2,1,0:T(8,128)S(1)}, f32[2,256,128]{2,1,0:T(8,128)S(1)}, u32[]{:S(2)}, u32[]{:S(2)}) collective-permute-start(f32[2,256,128]{2,1,0:T(8,128)S(1)} %slice.14), channel_id=1, source_target_pairs={{7,0},{0,1},{1,2},{2,3},{3,4},{4,5},{5,6},{6,7},{15,8},{8,9},{9,10... | collective-permute-start | bytes 786440 | tf_op jit(solution)/shard_map/ppermute | solution.py:376
  98.7 15.3 %collective-permute-start.22 = (f32[2,128,128]{2,1,0:T(8,128)S(1)}, f32[2,128,128]{2,1,0:T(8,128)S(1)}, u32[]{:S(2)}, u32[]{:S(2)}) collective-permute-start(f32[2,128,128]{2,1,0:T(8,128)S(1)} %get-tuple-element.108), channel_id=1, source_target_pairs={{248,0},{0,8},{8,16},{16,24},{24,32},{32,40},{40,48},{48,56},{56,6... | collective-permute-start | bytes 393224 | tf_op jit(solution)/shard_map/ppermute | solution.py:376
  98.7 11.6 %collective-permute-start.25 = (f32[2,128,128]{2,1,0:T(8,128)S(1)}, f32[2,128,128]{2,1,0:T(8,128)S(1)}, u32[]{:S(2)}, u32[]{:S(2)}) collective-permute-start(f32[2,128,128]{2,1,0:T(8,128)S(1)} %get-tuple-element.112), channel_id=1, source_target_pairs={{248,0},{0,8},{8,16},{16,24},{24,32},{32,40},{40,48},{48,56},{56,6... | collective-permute-start | bytes 393224 | tf_op jit(solution)/shard_map/ppermute | solution.py:376
  99.3 13.9 %collective-permute-start.24 = (f32[2,128,128]{2,1,0:T(8,128)S(1)}, f32[2,128,128]{2,1,0:T(8,128)S(1)}, u32[]{:S(2)}, u32[]{:S(2)}) collective-permute-start(f32[2,128,128]{2,1,0:T(8,128)S(1)} %shard_map.83), channel_id=1, source_target_pairs={{248,0},{0,8},{8,16},{16,24},{24,32},{32,40},{40,48},{48,56},{56,6... | collective-permute-start | bytes 393224 | tf_op jit(solution)/shard_map/ppermute | solution.py:376
  99.3 15.9 %collective-permute-start.21 = (f32[2,128,128]{2,1,0:T(8,128)S(1)}, f32[2,128,128]{2,1,0:T(8,128)S(1)}, u32[]{:S(2)}, u32[]{:S(2)}) collective-permute-start(f32[2,128,128]{2,1,0:T(8,128)S(1)} %shard_map.82), channel_id=1, source_target_pairs={{248,0},{0,8},{8,16},{16,24},{24,32},{32,40},{40,48},{48,56},{56,6... | collective-permute-start | bytes 393224 | tf_op jit(solution)/shard_map/ppermute | solution.py:376
  (11 other events, 125.9 us)
